TPU v7x, 32 devices: a whole 2x2x4 slice. The times are simulated.
32 devices in a mesh: groups: 2 (over x), tm: 8 (over z, y), rows: 2 (over core).
Axes of the slice: x: 2, y: 2, z: 4, core: 2. Of those that a mesh axis runs over, the one named last changes fastest.
Arguments:
- iterate: float32 [32, 512, 512], P(('groups', 'tm'), 'rows'), parts along dimension 0, may hold values from -6 to 6
- forcing: float32 [32, 512, 512], P(('groups', 'tm'), 'rows'), parts along dimension 0, may hold values from -18 to 18
- initial_state: float32 [1024, 512], P(('groups', 'rows')), parts along dimension 0, may hold values from -6 to 6
- diffusivity: float32 [1024, 512], P(('groups', 'rows')), parts along dimension 0, may hold values from 0.5 to 4
Outputs:
- updated: float32 [32, 512, 512], P(('groups', 'tm'), 'rows'), parts along dimension 0
- residual_rms: float32 [32], P(('groups', 'tm')), parts along dimension 0
There are 2 independent parts, one for each index of `groups`. A program takes and returns all parts, laid end to end along the dimension named above; each array names one. Nothing has to cross between parts.
All inputs are finite; a program needn't handle non-finite values.
Results may differ from a plain program's by a relative error of at most 0.0003.
Values sent between devices are 32-bit elements; how exact they have to be, the bound alone decides.
No kernel may reach another device: no remote copies, remote signals or barrier semaphores. Data moves between devices by JAX's collectives and lax.ppermute only.
A program may use at most 64 MiB of HBM per device.

v0:
```python
import jax
import jax.numpy as jnp
from jax import lax
from jax.sharding import PartitionSpec as P

CG_ITERS = 3


circulant_alpha = 0.05
time_step = 0.5
rms_eps = 1e-06


def extended(block, sides, width):
    for axis, dim in sides:
        count = lax.axis_size(axis)
        forward = [(i, i + 1) for i in range(count - 1)]
        backward = [(target, source) for source, target in forward]
        low = lax.ppermute(
            lax.slice_in_dim(block, block.shape[dim] - width, None, axis=dim), axis, forward
        )
        high = lax.ppermute(lax.slice_in_dim(block, 0, width, axis=dim), axis, backward)
        block = jnp.concatenate([low, block, high], axis=dim)
    return block


def from_behind(value, axis, steps):
    count = lax.axis_size(axis)
    initial, last = (max(0, -steps), min(count, count - steps))
    return lax.ppermute(value, axis, [(source, source + steps) for source in range(initial, last)])


def phase_table(first_index, second_index, length):
    product = first_index[:, None] * second_index[None, :] % length
    return 2.0 * jnp.pi / length * product.astype(jnp.float32)


def faces_from(padded_rows):
    centre = padded_rows[1:-1]
    columns = jnp.pad(centre, ((0, 0), (1, 1)), mode="edge")
    north_face = 0.5 * (centre + padded_rows[:-2])
    south_face = 0.5 * (centre + padded_rows[2:])
    west_face = 0.5 * (centre + columns[:, :-2])
    east_face = 0.5 * (centre + columns[:, 2:])
    return (north_face, south_face, west_face, east_face)


def apply_faces(padded_rows, weights):
    north_face, south_face, west_face, east_face = weights
    centre = padded_rows[..., 1:-1, :]
    lead_pad = [(0, 0)] * (centre.ndim - 1)
    columns = jnp.pad(centre, lead_pad + [(1, 1)])
    return (
        (north_face + south_face + west_face + east_face) * centre
        - north_face * padded_rows[..., :-2, :]
        - south_face * padded_rows[..., 2:, :]
        - west_face * columns[..., :-2]
        - east_face * columns[..., 2:]
    )


def high_dot(first_mat, second_mat):
    return jnp.dot(
        first_mat, second_mat, precision=lax.Precision.HIGHEST, preferred_element_type=jnp.float32
    )


def shards(iterate, forcing, initial_state, diffusivity):
    steps_dev, rows_dev, columns_dev = iterate.shape
    time_devices = lax.axis_size("tm")
    row_devices = lax.axis_size("rows")
    time_rank = lax.axis_index("tm")
    row_rank = lax.axis_index("rows")
    length = steps_dev * time_devices
    cell_count = rows_dev * row_devices * columns_dev
    rimmed = extended(diffusivity, (("rows", 0),), 1)
    top_row = jnp.where(row_rank == 0, diffusivity[:1], rimmed[:1])
    bottom_row = jnp.where(row_rank == row_devices - 1, diffusivity[-1:], rimmed[-1:])
    rimmed = jnp.concatenate([top_row, rimmed[1:-1], bottom_row], axis=0)
    local_faces = faces_from(rimmed)
    arriving = from_behind(iterate[-1], "tm", 1)
    first_previous = jnp.where(time_rank == 0, initial_state, arriving)
    previous = jnp.concatenate([first_previous[None], iterate[:-1]], axis=0)
    iterate_rim = extended(iterate, (("rows", 1),), 1)
    residual = (
        time_step * forcing + previous - iterate - time_step * apply_faces(iterate_rim, local_faces)
    )
    squares = lax.psum(jnp.sum(residual * residual, axis=(1, 2)), "rows")
    residual_rms = jnp.sqrt(squares / cell_count + rms_eps)
    step_index = time_rank * steps_dev + jnp.arange(steps_dev, dtype=jnp.int32)
    log_alpha = jnp.log(jnp.float32(circulant_alpha))
    growth = jnp.exp(log_alpha * step_index.astype(jnp.float32) / length)
    scaled = residual * growth[:, None, None]
    by_cells = lax.all_to_all(scaled, "tm", split_axis=1, concat_axis=0, tiled=True)
    slab_rows = by_cells.shape[1]
    all_index = jnp.arange(length, dtype=jnp.int32)
    angles = phase_table(all_index, all_index, length)
    flat_cells = by_cells.reshape(length, slab_rows * columns_dev)
    spectrum_real = high_dot(jnp.cos(angles), flat_cells)
    spectrum_imag = high_dot(-jnp.sin(angles), flat_cells)
    spectrum = jnp.stack([spectrum_real, spectrum_imag]).reshape(2, length, slab_rows, columns_dev)
    by_freq = lax.all_to_all(spectrum, "tm", split_axis=1, concat_axis=2, tiled=True)
    freq_index = time_rank * steps_dev + jnp.arange(steps_dev, dtype=jnp.int32)

    def rim_rows(values):
        return extended(values, (("rows", 2),), 1)

    def reduce_sums(values):
        return lax.psum(values, "rows")

    root_alpha = jnp.exp(log_alpha / length)
    freq_angle = 2.0 * jnp.pi / length * freq_index.astype(jnp.float32)
    real_shift = (1.0 - root_alpha * jnp.cos(freq_angle))[:, None, None]
    imag_shift = (root_alpha * jnp.sin(freq_angle))[:, None, None]

    def operate(values, orientation):
        spread = time_step * apply_faces(rim_rows(values), local_faces)
        swapped = jnp.stack([-values[1], values[0]])
        return real_shift * values + orientation * imag_shift * swapped + spread

    def freq_norm(values):
        return jnp.sum(values * values, axis=(0, 2, 3))

    def expand(values):
        return values[None, :, None, None]

    solution = jnp.zeros_like(by_freq)
    normal = operate(by_freq, -1.0)
    gamma_now = reduce_sums(freq_norm(normal))
    search = normal
    remain = by_freq
    for iteration in range(CG_ITERS):
        image_now = operate(search, 1.0)
        step_rate = gamma_now / reduce_sums(freq_norm(image_now))
        solution = solution + expand(step_rate) * search
        if iteration + 1 < CG_ITERS:
            remain = remain - expand(step_rate) * image_now
            normal = operate(remain, -1.0)
            gamma_next = reduce_sums(freq_norm(normal))
            search = normal + expand(gamma_next / gamma_now) * search
            gamma_now = gamma_next
    back_cells = lax.all_to_all(solution, "tm", split_axis=2, concat_axis=1, tiled=True)
    inverse_angles = phase_table(all_index, all_index, length)
    flat_real = back_cells[0].reshape(length, slab_rows * columns_dev)
    flat_imag = back_cells[1].reshape(length, slab_rows * columns_dev)
    correction = high_dot(jnp.cos(inverse_angles) / length, flat_real) - high_dot(
        jnp.sin(inverse_angles) / length, flat_imag
    )
    correction = correction.reshape(length, slab_rows, columns_dev)
    own_steps = lax.all_to_all(correction, "tm", split_axis=0, concat_axis=1, tiled=True)
    updated = iterate + own_steps / growth[:, None, None]
    return (updated, residual_rms)


def solution(mesh):
    placed = (
        P(("groups", "tm"), "rows", None),
        P(("groups", "tm"), "rows", None),
        P(("groups", "rows"), None),
        P(("groups", "rows"), None),
    )
    return jax.shard_map(
        shards,
        mesh=mesh,
        in_specs=placed,
        out_specs=(P(("groups", "tm"), "rows", None), P(("groups", "tm"))),
        check_vma=False,
    )
```

profile of v0, /device:TPU:0, one launch (start us, length us, event | category | flops | bytes accessed | tf_op | source)
XLA Modules:
  0.0 287.9 jit_solution(17938583159256987728)
XLA Ops:
  3.5 3.0 %collective-permute-start.3 = (f32[2,1,512]{2,1,0:T(1,128)S(1)}, f32[2,1,512]{2,1,0:T(1,128)S(1)}, u32[]{:S(2)}, u32[]{:S(2)}) collective-permute-start(f32[2,1,512]{2,1,0:T(1,128)S(1)} %get-tuple-element.53), channel_id=1, source_target_pairs={{0,1},{2,3},{4,5},{6,7},{8,9},{10,11},{12,13},{14,15},{16,17},{18,... | collective-permute-start | bytes 12296 | tf_op jit(solution)/shard_map/ppermute | solution.py:19
  7.8 2.1 slice_bitcast_fusion
  9.9 5.1 %collective-permute-start = (f32[256,512]{1,0:T(8,128)}, f32[256,512]{1,0:T(8,128)S(1)}, u32[]{:S(2)}, u32[]{:S(2)}) collective-permute-start(f32[256,512]{1,0:T(8,128)} %get-tuple-element.51), channel_id=1, source_target_pairs={{0,2},{2,4},{4,6},{6,8},{8,10},{10,12},{12,14},{1,3},{3,5},{5,7},{... | collective-permute-start | bytes 1572872 | tf_op jit(solution)/shard_map/ppermute | solution.py:30
  15.1 2.7 collective-permute-start.1
  19.1 8.3 %collective-permute-done = f32[256,512]{1,0:T(8,128)S(1)} collective-permute-done((f32[256,512]{1,0:T(8,128)}, f32[256,512]{1,0:T(8,128)S(1)}, u32[]{:S(2)}, u32[]{:S(2)}) %collective-permute-start) | collective-permute-done | bytes 524320 | tf_op jit(solution)/shard_map/ppermute | solution.py:30
  29.6 32.5 %all_to_all.66 = f32[2,256,512]{2,0,1:T(2,128)S(1)} all-to-all(f32[2,256,512]{2,0,1:T(2,128)S(1)} %copy.31), channel_id=1, replica_groups=mesh['groups'=2,'tm'=8,'rows'=2] {'tm'}, dimensions={1} | all-to-all | bytes 2097152 | tf_op jit(solution)/shard_map/all_to_all | solution.py:94
  62.3 1.5 convolution_bitcast_fusion
  63.8 1.5 convolution_bitcast_fusion.1
  65.7 2.6 copy.35
  68.2 3.6 %all-to-all-start.1 = ((f32[2,16,32,512]{3,2,0,1:T(8,128)}), f32[2,16,32,512]{3,2,0,1:T(8,128)S(1)}, u32[]{:S(2)}, u32[]{:S(2)}) async-start(f32[2,16,32,512]{3,2,0,1:T(8,128)} %copy.35), calls=%async_computation.1 | async-start | bytes 4194304 | tf_op jit(solution)/shard_map/all_to_all | solution.py:102
  72.0 47.8 %all-to-all-done.1 = f32[2,16,32,512]{3,2,0,1:T(8,128)S(1)} async-done(((f32[2,16,32,512]{3,2,0,1:T(8,128)}), f32[2,16,32,512]{3,2,0,1:T(8,128)S(1)}, u32[]{:S(2)}, u32[]{:S(2)}) %all-to-all-start.1) | async-done | bytes 2097184 | tf_op jit(solution)/shard_map/all_to_all | solution.py:102
  121.3 1.3 collective-permute-start.6
  124.6 2.5 multiply_reduce_fusion.4
  127.1 3.0 %collective-permute-start.7 = (f32[2,2,1,512]{3,2,1,0:T(1,128)S(1)}, f32[2,2,1,512]{3,2,1,0:T(1,128)S(1)}, u32[]{:S(2)}, u32[]{:S(2)}) collective-permute-start(f32[2,2,1,512]{3,2,1,0:T(1,128)S(1)} %get-tuple-element.45), channel_id=1, source_target_pairs={{0,1},{2,3},{4,5},{6,7},{8,9},{10,11},{12,13},{14,15},{16,17},{18,... | collective-permute-start | bytes 24584 | tf_op jit(solution)/shard_map/ppermute | solution.py:19
  130.1 1.5 collective-permute-start.8
  131.9 1.3 collective-permute-done.8
  133.2 3.4 %multiply_reduce_fusion.3 = (f32[2]{0:T(128)S(1)}, f32[2,2,256,512]{3,2,1,0:T(8,128)}) fusion(f32[256,512]{1,0:T(8,128)S(1)} %copy-done.15, f32[2,2,256,512]{3,2,1,0:T(8,128)S(1)} %get-tuple-element.19, f32[256,512]{1,0:T(8,128)S(1)} %copy-done.9, f32[2,2,1,512]{3,2,1,0:T(1,128)S(1)} %collective-permute-done.8, f32[256,512]{1,0:T(8,128)S(1)} %copy-done.3, ...), kind=kLoop, calls=%fused_computation.109 | loop fusion | flops 9961470 | bytes 8929304 | tf_op jit(solution)/shard_map/reduce_sum | solution.py:122
  136.6 2.4 all-reduce.8
  139.1 2.8 multiply_subtract_fusion.1
  141.9 2.1 collective-permute-start.9
  144.0 1.4 collective-permute-start.10
  145.7 1.5 collective-permute-done.10
  147.2 3.5 %multiply_reduce_fusion.2 = (f32[2]{0:T(128)S(1)}, f32[2,2,256,512]{3,2,1,0:T(8,128)}) fusion(f32[256,512]{1,0:T(8,128)S(1)} %copy-done.16, f32[2,2,256,512]{3,2,1,0:T(8,128)S(1)} %multiply_subtract_fusion.1, f32[256,512]{1,0:T(8,128)S(1)} %copy-done.10, f32[2,2,1,512]{3,2,1,0:T(1,128)S(1)} %collective-permute-done.10, f32[256,512]{1,0:T(8,128)S(1)} %copy-done.4, ...), kind=kLoop, calls=%fused_computation.107 | loop fusion | flops 9961470 | bytes 8929304 | tf_op jit(solution)/shard_map/reduce_sum | solution.py:122
  150.7 2.4 psum.51
  153.2 2.1 multiply_add_fusion.2
  155.4 2.1 collective-permute-start.11
  157.5 1.4 collective-permute-start.12
  159.2 1.5 collective-permute-done.12
  160.7 3.5 %multiply_reduce_fusion.1 = (f32[2]{0:T(128)S(1)}, f32[2,2,256,512]{3,2,1,0:T(8,128)}) fusion(f32[256,512]{1,0:T(8,128)S(1)} %copy-done.17, f32[2,2,256,512]{3,2,1,0:T(8,128)S(1)} %multiply_add_fusion.2, f32[256,512]{1,0:T(8,128)S(1)} %copy-done.11, f32[2,2,1,512]{3,2,1,0:T(1,128)S(1)} %collective-permute-done.12, f32[256,512]{1,0:T(8,128)S(1)} %copy-done.5, ...), kind=kLoop, calls=%fused_computation.105 | loop fusion | flops 9961470 | bytes 8929304 | tf_op jit(solution)/shard_map/reduce_sum | solution.py:122
  164.2 2.4 psum.52
  166.7 2.8 multiply_subtract_fusion
  169.5 2.1 collective-permute-start.13
  171.6 1.4 collective-permute-start.14
  173.3 1.5 collective-permute-done.14
  174.8 3.5 %multiply_reduce_fusion = (f32[2]{0:T(128)S(1)}, f32[2,2,256,512]{3,2,1,0:T(8,128)}) fusion(f32[256,512]{1,0:T(8,128)S(1)} %copy-done.18, f32[2,2,256,512]{3,2,1,0:T(8,128)S(1)} %multiply_subtract_fusion, f32[256,512]{1,0:T(8,128)S(1)} %copy-done.12, f32[2,2,1,512]{3,2,1,0:T(1,128)S(1)} %collective-permute-done.14, f32[256,512]{1,0:T(8,128)S(1)} %copy-done.6, ...), kind=kLoop, calls=%fused_computation.103 | loop fusion | flops 9961470 | bytes 8929304 | tf_op jit(solution)/shard_map/reduce_sum | solution.py:122
  178.3 2.4 psum.53
  180.8 2.8 multiply_add_fusion.1
  183.6 2.1 collective-permute-start.15
  185.7 1.4 collective-permute-start.16
  187.4 1.5 collective-permute-done.16
  188.9 2.5 fusion.36
  191.4 2.7 all-reduce.7
  194.0 3.1 %multiply_add_fusion = f32[2,2,256,512]{3,2,1,0:T(8,128)S(1)} fusion(f32[2,2,256,512]{3,2,1,0:T(8,128)} %copy-done, f32[2,2,256,512]{3,2,1,0:T(8,128)S(1)} %get-tuple-element.19, f32[2]{0:T(128)S(1)} %div.42, f32[2]{0:T(128)S(1)} %div.40, f32[2]{0:T(128)S(1)} %div.38, f32[2,2,256,512]{3,2,1,0:T(8,128)} %get-tuple-element.11, f32[2]{0:T(128)S(1)} %div.41), kind=kLoop, calls=%fused_computation.101 | loop fusion | flops 3670016 | bytes 8388640 | tf_op jit(solution)/shard_map/add | solution.py:135
  197.1 1.6 copy.40
  198.7 52.6 %all_to_all.67 = f32[2,2,256,512]{3,1,0,2:T(2,128)S(1)} all-to-all(f32[2,2,256,512]{3,1,0,2:T(2,128)S(1)} %copy.40), channel_id=1, replica_groups=mesh['groups'=2,'tm'=8,'rows'=2] {'tm'}, dimensions={2} | all-to-all | bytes 4194304 | tf_op jit(solution)/shard_map/all_to_all | solution.py:142
  255.6 1.6 copy.48
  257.2 3.8 %all-to-all-start.3 = ((f32[16,32,512]{2,1,0:T(8,128)}), f32[16,32,512]{2,1,0:T(8,128)S(1)}, u32[]{:S(2)}, u32[]{:S(2)}) async-start(f32[16,32,512]{2,1,0:T(8,128)} %bitcast.34), calls=%async_computation.3 | async-start | bytes 2097152 | tf_op jit(solution)/shard_map/all_to_all | solution.py:150
  261.5 25.0 %all-to-all-done.3 = f32[16,32,512]{2,1,0:T(8,128)S(1)} async-done(((f32[16,32,512]{2,1,0:T(8,128)}), f32[16,32,512]{2,1,0:T(8,128)S(1)}, u32[]{:S(2)}, u32[]{:S(2)}) %all-to-all-start.3) | async-done | bytes 1048608 | tf_op jit(solution)/shard_map/all_to_all | solution.py:150
  (112 shorter events, 19.2 us)
Async XLA Ops:
  0.6 14.3 %copy-start.23 = (f32[256,512]{1,0:T(8,128)S(1)}, f32[256,512]{1,0:T(8,128)}, u32[]{:S(2)}) copy-start(f32[256,512]{1,0:T(8,128)} %param.7) | copy-start | bytes 1572868
  1.4 13.6 %collective-permute-start.2 = (f32[1,512]{1,0:T(1,128)S(1)}, f32[1,512]{1,0:T(1,128)S(1)}, u32[]{:S(2)}, u32[]{:S(2)}) collective-permute-start(f32[1,512]{1,0:T(1,128)S(1)} %slice.228), channel_id=1, source_target_pairs={{1,0},{3,2},{5,4},{7,6},{9,8},{11,10},{13,12},{15,14},{17,16},{19,... | collective-permute-start | bytes 6152 | tf_op jit(solution)/shard_map/ppermute | solution.py:22
  3.5 24.0 %collective-permute-start.3 = (f32[2,1,512]{2,1,0:T(1,128)S(1)}, f32[2,1,512]{2,1,0:T(1,128)S(1)}, u32[]{:S(2)}, u32[]{:S(2)}) collective-permute-start(f32[2,1,512]{2,1,0:T(1,128)S(1)} %get-tuple-element.53), channel_id=1, source_target_pairs={{0,1},{2,3},{4,5},{6,7},{8,9},{10,11},{12,13},{14,15},{16,17},{18,... | collective-permute-start | bytes 12296 | tf_op jit(solution)/shard_map/ppermute | solution.py:19
  6.5 21.0 %collective-permute-start.4 = (f32[2,1,512]{2,1,0:T(1,128)S(1)}, f32[2,1,512]{2,1,0:T(1,128)S(1)}, u32[]{:S(2)}, u32[]{:S(2)}) collective-permute-start(f32[2,1,512]{2,1,0:T(1,128)S(1)} %get-tuple-element.54), channel_id=1, source_target_pairs={{1,0},{3,2},{5,4},{7,6},{9,8},{11,10},{13,12},{15,14},{17,16},{19,... | collective-permute-start | bytes 12296 | tf_op jit(solution)/shard_map/ppermute | solution.py:22
  9.9 17.5 %copy-start.25 = (f32[256,512]{1,0:T(8,128)S(1)}, f32[256,512]{1,0:T(8,128)}, u32[]{:S(2)}) copy-start(f32[256,512]{1,0:T(8,128)} %param.6) | copy-start | bytes 1572868
  9.9 17.5 %collective-permute-start = (f32[256,512]{1,0:T(8,128)}, f32[256,512]{1,0:T(8,128)S(1)}, u32[]{:S(2)}, u32[]{:S(2)}) collective-permute-start(f32[256,512]{1,0:T(8,128)} %get-tuple-element.51), channel_id=1, source_target_pairs={{0,2},{2,4},{4,6},{6,8},{8,10},{10,12},{12,14},{1,3},{3,5},{5,7},{... | collective-permute-start | bytes 1572872 | tf_op jit(solution)/shard_map/ppermute | solution.py:30
  15.1 3.6 %collective-permute-start.1 = (f32[1,512]{1,0:T(1,128)S(1)}, f32[1,512]{1,0:T(1,128)S(1)}, u32[]{:S(2)}, u32[]{:S(2)}) collective-permute-start(f32[1,512]{1,0:T(1,128)S(1)} %get-tuple-element.58), channel_id=1, source_target_pairs={{0,1},{2,3},{4,5},{6,7},{8,9},{10,11},{12,13},{14,15},{16,17},{18,... | collective-permute-start | bytes 6152 | tf_op jit(solution)/shard_map/ppermute | solution.py:19
  18.6 8.8 %copy-start.21 = (f32[2,256,512]{2,1,0:T(8,128)S(1)}, f32[2,256,512]{2,1,0:T(8,128)}, u32[]{:S(2)}) copy-start(f32[2,256,512]{2,1,0:T(8,128)} %param.4) | copy-start | bytes 3145732
  18.7 8.8 %copy-start.24 = (f32[2,256,512]{2,1,0:T(8,128)S(1)}, f32[2,256,512]{2,1,0:T(8,128)}, u32[]{:S(2)}) copy-start(f32[2,256,512]{2,1,0:T(8,128)} %param.5) | copy-start | bytes 3145732
  19.1 9.6 %copy-start.2 = (f32[256,512]{1,0:T(8,128)}, f32[256,512]{1,0:T(8,128)S(1)}, u32[]{:S(2)}) copy-start(f32[256,512]{1,0:T(8,128)S(1)} %get-tuple-element.22) | copy-start | bytes 1572868
  19.1 9.6 %copy-start.8 = (f32[256,512]{1,0:T(8,128)}, f32[256,512]{1,0:T(8,128)S(1)}, u32[]{:S(2)}) copy-start(f32[256,512]{1,0:T(8,128)S(1)} %get-tuple-element.23) | copy-start | bytes 1572868
  19.1 9.5 %copy-start.14 = (f32[256,512]{1,0:T(8,128)}, f32[256,512]{1,0:T(8,128)S(1)}, u32[]{:S(2)}) copy-start(f32[256,512]{1,0:T(8,128)S(1)} %get-tuple-element.24) | copy-start | bytes 1572868
  68.2 51.5 %all-to-all-start.1 = ((f32[2,16,32,512]{3,2,0,1:T(8,128)}), f32[2,16,32,512]{3,2,0,1:T(8,128)S(1)}, u32[]{:S(2)}, u32[]{:S(2)}) async-start(f32[2,16,32,512]{3,2,0,1:T(8,128)} %copy.35), calls=%async_computation.1 | async-start | bytes 4194304 | tf_op jit(solution)/shard_map/all_to_all | solution.py:102
  120.0 4.4 %copy-start.20 = (f32[2,2,8,32,512]{4,3,2,1,0:T(8,128)}, f32[2,2,8,32,512]{4,3,2,1,0:T(8,128)S(1)}, u32[]{:S(2)}) copy-start(f32[2,2,8,32,512]{4,3,2,1,0:T(8,128)S(1)} %copy.37) | copy-start | bytes 6291460
  120.0 3.4 %collective-permute-start.5 = (f32[2,2,1,512]{3,2,1,0:T(1,128)S(1)}, f32[2,2,1,512]{3,2,1,0:T(1,128)S(1)}, u32[]{:S(2)}, u32[]{:S(2)}) collective-permute-start(f32[2,2,1,512]{3,2,1,0:T(1,128)S(1)} %get-tuple-element.49), channel_id=1, source_target_pairs={{0,1},{2,3},{4,5},{6,7},{8,9},{10,11},{12,13},{14,15},{16,17},{18,... | collective-permute-start | bytes 24584 | tf_op jit(solution)/shard_map/ppermute | solution.py:19
  121.3 3.1 %collective-permute-start.6 = (f32[2,2,1,512]{3,2,1,0:T(1,128)S(1)}, f32[2,2,1,512]{3,2,1,0:T(1,128)S(1)}, u32[]{:S(2)}, u32[]{:S(2)}) collective-permute-start(f32[2,2,1,512]{3,2,1,0:T(1,128)S(1)} %get-tuple-element.50), channel_id=1, source_target_pairs={{1,0},{3,2},{5,4},{7,6},{9,8},{11,10},{13,12},{15,14},{17,16},{19,... | collective-permute-start | bytes 24584 | tf_op jit(solution)/shard_map/ppermute | solution.py:22
  123.2 1.2 copy-start.3
  123.2 1.2 copy-start.9
  123.2 1.3 copy-start.15
  127.1 4.7 %collective-permute-start.7 = (f32[2,2,1,512]{3,2,1,0:T(1,128)S(1)}, f32[2,2,1,512]{3,2,1,0:T(1,128)S(1)}, u32[]{:S(2)}, u32[]{:S(2)}) collective-permute-start(f32[2,2,1,512]{3,2,1,0:T(1,128)S(1)} %get-tuple-element.45), channel_id=1, source_target_pairs={{0,1},{2,3},{4,5},{6,7},{8,9},{10,11},{12,13},{14,15},{16,17},{18,... | collective-permute-start | bytes 24584 | tf_op jit(solution)/shard_map/ppermute | solution.py:19
  130.1 3.1 %collective-permute-start.8 = (f32[2,2,1,512]{3,2,1,0:T(1,128)S(1)}, f32[2,2,1,512]{3,2,1,0:T(1,128)S(1)}, u32[]{:S(2)}, u32[]{:S(2)}) collective-permute-start(f32[2,2,1,512]{3,2,1,0:T(1,128)S(1)} %get-tuple-element.46), channel_id=1, source_target_pairs={{1,0},{3,2},{5,4},{7,6},{9,8},{11,10},{13,12},{15,14},{17,16},{19,... | collective-permute-start | bytes 24584 | tf_op jit(solution)/shard_map/ppermute | solution.py:22
  141.8 5.4 %copy-start.1 = (f32[2,2,256,512]{3,2,1,0:T(8,128)}, f32[2,2,256,512]{3,2,1,0:T(8,128)S(1)}, u32[]{:S(2)}) copy-start(f32[2,2,256,512]{3,2,1,0:T(8,128)S(1)} %multiply_subtract_fusion.1) | copy-start | bytes 6291460
  141.9 3.8 %collective-permute-start.9 = (f32[2,2,1,512]{3,2,1,0:T(1,128)S(1)}, f32[2,2,1,512]{3,2,1,0:T(1,128)S(1)}, u32[]{:S(2)}, u32[]{:S(2)}) collective-permute-start(f32[2,2,1,512]{3,2,1,0:T(1,128)S(1)} %get-tuple-element.41), channel_id=1, source_target_pairs={{0,1},{2,3},{4,5},{6,7},{8,9},{10,11},{12,13},{14,15},{16,17},{18,... | collective-permute-start | bytes 24584 | tf_op jit(solution)/shard_map/ppermute | solution.py:19
  144.0 3.2 %copy-start.4 = (f32[256,512]{1,0:T(8,128)S(1)}, f32[256,512]{1,0:T(8,128)}, u32[]{:S(2)}) copy-start(f32[256,512]{1,0:T(8,128)} %copy-done.2) | copy-start | bytes 1572868
  144.0 3.2 %copy-start.10 = (f32[256,512]{1,0:T(8,128)S(1)}, f32[256,512]{1,0:T(8,128)}, u32[]{:S(2)}) copy-start(f32[256,512]{1,0:T(8,128)} %copy-done.8) | copy-start | bytes 1572868
  144.0 3.2 %copy-start.16 = (f32[256,512]{1,0:T(8,128)S(1)}, f32[256,512]{1,0:T(8,128)}, u32[]{:S(2)}) copy-start(f32[256,512]{1,0:T(8,128)} %copy-done.14) | copy-start | bytes 1572868
  144.0 3.2 %collective-permute-start.10 = (f32[2,2,1,512]{3,2,1,0:T(1,128)S(1)}, f32[2,2,1,512]{3,2,1,0:T(1,128)S(1)}, u32[]{:S(2)}, u32[]{:S(2)}) collective-permute-start(f32[2,2,1,512]{3,2,1,0:T(1,128)S(1)} %get-tuple-element.42), channel_id=1, source_target_pairs={{1,0},{3,2},{5,4},{7,6},{9,8},{11,10},{13,12},{15,14},{17,16},{19,... | collective-permute-start | bytes 24584 | tf_op jit(solution)/shard_map/ppermute | solution.py:22
  155.3 5.3 %copy-start = (f32[2,2,256,512]{3,2,1,0:T(8,128)}, f32[2,2,256,512]{3,2,1,0:T(8,128)S(1)}, u32[]{:S(2)}) copy-start(f32[2,2,256,512]{3,2,1,0:T(8,128)S(1)} %multiply_add_fusion.2) | copy-start | bytes 6291460
  155.4 3.8 %collective-permute-start.11 = (f32[2,2,1,512]{3,2,1,0:T(1,128)S(1)}, f32[2,2,1,512]{3,2,1,0:T(1,128)S(1)}, u32[]{:S(2)}, u32[]{:S(2)}) collective-permute-start(f32[2,2,1,512]{3,2,1,0:T(1,128)S(1)} %get-tuple-element.37), channel_id=1, source_target_pairs={{0,1},{2,3},{4,5},{6,7},{8,9},{10,11},{12,13},{14,15},{16,17},{18,... | collective-permute-start | bytes 24584 | tf_op jit(solution)/shard_map/ppermute | solution.py:19
  157.4 3.2 %copy-start.5 = (f32[256,512]{1,0:T(8,128)S(1)}, f32[256,512]{1,0:T(8,128)}, u32[]{:S(2)}) copy-start(f32[256,512]{1,0:T(8,128)} %copy-done.2) | copy-start | bytes 1572868
  157.5 3.2 %copy-start.11 = (f32[256,512]{1,0:T(8,128)S(1)}, f32[256,512]{1,0:T(8,128)}, u32[]{:S(2)}) copy-start(f32[256,512]{1,0:T(8,128)} %copy-done.8) | copy-start | bytes 1572868
  157.5 3.2 %copy-start.17 = (f32[256,512]{1,0:T(8,128)S(1)}, f32[256,512]{1,0:T(8,128)}, u32[]{:S(2)}) copy-start(f32[256,512]{1,0:T(8,128)} %copy-done.14) | copy-start | bytes 1572868
  157.5 3.2 %collective-permute-start.12 = (f32[2,2,1,512]{3,2,1,0:T(1,128)S(1)}, f32[2,2,1,512]{3,2,1,0:T(1,128)S(1)}, u32[]{:S(2)}, u32[]{:S(2)}) collective-permute-start(f32[2,2,1,512]{3,2,1,0:T(1,128)S(1)} %get-tuple-element.38), channel_id=1, source_target_pairs={{1,0},{3,2},{5,4},{7,6},{9,8},{11,10},{13,12},{15,14},{17,16},{19,... | collective-permute-start | bytes 24584 | tf_op jit(solution)/shard_map/ppermute | solution.py:22
  169.5 3.8 %collective-permute-start.13 = (f32[2,2,1,512]{3,2,1,0:T(1,128)S(1)}, f32[2,2,1,512]{3,2,1,0:T(1,128)S(1)}, u32[]{:S(2)}, u32[]{:S(2)}) collective-permute-start(f32[2,2,1,512]{3,2,1,0:T(1,128)S(1)} %get-tuple-element.33), channel_id=1, source_target_pairs={{0,1},{2,3},{4,5},{6,7},{8,9},{10,11},{12,13},{14,15},{16,17},{18,... | collective-permute-start | bytes 24584 | tf_op jit(solution)/shard_map/ppermute | solution.py:19
  171.6 3.2 %copy-start.6 = (f32[256,512]{1,0:T(8,128)S(1)}, f32[256,512]{1,0:T(8,128)}, u32[]{:S(2)}) copy-start(f32[256,512]{1,0:T(8,128)} %copy-done.2) | copy-start | bytes 1572868
  171.6 3.2 %copy-start.12 = (f32[256,512]{1,0:T(8,128)S(1)}, f32[256,512]{1,0:T(8,128)}, u32[]{:S(2)}) copy-start(f32[256,512]{1,0:T(8,128)} %copy-done.8) | copy-start | bytes 1572868
  171.6 3.2 %copy-start.18 = (f32[256,512]{1,0:T(8,128)S(1)}, f32[256,512]{1,0:T(8,128)}, u32[]{:S(2)}) copy-start(f32[256,512]{1,0:T(8,128)} %copy-done.14) | copy-start | bytes 1572868
  171.6 3.2 %collective-permute-start.14 = (f32[2,2,1,512]{3,2,1,0:T(1,128)S(1)}, f32[2,2,1,512]{3,2,1,0:T(1,128)S(1)}, u32[]{:S(2)}, u32[]{:S(2)}) collective-permute-start(f32[2,2,1,512]{3,2,1,0:T(1,128)S(1)} %get-tuple-element.34), channel_id=1, source_target_pairs={{1,0},{3,2},{5,4},{7,6},{9,8},{11,10},{13,12},{15,14},{17,16},{19,... | collective-permute-start | bytes 24584 | tf_op jit(solution)/shard_map/ppermute | solution.py:22
  183.6 3.8 %collective-permute-start.15 = (f32[2,2,1,512]{3,2,1,0:T(1,128)S(1)}, f32[2,2,1,512]{3,2,1,0:T(1,128)S(1)}, u32[]{:S(2)}, u32[]{:S(2)}) collective-permute-start(f32[2,2,1,512]{3,2,1,0:T(1,128)S(1)} %get-tuple-element.29), channel_id=1, source_target_pairs={{0,1},{2,3},{4,5},{6,7},{8,9},{10,11},{12,13},{14,15},{16,17},{18,... | collective-permute-start | bytes 24584 | tf_op jit(solution)/shard_map/ppermute | solution.py:19
  185.7 3.2 %copy-start.7 = (f32[256,512]{1,0:T(8,128)S(1)}, f32[256,512]{1,0:T(8,128)}, u32[]{:S(2)}) copy-start(f32[256,512]{1,0:T(8,128)} %copy-done.2) | copy-start | bytes 1572868
  185.7 3.2 %copy-start.13 = (f32[256,512]{1,0:T(8,128)S(1)}, f32[256,512]{1,0:T(8,128)}, u32[]{:S(2)}) copy-start(f32[256,512]{1,0:T(8,128)} %copy-done.8) | copy-start | bytes 1572868
  185.7 3.2 %copy-start.19 = (f32[256,512]{1,0:T(8,128)S(1)}, f32[256,512]{1,0:T(8,128)}, u32[]{:S(2)}) copy-start(f32[256,512]{1,0:T(8,128)} %copy-done.14) | copy-start | bytes 1572868
  185.7 3.2 %collective-permute-start.16 = (f32[2,2,1,512]{3,2,1,0:T(1,128)S(1)}, f32[2,2,1,512]{3,2,1,0:T(1,128)S(1)}, u32[]{:S(2)}, u32[]{:S(2)}) collective-permute-start(f32[2,2,1,512]{3,2,1,0:T(1,128)S(1)} %get-tuple-element.30), channel_id=1, source_target_pairs={{1,0},{3,2},{5,4},{7,6},{9,8},{11,10},{13,12},{15,14},{17,16},{19,... | collective-permute-start | bytes 24584 | tf_op jit(solution)/shard_map/ppermute | solution.py:22
  257.2 29.4 %copy-start.22 = (f32[2,256,512]{2,1,0:T(8,128)S(1)}, f32[2,256,512]{2,1,0:T(8,128)}, u32[]{:S(2)}) copy-start(f32[2,256,512]{2,1,0:T(8,128)} %param.4) | copy-start | bytes 3145732
  257.2 29.3 %all-to-all-start.3 = ((f32[16,32,512]{2,1,0:T(8,128)}), f32[16,32,512]{2,1,0:T(8,128)S(1)}, u32[]{:S(2)}, u32[]{:S(2)}) async-start(f32[16,32,512]{2,1,0:T(8,128)} %bitcast.34), calls=%async_computation.3 | async-start | bytes 2097152 | tf_op jit(solution)/shard_map/all_to_all | solution.py:150
where the time goes:
time: 289 us; the launch traced here: 288 us
  blocking collectives  97.5 us (34%)
  waiting for transfers between devices  90.2 us (31%)
  starting transfers between devices  41.9 us (14%)
  other arithmetic  38 us (13%)
  local copies, waits for them, and re-layouts  13.8 us (5%)
  matrix products  5.1 us (2%)
    all_to_all x1, blocking collectives, shards(): lax.all_to_all(solution, 'tm', split_axis=2, concat_axis=1, tiled=True)  52.6 us
    all_to_all x1, waiting for transfers between devices, shards(): lax.all_to_all(spectrum, 'tm', split_axis=1, concat_axis=2, tiled=True)  47.8 us
    all_to_all x1, blocking collectives, shards(): lax.all_to_all(scaled, 'tm', split_axis=1, concat_axis=0, tiled=True)  32.5 us
    all_to_all x1, waiting for transfers between devices, shards(): lax.all_to_all(correction, 'tm', split_axis=0, concat_axis=1, tiled=True)  25 us
    reduce_sum x6, other arithmetic, freq_norm(): return jnp.sum(values * values, axis=(0, 2, 3))  19 us
    ppermute x8, starting transfers between devices, extended(): lax.ppermute(lax.slice_in_dim(block, block.shape[dim] - width, None, axis...  18.4 us
    psum x5, blocking collectives, reduce_sums(): return lax.psum(values, 'rows')  12.4 us
    ppermute x8, starting transfers between devices, extended(): lax.ppermute(lax.slice_in_dim(block, 0, width, axis=dim), axis, backward)  11 us
  transfers between devices with their start and end apart: 19, of which 10 were waited for; matrix products, arithmetic and copies ran while one was open for 2% of the time, Pallas kernels for 0%

commit v1 on v0

v1 whole, which is shorter than its diff:
```python
import functools
import math

import jax
import jax.numpy as jnp
import numpy as np
from jax import lax
from jax.experimental import pallas as pl
from jax.experimental.pallas import tpu as pltpu
from jax.sharding import PartitionSpec as P

CG_ITERS = 3
DEPTH = 2 * CG_ITERS
MOMENTS = 2 * DEPTH + 1

circulant_alpha = 0.05
time_step = 0.5
rms_eps = 1e-06


def extended(block, sides, width):
    for axis, dim in sides:
        count = lax.axis_size(axis)
        forward = [(i, i + 1) for i in range(count - 1)]
        backward = [(target, source) for source, target in forward]
        low = lax.ppermute(
            lax.slice_in_dim(block, block.shape[dim] - width, None, axis=dim), axis, forward
        )
        high = lax.ppermute(lax.slice_in_dim(block, 0, width, axis=dim), axis, backward)
        block = jnp.concatenate([low, block, high], axis=dim)
    return block


def from_behind(value, axis, steps):
    count = lax.axis_size(axis)
    initial, last = (max(0, -steps), min(count, count - steps))
    return lax.ppermute(value, axis, [(source, source + steps) for source in range(initial, last)])


def faces_from(padded_rows):
    centre = padded_rows[1:-1]
    columns = jnp.pad(centre, ((0, 0), (1, 1)), mode="edge")
    north_face = 0.5 * (centre + padded_rows[:-2])
    south_face = 0.5 * (centre + padded_rows[2:])
    west_face = 0.5 * (centre + columns[:, :-2])
    east_face = 0.5 * (centre + columns[:, 2:])
    return (north_face, south_face, west_face, east_face)


def apply_faces(padded_rows, weights):
    north_face, south_face, west_face, east_face = weights
    centre = padded_rows[..., 1:-1, :]
    lead_pad = [(0, 0)] * (centre.ndim - 1)
    columns = jnp.pad(centre, lead_pad + [(1, 1)])
    return (
        (north_face + south_face + west_face + east_face) * centre
        - north_face * padded_rows[..., :-2, :]
        - south_face * padded_rows[..., 2:, :]
        - west_face * columns[..., :-2]
        - east_face * columns[..., 2:]
    )


def growth_of(length):
    return np.exp(math.log(circulant_alpha) * np.arange(length) / length)


def forward_matrix(length):
    half = length // 2
    steps = np.arange(length)
    table = np.zeros((length, length))
    for j in range(half):
        turn = 2 * np.pi * ((j * steps) % length) / length
        table[j] = np.cos(turn)
        table[half + j] = -np.sin(turn)
    table[half] = np.cos(2 * np.pi * ((half * steps) % length) / length)
    return table * growth_of(length)[None, :]


def inverse_matrix(length):
    half = length // 2
    steps = np.arange(length)
    table = np.zeros((length, length))
    for j in range(half):
        turn = 2 * np.pi * ((j * steps) % length) / length
        weight = 1.0 if j == 0 else 2.0
        table[:, j] = weight * np.cos(turn) / length
        table[:, half + j] = -weight * np.sin(turn) / length
    table[:, half] = np.cos(2 * np.pi * ((half * steps) % length) / length) / length
    return table / growth_of(length)[:, None]


def block_forward(length, rows):
    full = np.einsum("cn,rs->rcns", forward_matrix(length), np.eye(rows))
    return full.reshape(rows * length, length * rows).astype(np.float32)


def block_inverse(length, rows):
    full = np.einsum("nc,rs->nrsc", inverse_matrix(length), np.eye(rows))
    return full.reshape(length * rows, rows * length).astype(np.float32)


def channel_shifts(length):
    half = length // 2
    root = math.exp(math.log(circulant_alpha) / length)
    freq = np.concatenate([np.arange(half), np.arange(half)])
    freq[half] = half
    angle = 2 * np.pi * freq / length
    real = 1 - root * np.cos(angle)
    imag = root * np.sin(angle)
    imag[0] = 0.0
    imag[half] = 0.0
    return real, imag


def power_table(length):
    real, imag = channel_shifts(length)
    base = np.stack([real**2 + imag**2, 2 * real, np.ones_like(real)], axis=1)
    powers = [np.concatenate([np.ones((length, 1)), np.zeros((length, MOMENTS - 1))], axis=1)]
    for _ in range(DEPTH):
        last = powers[-1]
        following = np.zeros_like(last)
        for m in range(3):
            following[:, m:] += base[:, m : m + 1] * last[:, : MOMENTS - m]
        powers.append(following)
    return np.stack(powers)


def krylov_body(length, slab, halo, place_ref, pieces_ref, diff_ref, mix_ref, *rest):
    power_refs = rest[:DEPTH]
    moments_ref = rest[DEPTH]
    vectors = rest[DEPTH + 1 : 2 * DEPTH + 2]
    weights_ref = rest[2 * DEPTH + 2]
    rows = slab + 2 * halo
    columns = diff_ref.shape[-1]
    steps_dev = pieces_ref.shape[1] // rows

    centre = diff_ref[...]
    above = jnp.concatenate([centre[:1], centre[:-1]], axis=0)
    below = jnp.concatenate([centre[1:], centre[-1:]], axis=0)
    lane = lax.broadcasted_iota(jnp.int32, (rows, columns), 1)
    row = lax.broadcasted_iota(jnp.int32, (rows, columns), 0) + place_ref[0]
    left_edge = lane == 0
    right_edge = lane == columns - 1
    before = jnp.where(left_edge, centre, pltpu.roll(centre, 1, 1))
    after = jnp.where(right_edge, centre, pltpu.roll(centre, columns - 1, 1))
    quarter = 0.5 * time_step
    north = quarter * (centre + above)
    south = quarter * (centre + below)
    west = quarter * (centre + before)
    east = quarter * (centre + after)
    weights_ref[0] = north + south + west + east
    weights_ref[1] = jnp.where(row == 0, 0.0, north)
    weights_ref[2] = jnp.where(row == place_ref[1] - 1, 0.0, south)
    weights_ref[3] = jnp.where(left_edge, 0.0, west)
    weights_ref[4] = jnp.where(right_edge, 0.0, east)

    mix = mix_ref[...]
    starts = list(range(0, rows - 7, 8))
    if starts[-1] + 8 < rows:
        starts.append(rows - 8)
    for start in starts:
        cells = []
        for source in range(length // steps_dev):
            for step in range(steps_dev):
                at = step * rows + start
                cells.append(pieces_ref[source, at : at + 8, :])
        block = jnp.concatenate(cells, axis=0)
        vectors[0][start * length : (start + 8) * length, :] = jnp.dot(
            mix, block, precision=lax.Precision.HIGHEST, preferred_element_type=jnp.float32
        )

    def stencil(source, r):
        at = pl.multiple_of(r * length, 8)
        here = source[pl.ds(at, length), :]
        up = source[pl.ds(pl.multiple_of(at - length, 8), length), :]
        down = source[pl.ds(pl.multiple_of(at + length, 8), length), :]

        def weight(index):
            return weights_ref[index, pl.ds(r, 1), :]

        return here, (
            weight(0) * here
            - weight(1) * up
            - weight(2) * down
            - weight(3) * pltpu.roll(here, 1, 1)
            - weight(4) * pltpu.roll(here, columns - 1, 1)
        )

    lanes = lax.broadcasted_iota(jnp.int32, (length, 128), 1)
    table = jnp.zeros((length, 128), jnp.float32)

    def put(table, index, sums):
        return jnp.where(lanes == index, jnp.sum(sums, axis=1, keepdims=True), table)

    for power in range(DEPTH):
        source, target = vectors[power], vectors[power + 1]

        def plain(r, carry):
            _, value = stencil(source, r)
            target[pl.ds(pl.multiple_of(r * length, 8), length), :] = value
            return carry

        def summed(r, carry):
            here, value = stencil(source, r)
            if power + 1 < DEPTH:
                target[pl.ds(pl.multiple_of(r * length, 8), length), :] = value
            squares, products, last = carry
            squares = squares + here * here
            products = products + here * value
            if power + 1 == DEPTH:
                last = last + value * value
            return squares, products, last

        first, final = power + 1, rows - 1 - power
        if first < halo:
            lax.fori_loop(first, halo, plain, 0)
            lax.fori_loop(halo + slab, final, plain, 0)
        zero = jnp.zeros((length, columns), jnp.float32)
        squares, products, last = lax.fori_loop(
            halo, halo + slab, summed, (zero, zero, zero if power + 1 == DEPTH else 0.0)
        )
        table = put(table, 2 * power, squares)
        table = put(table, 2 * power + 1, products)
        if power + 1 == DEPTH:
            table = put(table, 2 * DEPTH, last)
        power_refs[power][...] = source[halo * length : (halo + slab) * length, :]
    moments_ref[...] = table


def combine_body(length, slab, moments_ref, table_ref, shift_ref, mix_ref, *rest):
    power_refs = rest[:DEPTH]
    out_ref = rest[DEPTH]
    steps_dev = out_ref.shape[1] // slab
    half = length // 2
    own = moments_ref[...]
    swapped = jnp.concatenate([own[half:], own[:half]], axis=0)
    channel = lax.broadcasted_iota(jnp.int32, own.shape, 0)
    alone = (channel == 0) | (channel == half)
    sums = jnp.where(alone, own, own + swapped)
    mu = [
        jnp.sum(sums * table_ref[k + 1], axis=1, keepdims=True) for k in range(2 * CG_ITERS)
    ]
    low1, low2 = mu[2] / mu[1], mu[3] / mu[1]
    pivot1 = mu[3] - low1 * mu[2]
    cross = mu[4] - low1 * mu[3]
    pivot2 = mu[5] - low2 * mu[3]
    right1 = mu[1] - low1 * mu[0]
    right2 = mu[2] - low2 * mu[0]
    low3 = cross / pivot1
    pivot2 = pivot2 - low3 * cross
    right2 = right2 - low3 * right1
    c2 = right2 / pivot2
    c1 = (right1 - cross * c2) / pivot1
    c0 = (mu[0] - mu[2] * c1 - mu[3] * c2) / mu[1]
    inner = c0 * table_ref[0] + c1 * table_ref[1] + c2 * table_ref[2]
    real = shift_ref[0]
    imag = shift_ref[1]
    lanes = lax.broadcasted_iota(jnp.int32, inner.shape, 1)
    outer = real * inner + jnp.where(lanes == 0, 0.0, pltpu.roll(inner, 1, 1))
    crossed = imag * inner
    sign = jnp.where(lax.broadcasted_iota(jnp.int32, inner.shape, 0) < half, 1.0, -1.0)
    crossed = sign * crossed
    columns = out_ref.shape[-1]

    def spread(values, index):
        return jnp.broadcast_to(values[:, index : index + 1], (length, columns))[None]

    for start in range(0, slab, 8):
        total = jnp.zeros((8, length, columns), jnp.float32)
        other = jnp.zeros((8, length, columns), jnp.float32)
        for power in range(DEPTH):
            here = power_refs[power][start * length : (start + 8) * length, :].reshape(
                8, length, columns
            )
            total = total + spread(outer, power) * here
            if power + 1 < DEPTH:
                flipped = jnp.concatenate([here[:, half:], here[:, :half]], axis=1)
                other = other + spread(crossed, power) * flipped
        block = (total + other).reshape(8 * length, columns)
        result = jnp.dot(
            mix_ref[...], block, precision=lax.Precision.HIGHEST, preferred_element_type=jnp.float32
        )
        for step in range(length):
            at = (step % steps_dev) * slab + start
            out_ref[step // steps_dev, at : at + 8, :] = result[step * 8 : step * 8 + 8]


def shards(iterate, forcing, initial_state, diffusivity):
    steps_dev, rows_dev, columns_dev = iterate.shape
    time_devices = lax.axis_size("tm")
    row_devices = lax.axis_size("rows")
    time_rank = lax.axis_index("tm")
    row_rank = lax.axis_index("rows")
    length = steps_dev * time_devices
    cell_count = rows_dev * row_devices * columns_dev
    slab = rows_dev // time_devices
    halo = DEPTH
    rows = slab + 2 * halo

    rimmed = extended(diffusivity, (("rows", 0),), halo)
    here = lax.broadcasted_iota(jnp.int32, (rimmed.shape[0], 1), 0)
    rimmed = jnp.where((row_rank == 0) & (here < halo), diffusivity[:1], rimmed)
    rimmed = jnp.where(
        (row_rank == row_devices - 1) & (here >= halo + rows_dev), diffusivity[-1:], rimmed
    )
    local_faces = faces_from(rimmed[halo - 1 : halo + rows_dev + 1])
    arriving = from_behind(iterate[-1], "tm", 1)
    first_previous = jnp.where(time_rank == 0, initial_state, arriving)
    previous = jnp.concatenate([first_previous[None], iterate[:-1]], axis=0)
    iterate_rim = extended(iterate, (("rows", 1),), 1)
    residual = (
        time_step * forcing + previous - iterate - time_step * apply_faces(iterate_rim, local_faces)
    )
    squares = lax.psum(jnp.sum(residual * residual, axis=(1, 2)), "rows")
    residual_rms = jnp.sqrt(squares / cell_count + rms_eps)

    wide = extended(residual, (("rows", 1),), halo)
    pieces = jnp.stack(
        [
            lax.slice_in_dim(wide, slab * k, slab * k + rows, axis=1).reshape(
                steps_dev * rows, columns_dev
            )
            for k in range(time_devices)
        ]
    )
    by_cells = lax.all_to_all(pieces, "tm", split_axis=0, concat_axis=0, tiled=True)
    diff_slab = lax.dynamic_slice_in_dim(rimmed, slab * time_rank, rows, axis=0)
    place = jnp.stack(
        [row_rank * rows_dev + time_rank * slab - halo, jnp.int32(rows_dev * row_devices)]
    ).astype(jnp.int32)

    vmem = pl.BlockSpec(memory_space=pltpu.VMEM)
    smem = pl.BlockSpec(memory_space=pltpu.SMEM)
    own = jax.ShapeDtypeStruct((slab * length, columns_dev), jnp.float32)
    *powers, moments = pl.pallas_call(
        functools.partial(krylov_body, length, slab, halo),
        out_shape=[own] * DEPTH + [jax.ShapeDtypeStruct((length, 128), jnp.float32)],
        in_specs=[smem, vmem, vmem, vmem],
        out_specs=[vmem] * (DEPTH + 1),
        scratch_shapes=[pltpu.VMEM((rows * length, columns_dev), jnp.float32)] * (DEPTH + 1)
        + [pltpu.VMEM((5, rows, columns_dev), jnp.float32)],
        name="krylov",
    )(place, by_cells, diff_slab, jnp.asarray(block_forward(length, 8)))

    for axis in ("rows", "tm"):
        count = lax.axis_size(axis)
        if count & (count - 1):
            moments = lax.psum(moments, axis)
        else:
            step = 1
            while step < count:
                pairs = [(i, i ^ step) for i in range(count)]
                moments = moments + lax.ppermute(moments, axis, pairs)
                step *= 2

    real, imag = channel_shifts(length)
    shift = np.broadcast_to(np.stack([real, imag])[:, :, None], (2, length, 128))
    table = np.zeros((DEPTH + 1, length, 128))
    table[:, :, :MOMENTS] = power_table(length)
    corrected = pl.pallas_call(
        functools.partial(combine_body, length, slab),
        out_shape=jax.ShapeDtypeStruct((time_devices, steps_dev * slab, columns_dev), jnp.float32),
        in_specs=[vmem] * (4 + DEPTH),
        out_specs=vmem,
        name="combine",
    )(
        moments,
        jnp.asarray(table, jnp.float32),
        jnp.asarray(shift, jnp.float32),
        jnp.asarray(block_inverse(length, 8)),
        *powers,
    )
    back = lax.all_to_all(corrected, "tm", split_axis=0, concat_axis=0, tiled=True)
    own_steps = back.reshape(time_devices, steps_dev, slab, columns_dev)
    own_steps = jnp.swapaxes(own_steps, 0, 1).reshape(steps_dev, rows_dev, columns_dev)
    updated = iterate + own_steps
    return (updated, residual_rms)


def solution(mesh):
    placed = (
        P(("groups", "tm"), "rows", None),
        P(("groups", "tm"), "rows", None),
        P(("groups", "rows"), None),
        P(("groups", "rows"), None),
    )
    return jax.shard_map(
        shards,
        mesh=mesh,
        in_specs=placed,
        out_specs=(P(("groups", "tm"), "rows", None), P(("groups", "tm"))),
        check_vma=False,
    )
```

time: 289 us -> 157 us (0.54)
  blocking collectives: 97.5 us -> 2.45 us
  other arithmetic: 38 us -> 5.72 us
  Pallas kernels: 0 us -> 30.9 us
  waiting for transfers between devices: 90.2 us -> 76.4 us
  starting transfers between devices: 41.9 us -> 29.3 us
  matrix products: 5.1 us -> 0 us
  local copies, waits for them, and re-layouts: 13.8 us -> 10.6 us
    all_to_all x2 -> x0, blocking collectives: 85.1 us -> none  [the longest x1 52.6 us: shards(): lax.all_to_all(solution, 'tm', split_axis=2, concat_axis=1, tiled=True)]
    pallas_call x0 -> x2, Pallas kernels: none -> 30.9 us  [the longest x1 25.3 us: shards(): pl.pallas_call(functools.partial(krylov_body, length, slab, halo), out_sh...]
    all_to_all x2, waiting for transfers between devices: 72.8 us -> 53.4 us  [the longest x1 33.4 us: shards(): lax.all_to_all(pieces, 'tm', split_axis=0, concat_axis=0, tiled=True)]
    reduce_sum x6 -> x0, other arithmetic: 19 us -> none  [freq_norm(): return jnp.sum(values * values, axis=(0, 2, 3))]
    ppermute x0 -> x4, waiting for transfers between devices: none -> 11 us  [shards(): moments = moments + lax.ppermute(moments, axis, pairs)]
    psum x5 -> x1, blocking collectives: 12.4 us -> 2.45 us  [shards(): squares = lax.psum(jnp.sum(residual * residual, axis=(1, 2)), 'rows')]
    ppermute x8 -> x3, starting transfers between devices: 18.4 us -> 8.43 us  [extended(): lax.ppermute(lax.slice_in_dim(block, block.shape[dim] - width, None, axis...]
    ppermute x8 -> x3, waiting for transfers between devices: 8.37 us -> 0.01 us  [extended(): lax.ppermute(lax.slice_in_dim(block, 0, width, axis=dim), axis, backward)]
  transfers between devices with their start and end apart: 19 -> 13, of which waited for: 10 -> 8; matrix products, arithmetic and copies ran while one was open for 2% -> 3% of each run, Pallas kernels for 0% -> 0%
where the time goes in v1:
time: 157 us; the launch traced here: 156 us
  waiting for transfers between devices  76.4 us (49%)
  Pallas kernels  30.9 us (20%)
  starting transfers between devices  29.3 us (19%)
  local copies, waits for them, and re-layouts  10.6 us (7%)
  other arithmetic  5.72 us (4%)
  blocking collectives  2.45 us (2%)
    all_to_all x1, waiting for transfers between devices, shards(): lax.all_to_all(pieces, 'tm', split_axis=0, concat_axis=0, tiled=True)  33.4 us
    pallas_call x1, Pallas kernels, shards(): pl.pallas_call(functools.partial(krylov_body, length, slab, halo), out_sh...  25.3 us
    all_to_all x1, waiting for transfers between devices, shards(): lax.all_to_all(corrected, 'tm', split_axis=0, concat_axis=0, tiled=True)  20 us
    ppermute x1, waiting for transfers between devices, from_behind(): lax.ppermute(value, axis, [(source, source + steps) for source in range(i...  11.2 us
    ppermute x4, waiting for transfers between devices, shards(): moments = moments + lax.ppermute(moments, axis, pairs)  11 us
    ppermute x3, starting transfers between devices, extended(): lax.ppermute(lax.slice_in_dim(block, block.shape[dim] - width, None, axis...  8.43 us
    all_to_all x1, starting transfers between devices, shards(): lax.all_to_all(pieces, 'tm', split_axis=0, concat_axis=0, tiled=True)  6.8 us
    unnamed x17, local copies, waits for them, and re-layouts  5.95 us
  transfers between devices with their start and end apart: 13, of which 8 were waited for; matrix products, arithmetic and copies ran while one was open for 3% of the time, Pallas kernels for 0%

profile of v1, /device:TPU:0, one launch (start us, length us, event | category | flops | bytes accessed | tf_op | source)
XLA Modules:
  0.0 156.3 jit_solution(14676219704962975988)
XLA Ops:
  0.6 0.0 copy-start.3
  0.6 0.8 fusion.26
  1.5 2.4 %collective-permute-start.3 = (f32[2,1,512]{2,1,0:T(1,128)S(1)}, f32[2,1,512]{2,1,0:T(1,128)S(1)}, u32[]{:S(2)}, u32[]{:S(2)}) collective-permute-start(f32[2,1,512]{2,1,0:T(1,128)S(1)} %get-tuple-element.35), channel_id=1, source_target_pairs={{0,1},{2,3},{4,5},{6,7},{8,9},{10,11},{12,13},{14,15},{16,17},{18,... | collective-permute-start | bytes 12296 | tf_op jit(solution)/shard_map/ppermute | solution.py:26
  3.9 1.3 collective-permute-start.4
  5.2 0.7 fusion.29
  5.9 3.0 %collective-permute-start.1 = (f32[6,512]{1,0:T(8,128)S(1)}, f32[6,512]{1,0:T(8,128)S(1)}, u32[]{:S(2)}, u32[]{:S(2)}) collective-permute-start(f32[6,512]{1,0:T(8,128)S(1)} %get-tuple-element.41), channel_id=1, source_target_pairs={{0,1},{2,3},{4,5},{6,7},{8,9},{10,11},{12,13},{14,15},{16,17},{18,... | collective-permute-start | bytes 36872 | tf_op jit(solution)/shard_map/ppermute | solution.py:26
  8.9 1.3 collective-permute-start.2
  10.2 1.3 slice_bitcast_fusion
  11.5 4.3 %collective-permute-start = (f32[256,512]{1,0:T(8,128)S(1)}, f32[256,512]{1,0:T(8,128)S(1)}, u32[]{:S(2)}, u32[]{:S(2)}) collective-permute-start(f32[256,512]{1,0:T(8,128)S(1)} %get-tuple-element.33), channel_id=1, source_target_pairs={{0,2},{2,4},{4,6},{6,8},{8,10},{10,12},{12,14},{1,3},{3,5},{5,7},{... | collective-permute-start | bytes 1572872 | tf_op jit(solution)/shard_map/ppermute | solution.py:37
  15.9 0.2 fusion.11
  16.1 0.1 fusion.27
  16.2 0.4 add_add_fusion
  16.7 11.2 %collective-permute-done = f32[256,512]{1,0:T(8,128)S(1)} collective-permute-done((f32[256,512]{1,0:T(8,128)S(1)}, f32[256,512]{1,0:T(8,128)S(1)}, u32[]{:S(2)}, u32[]{:S(2)}) %collective-permute-start) | collective-permute-done | bytes 524320 | tf_op jit(solution)/shard_map/ppermute | solution.py:37
  27.9 0.1 select_bitcast_fusion
  28.0 1.2 multiply_reduce_fusion
  29.2 1.3 collective-permute-start.6
  30.5 3.0 %collective-permute-start.5 = (f32[2,6,512]{2,1,0:T(8,128)S(1)}, f32[2,6,512]{2,1,0:T(8,128)S(1)}, u32[]{:S(2)}, u32[]{:S(2)}) collective-permute-start(f32[2,6,512]{2,1,0:T(8,128)S(1)} %get-tuple-element.32), channel_id=1, source_target_pairs={{0,1},{2,3},{4,5},{6,7},{8,9},{10,11},{12,13},{14,15},{16,17},{18,... | collective-permute-start | bytes 73736 | tf_op jit(solution)/shard_map/ppermute | solution.py:26
  33.6 0.8 collective-permute-done.5
  34.4 0.2 pad_maximum_fusion.4
  34.8 0.7 constant_dynamic-update-slice_fusion.7
  35.5 0.7 constant_dynamic-update-slice_fusion.6
  36.2 0.7 constant_dynamic-update-slice_fusion.5
  36.9 0.7 constant_dynamic-update-slice_fusion.4
  37.6 0.7 constant_dynamic-update-slice_fusion.3
  38.3 0.7 constant_dynamic-update-slice_fusion.2
  39.0 0.7 constant_dynamic-update-slice_fusion.1
  39.6 0.7 constant_dynamic-update-slice_fusion
  40.3 6.8 %all-to-all-start = ((f32[8,88,512]{2,1,0:T(8,128)}), f32[8,88,512]{2,1,0:T(8,128)S(1)}, u32[]{:S(2)}, u32[]{:S(2)}) async-start(f32[8,88,512]{2,1,0:T(8,128)} %constant_dynamic-update-slice_fusion), calls=%async_computation | async-start | bytes 2883584 | tf_op jit(solution)/shard_map/all_to_all | solution.py:327
  47.1 0.6 pad_add_fusion.place_ref
  47.8 0.6 constant_dynamic-slice_fusion.diff_ref
  48.4 33.4 %all-to-all-done.pieces_ref = f32[8,88,512]{2,1,0:T(8,128)S(1)} async-done(((f32[8,88,512]{2,1,0:T(8,128)}), f32[8,88,512]{2,1,0:T(8,128)S(1)}, u32[]{:S(2)}, u32[]{:S(2)}) %all-to-all-start) | async-done | bytes 1441824 | tf_op jit(solution)/shard_map/all_to_all | solution.py:327
  81.8 1.1 copy-done.1
  83.0 25.3 %krylov.1 = (f32[512,512]{1,0:T(8,128)}, f32[512,512]{1,0:T(8,128)}, f32[512,512]{1,0:T(8,128)}, f32[512,512]{1,0:T(8,128)}, f32[512,512]{1,0:T(8,128)}, /*index=5*/f32[512,512]{1,0:T(8,128)}, f32[16,128]{1,0:T(8,128)}) custom-call(s32[2]{0:T(128)} %pad_add_fusion.place_ref, f32[8,88,512]{2,1,0:T(8,128)} %copy-done.1, ...), custom_call_target="tpu_custom_call" | custom-call | tf_op jit(solution)/shard_map/krylov/pallas_call | solution.py:336
  108.3 1.4 collective-permute-done.7
  109.7 0.7 add.63
  110.4 1.5 collective-permute-start.8
  111.9 2.2 %collective-permute-done.8 = f32[16,128]{1,0:T(8,128)S(1)} collective-permute-done((f32[16,128]{1,0:T(8,128)S(1)}, f32[16,128]{1,0:T(8,128)S(1)}, u32[]{:S(2)}, u32[]{:S(2)}) %collective-permute-start.8) | collective-permute-done | bytes 8224 | tf_op jit(solution)/shard_map/ppermute | solution.py:354
  114.0 3.6 %collective-permute-done.9 = f32[16,128]{1,0:T(8,128)S(1)} collective-permute-done((f32[16,128]{1,0:T(8,128)S(1)}, f32[16,128]{1,0:T(8,128)S(1)}, u32[]{:S(2)}, u32[]{:S(2)}) %collective-permute-start.9) | collective-permute-done | bytes 8224 | tf_op jit(solution)/shard_map/ppermute | solution.py:354
  117.7 0.8 collective-permute-start.10
  118.5 3.7 %collective-permute-done.10 = f32[16,128]{1,0:T(8,128)S(1)} collective-permute-done((f32[16,128]{1,0:T(8,128)S(1)}, f32[16,128]{1,0:T(8,128)S(1)}, u32[]{:S(2)}, u32[]{:S(2)}) %collective-permute-start.10) | collective-permute-done | bytes 8224 | tf_op jit(solution)/shard_map/ppermute | solution.py:354
  122.3 0.6 add.66.moments_ref
  122.8 5.6 %combine.1 = f32[8,64,512]{2,1,0:T(8,128)} custom-call(f32[16,128]{1,0:T(8,128)} %add.66.moments_ref, f32[7,16,128]{2,1,0:T(8,128)} %constant.47.clone.table_ref, f32[2,16,128]{2,1,0:T(8,128)} %constant.48.clone.shift_ref, f32[128,128]{1,0:T(8,128)} %constant.49.clone.mix_ref, f32[512,512]{1,0:T(8,128)} %get-tuple-element.10.rest_0_, ...), custom_call_target="tpu_custom_call" | custom-call | tf_op jit(solution)/shard_map/combine/pallas_call | solution.py:361
  128.4 3.6 %all-to-all-start.1 = ((f32[8,64,512]{2,1,0:T(8,128)}), f32[8,64,512]{2,1,0:T(8,128)S(1)}, u32[]{:S(2)}, u32[]{:S(2)}) async-start(f32[8,64,512]{2,1,0:T(8,128)} %combine.1), calls=%async_computation.1 | async-start | bytes 2097152 | tf_op jit(solution)/shard_map/all_to_all | solution.py:374
  132.0 2.5 %psum.7 = f32[2]{0:T(128)S(1)} all-reduce(f32[2]{0:T(128)S(1)} %get-tuple-element.16), channel_id=1, replica_groups=mesh['groups'=2,'tm'=8,'rows'=2] {'rows'}, use_global_device_ids=true, to_apply=%region_1.2 | all-reduce | flops 2 | bytes 16 | tf_op jit(solution)/shard_map/psum | solution.py:315
  134.5 0.5 add_sqrt_fusion
  135.0 20.0 %all-to-all-done.1 = f32[8,64,512]{2,1,0:T(8,128)S(1)} async-done(((f32[8,64,512]{2,1,0:T(8,128)}), f32[8,64,512]{2,1,0:T(8,128)S(1)}, u32[]{:S(2)}, u32[]{:S(2)}) %all-to-all-start.1) | async-done | bytes 1048608 | tf_op jit(solution)/shard_map/all_to_all | solution.py:374
  155.0 0.1 copy.11
  155.1 1.2 bitcast_add_fusion
  (29 shorter events, 0.3 us)
Async XLA Ops:
  0.6 15.2 %copy-start.3 = (f32[256,512]{1,0:T(8,128)S(1)}, f32[256,512]{1,0:T(8,128)}, u32[]{:S(2)}) copy-start(f32[256,512]{1,0:T(8,128)} %param.11) | copy-start | bytes 1572868
  1.5 26.5 %collective-permute-start.3 = (f32[2,1,512]{2,1,0:T(1,128)S(1)}, f32[2,1,512]{2,1,0:T(1,128)S(1)}, u32[]{:S(2)}, u32[]{:S(2)}) collective-permute-start(f32[2,1,512]{2,1,0:T(1,128)S(1)} %get-tuple-element.35), channel_id=1, source_target_pairs={{0,1},{2,3},{4,5},{6,7},{8,9},{10,11},{12,13},{14,15},{16,17},{18,... | collective-permute-start | bytes 12296 | tf_op jit(solution)/shard_map/ppermute | solution.py:26
  3.9 24.1 %collective-permute-start.4 = (f32[2,1,512]{2,1,0:T(1,128)S(1)}, f32[2,1,512]{2,1,0:T(1,128)S(1)}, u32[]{:S(2)}, u32[]{:S(2)}) collective-permute-start(f32[2,1,512]{2,1,0:T(1,128)S(1)} %get-tuple-element.36), channel_id=1, source_target_pairs={{1,0},{3,2},{5,4},{7,6},{9,8},{11,10},{13,12},{15,14},{17,16},{19,... | collective-permute-start | bytes 12296 | tf_op jit(solution)/shard_map/ppermute | solution.py:29
  5.9 9.9 %collective-permute-start.1 = (f32[6,512]{1,0:T(8,128)S(1)}, f32[6,512]{1,0:T(8,128)S(1)}, u32[]{:S(2)}, u32[]{:S(2)}) collective-permute-start(f32[6,512]{1,0:T(8,128)S(1)} %get-tuple-element.41), channel_id=1, source_target_pairs={{0,1},{2,3},{4,5},{6,7},{8,9},{10,11},{12,13},{14,15},{16,17},{18,... | collective-permute-start | bytes 36872 | tf_op jit(solution)/shard_map/ppermute | solution.py:26
  8.9 6.9 %collective-permute-start.2 = (f32[6,512]{1,0:T(8,128)S(1)}, f32[6,512]{1,0:T(8,128)S(1)}, u32[]{:S(2)}, u32[]{:S(2)}) collective-permute-start(f32[6,512]{1,0:T(8,128)S(1)} %get-tuple-element.42), channel_id=1, source_target_pairs={{1,0},{3,2},{5,4},{7,6},{9,8},{11,10},{13,12},{15,14},{17,16},{19,... | collective-permute-start | bytes 36872 | tf_op jit(solution)/shard_map/ppermute | solution.py:29
  11.5 16.4 %collective-permute-start = (f32[256,512]{1,0:T(8,128)S(1)}, f32[256,512]{1,0:T(8,128)S(1)}, u32[]{:S(2)}, u32[]{:S(2)}) collective-permute-start(f32[256,512]{1,0:T(8,128)S(1)} %get-tuple-element.33), channel_id=1, source_target_pairs={{0,2},{2,4},{4,6},{6,8},{8,10},{10,12},{12,14},{1,3},{3,5},{5,7},{... | collective-permute-start | bytes 1572872 | tf_op jit(solution)/shard_map/ppermute | solution.py:37
  16.2 11.7 %copy-start.4 = (f32[256,512]{1,0:T(8,128)S(1)}, f32[256,512]{1,0:T(8,128)}, u32[]{:S(2)}) copy-start(f32[256,512]{1,0:T(8,128)} %param.10) | copy-start | bytes 1572868
  16.2 11.8 %copy-start.2 = (f32[2,256,512]{2,1,0:T(8,128)S(1)}, f32[2,256,512]{2,1,0:T(8,128)}, u32[]{:S(2)}) copy-start(f32[2,256,512]{2,1,0:T(8,128)} %param.9) | copy-start | bytes 3145732
  16.7 11.4 %copy-start = (f32[2,256,512]{2,1,0:T(8,128)S(1)}, f32[2,256,512]{2,1,0:T(8,128)}, u32[]{:S(2)}) copy-start(f32[2,256,512]{2,1,0:T(8,128)} %param.8) | copy-start | bytes 3145732
  29.2 4.3 %collective-permute-start.6 = (f32[2,6,512]{2,1,0:T(8,128)S(1)}, f32[2,6,512]{2,1,0:T(8,128)S(1)}, u32[]{:S(2)}, u32[]{:S(2)}) collective-permute-start(f32[2,6,512]{2,1,0:T(8,128)S(1)} %get-tuple-element.31), channel_id=1, source_target_pairs={{1,0},{3,2},{5,4},{7,6},{9,8},{11,10},{13,12},{15,14},{17,16},{19,... | collective-permute-start | bytes 73736 | tf_op jit(solution)/shard_map/ppermute | solution.py:29
  30.5 3.9 %collective-permute-start.5 = (f32[2,6,512]{2,1,0:T(8,128)S(1)}, f32[2,6,512]{2,1,0:T(8,128)S(1)}, u32[]{:S(2)}, u32[]{:S(2)}) collective-permute-start(f32[2,6,512]{2,1,0:T(8,128)S(1)} %get-tuple-element.32), channel_id=1, source_target_pairs={{0,1},{2,3},{4,5},{6,7},{8,9},{10,11},{12,13},{14,15},{16,17},{18,... | collective-permute-start | bytes 73736 | tf_op jit(solution)/shard_map/ppermute | solution.py:26
  40.3 41.5 %all-to-all-start = ((f32[8,88,512]{2,1,0:T(8,128)}), f32[8,88,512]{2,1,0:T(8,128)S(1)}, u32[]{:S(2)}, u32[]{:S(2)}) async-start(f32[8,88,512]{2,1,0:T(8,128)} %constant_dynamic-update-slice_fusion), calls=%async_computation | async-start | bytes 2883584 | tf_op jit(solution)/shard_map/all_to_all | solution.py:327
  81.8 1.1 copy-start.1
  108.3 1.4 collective-permute-start.7
  110.4 3.7 %collective-permute-start.8 = (f32[16,128]{1,0:T(8,128)S(1)}, f32[16,128]{1,0:T(8,128)S(1)}, u32[]{:S(2)}, u32[]{:S(2)}) collective-permute-start(f32[16,128]{1,0:T(8,128)S(1)} %add.63), channel_id=1, source_target_pairs={{0,2},{2,0},{4,6},{6,4},{8,10},{10,8},{12,14},{14,12},{1,3},{3,1},... | collective-permute-start | bytes 24584 | tf_op jit(solution)/shard_map/ppermute | solution.py:354
  114.0 3.7 %collective-permute-start.9 = (f32[16,128]{1,0:T(8,128)S(1)}, f32[16,128]{1,0:T(8,128)S(1)}, u32[]{:S(2)}, u32[]{:S(2)}) collective-permute-start(f32[16,128]{1,0:T(8,128)S(1)} %add.64), channel_id=1, source_target_pairs={{0,4},{2,6},{4,0},{6,2},{8,12},{10,14},{12,8},{14,10},{1,5},{3,7},... | collective-permute-start | bytes 24584 | tf_op jit(solution)/shard_map/ppermute | solution.py:354
  117.7 4.5 %collective-permute-start.10 = (f32[16,128]{1,0:T(8,128)S(1)}, f32[16,128]{1,0:T(8,128)S(1)}, u32[]{:S(2)}, u32[]{:S(2)}) collective-permute-start(f32[16,128]{1,0:T(8,128)S(1)} %add.65), channel_id=1, source_target_pairs={{0,8},{2,10},{4,12},{6,14},{8,0},{10,2},{12,4},{14,6},{1,9},{3,11}... | collective-permute-start | bytes 24584 | tf_op jit(solution)/shard_map/ppermute | solution.py:354
  128.4 26.6 %all-to-all-start.1 = ((f32[8,64,512]{2,1,0:T(8,128)}), f32[8,64,512]{2,1,0:T(8,128)S(1)}, u32[]{:S(2)}, u32[]{:S(2)}) async-start(f32[8,64,512]{2,1,0:T(8,128)} %combine.1), calls=%async_computation.1 | async-start | bytes 2097152 | tf_op jit(solution)/shard_map/all_to_all | solution.py:374

commit v2 on v1

--- a/solution.py
+++ b/solution.py
@@ -12,6 +12,7 @@
 CG_ITERS = 3
 DEPTH = 2 * CG_ITERS
 MOMENTS = 2 * DEPTH + 1
+UNROLL = 16
 
 circulant_alpha = 0.05
 time_step = 0.5
@@ -127,33 +128,30 @@
 
 
 def krylov_body(length, slab, halo, place_ref, pieces_ref, diff_ref, mix_ref, *rest):
-    power_refs = rest[:DEPTH]
-    moments_ref = rest[DEPTH]
-    vectors = rest[DEPTH + 1 : 2 * DEPTH + 2]
-    weights_ref = rest[2 * DEPTH + 2]
+    vectors = rest[:DEPTH]
+    moments_ref, south_ref, east_ref, west_ref = rest[DEPTH:]
     rows = slab + 2 * halo
     columns = diff_ref.shape[-1]
+    groups = length // 8
+    tiles = columns // 128
     steps_dev = pieces_ref.shape[1] // rows
 
     centre = diff_ref[...]
-    above = jnp.concatenate([centre[:1], centre[:-1]], axis=0)
     below = jnp.concatenate([centre[1:], centre[-1:]], axis=0)
     lane = lax.broadcasted_iota(jnp.int32, (rows, columns), 1)
-    row = lax.broadcasted_iota(jnp.int32, (rows, columns), 0) + place_ref[0]
-    left_edge = lane == 0
-    right_edge = lane == columns - 1
-    before = jnp.where(left_edge, centre, pltpu.roll(centre, 1, 1))
-    after = jnp.where(right_edge, centre, pltpu.roll(centre, columns - 1, 1))
+    after = jnp.where(lane == columns - 1, centre, pltpu.roll(centre, columns - 1, 1))
     quarter = 0.5 * time_step
-    north = quarter * (centre + above)
     south = quarter * (centre + below)
-    west = quarter * (centre + before)
     east = quarter * (centre + after)
-    weights_ref[0] = north + south + west + east
-    weights_ref[1] = jnp.where(row == 0, 0.0, north)
-    weights_ref[2] = jnp.where(row == place_ref[1] - 1, 0.0, south)
-    weights_ref[3] = jnp.where(left_edge, 0.0, west)
-    weights_ref[4] = jnp.where(right_edge, 0.0, east)
+    west = (2.0 * quarter) * centre[:, :128]
+    for r in range(rows):
+        south_ref[8 * r : 8 * r + 8, :] = jnp.broadcast_to(south[r : r + 1], (8, columns))
+        east_ref[8 * r : 8 * r + 8, :] = jnp.broadcast_to(east[r : r + 1], (8, columns))
+        west_ref[8 * r : 8 * r + 8, :] = jnp.broadcast_to(west[r : r + 1], (8, 128))
+    first_row = place_ref[0] + halo == 0
+    last_row = place_ref[0] + halo + slab == place_ref[1]
+    keep_above = jnp.where(first_row, 0.0, 1.0)
+    keep_below = jnp.where(last_row, 0.0, 1.0)
 
     mix = mix_ref[...]
     starts = list(range(0, rows - 7, 8))
@@ -170,65 +168,97 @@
             mix, block, precision=lax.Precision.HIGHEST, preferred_element_type=jnp.float32
         )
 
-    def stencil(source, r):
-        at = pl.multiple_of(r * length, 8)
-        here = source[pl.ds(at, length), :]
-        up = source[pl.ds(pl.multiple_of(at - length, 8), length), :]
-        down = source[pl.ds(pl.multiple_of(at + length, 8), length), :]
-
-        def weight(index):
-            return weights_ref[index, pl.ds(r, 1), :]
-
-        return here, (
-            weight(0) * here
-            - weight(1) * up
-            - weight(2) * down
-            - weight(3) * pltpu.roll(here, 1, 1)
-            - weight(4) * pltpu.roll(here, columns - 1, 1)
-        )
-
-    lanes = lax.broadcasted_iota(jnp.int32, (length, 128), 1)
-    table = jnp.zeros((length, 128), jnp.float32)
-
-    def put(table, index, sums):
-        return jnp.where(lanes == index, jnp.sum(sums, axis=1, keepdims=True), table)
+    lane8 = lax.broadcasted_iota(jnp.int32, (8, 128), 1)
+    is_first = lane8 == 0
+    is_last = lane8 == 127
+
+    def load(source, r, group):
+        at = pl.multiple_of(r * length + 8 * group, 8)
+        return [source[pl.ds(at, 8), 128 * t : 128 * t + 128] for t in range(tiles)]
+
+    def row_of(ref, r, t):
+        return ref[pl.ds(pl.multiple_of(8 * r, 8), 8), 128 * t : 128 * t + 128]
+
+    def south_flux(r, here, under):
+        return [row_of(south_ref, r, t) * (under[t] - here[t]) for t in range(tiles)]
+
+    def stencil(r, here, under, north):
+        south = south_flux(r, here, under)
+        turned = [pltpu.roll(v, 127, 1) for v in here] + [0.0]
+        east = [
+            row_of(east_ref, r, t) * (jnp.where(is_last, turned[t + 1], turned[t]) - here[t])
+            for t in range(tiles)
+        ]
+        moved = [row_of(west_ref, r, 0) * here[0]] + [pltpu.roll(f, 1, 1) for f in east]
+        value = [
+            (jnp.where(is_first, moved[t], moved[t + 1]) - east[t]) + (north[t] - south[t])
+            for t in range(tiles)
+        ]
+        return value, south
+
+    def total(parts):
+        while len(parts) > 1:
+            parts = [parts[i] + parts[i + 1] for i in range(0, len(parts) - 1, 2)] + (
+                [parts[-1]] if len(parts) % 2 else []
+            )
+        return parts[0]
+
+    table = [jnp.zeros((8, 128), jnp.float32) for _ in range(groups)]
+
+    def put(entry, index, sums):
+        return jnp.where(lane8 == index, jnp.sum(sums, axis=1, keepdims=True), entry)
 
     for power in range(DEPTH):
-        source, target = vectors[power], vectors[power + 1]
-
-        def plain(r, carry):
-            _, value = stencil(source, r)
-            target[pl.ds(pl.multiple_of(r * length, 8), length), :] = value
-            return carry
-
-        def summed(r, carry):
-            here, value = stencil(source, r)
-            if power + 1 < DEPTH:
-                target[pl.ds(pl.multiple_of(r * length, 8), length), :] = value
-            squares, products, last = carry
-            squares = squares + here * here
-            products = products + here * value
-            if power + 1 == DEPTH:
-                last = last + value * value
-            return squares, products, last
-
+        source = vectors[power]
+        target = vectors[power + 1] if power + 1 < DEPTH else None
         first, final = power + 1, rows - 1 - power
-        if first < halo:
-            lax.fori_loop(first, halo, plain, 0)
-            lax.fori_loop(halo + slab, final, plain, 0)
-        zero = jnp.zeros((length, columns), jnp.float32)
-        squares, products, last = lax.fori_loop(
-            halo, halo + slab, summed, (zero, zero, zero if power + 1 == DEPTH else 0.0)
-        )
-        table = put(table, 2 * power, squares)
-        table = put(table, 2 * power + 1, products)
-        if power + 1 == DEPTH:
-            table = put(table, 2 * DEPTH, last)
-        power_refs[power][...] = source[halo * length : (halo + slab) * length, :]
-    moments_ref[...] = table
-
-
-def combine_body(length, slab, moments_ref, table_ref, shift_ref, mix_ref, *rest):
+        for group in range(groups):
+
+            def step(r, carry, summing):
+                here, north, sums = carry
+                under = load(source, r + 1, group)
+                value, south = stencil(r, here, under, north)
+                if target is not None:
+                    at = pl.multiple_of(r * length + 8 * group, 8)
+                    for t in range(tiles):
+                        target[pl.ds(at, 8), 128 * t : 128 * t + 128] = value[t]
+                if summing:
+                    products = [
+                        sums[0] + total([v * v for v in here]),
+                        sums[1] + total([v * w for v, w in zip(here, value)]),
+                    ]
+                    if target is None:
+                        products.append(sums[2] + total([w * w for w in value]))
+                    sums = tuple(products)
+                return tuple(under), tuple(south), sums
+
+            top = load(source, first - 1, group)
+            here = load(source, first, group)
+            carry = (tuple(here), tuple(south_flux(first - 1, top, here)), ())
+            if first < halo:
+                carry = lax.fori_loop(
+                    first, halo, functools.partial(step, summing=False), carry, unroll=True
+                )
+            zero = jnp.zeros((8, 128), jnp.float32)
+            carry = (carry[0], carry[1], (zero,) * (2 if target is not None else 3))
+            carry = lax.fori_loop(
+                halo, halo + slab, functools.partial(step, summing=True), carry, unroll=min(UNROLL, max(1, slab // 2))
+            )
+            for index, sums in enumerate(carry[2]):
+                table[group] = put(table[group], 2 * power + index, sums)
+            if first < halo:
+                carry = (carry[0], carry[1], ())
+                lax.fori_loop(
+                    halo + slab, final, functools.partial(step, summing=False), carry, unroll=True
+                )
+            if target is not None and first < halo:
+                for r, keep in ((halo - 1, keep_above), (halo + slab, keep_below)):
+                    at = r * length + 8 * group
+                    target[at : at + 8, :] = target[at : at + 8, :] * keep
+    moments_ref[...] = jnp.concatenate(table, axis=0)
+
+
+def combine_body(length, slab, halo, moments_ref, table_ref, shift_ref, mix_ref, *rest):
     power_refs = rest[:DEPTH]
     out_ref = rest[DEPTH]
     steps_dev = out_ref.shape[1] // slab
@@ -270,9 +300,8 @@
         total = jnp.zeros((8, length, columns), jnp.float32)
         other = jnp.zeros((8, length, columns), jnp.float32)
         for power in range(DEPTH):
-            here = power_refs[power][start * length : (start + 8) * length, :].reshape(
-                8, length, columns
-            )
+            at = (halo + start) * length
+            here = power_refs[power][at : at + 8 * length, :].reshape(8, length, columns)
             total = total + spread(outer, power) * here
             if power + 1 < DEPTH:
                 flipped = jnp.concatenate([here[:, half:], here[:, :half]], axis=1)
@@ -332,14 +361,18 @@
 
     vmem = pl.BlockSpec(memory_space=pltpu.VMEM)
     smem = pl.BlockSpec(memory_space=pltpu.SMEM)
-    own = jax.ShapeDtypeStruct((slab * length, columns_dev), jnp.float32)
+    vector = pltpu.VMEM((rows * length, columns_dev), jnp.float32)
     *powers, moments = pl.pallas_call(
         functools.partial(krylov_body, length, slab, halo),
-        out_shape=[own] * DEPTH + [jax.ShapeDtypeStruct((length, 128), jnp.float32)],
+        out_shape=[vector] * DEPTH + [jax.ShapeDtypeStruct((length, 128), jnp.float32)],
         in_specs=[smem, vmem, vmem, vmem],
         out_specs=[vmem] * (DEPTH + 1),
-        scratch_shapes=[pltpu.VMEM((rows * length, columns_dev), jnp.float32)] * (DEPTH + 1)
-        + [pltpu.VMEM((5, rows, columns_dev), jnp.float32)],
+        scratch_shapes=[
+            pltpu.VMEM((rows * 8, columns_dev), jnp.float32),
+            pltpu.VMEM((rows * 8, columns_dev), jnp.float32),
+            pltpu.VMEM((rows * 8, 128), jnp.float32),
+        ],
+        compiler_params=pltpu.CompilerParams(vmem_limit_bytes=24 * 2**20),
         name="krylov",
     )(place, by_cells, diff_slab, jnp.asarray(block_forward(length, 8)))
 
@@ -359,10 +392,11 @@
     table = np.zeros((DEPTH + 1, length, 128))
     table[:, :, :MOMENTS] = power_table(length)
     corrected = pl.pallas_call(
-        functools.partial(combine_body, length, slab),
+        functools.partial(combine_body, length, slab, halo),
         out_shape=jax.ShapeDtypeStruct((time_devices, steps_dev * slab, columns_dev), jnp.float32),
         in_specs=[vmem] * (4 + DEPTH),
         out_specs=vmem,
+        compiler_params=pltpu.CompilerParams(vmem_limit_bytes=24 * 2**20),
         name="combine",
     )(
         moments,

time: 157 us -> 139 us (0.89)
  Pallas kernels: 30.9 us -> 13 us
  starting transfers between devices: 29.3 us -> 31.2 us
  other arithmetic: 5.72 us -> 3.87 us
    pallas_call x1, Pallas kernels: 25.3 us -> 10.2 us  [shards(): pl.pallas_call(functools.partial(krylov_body, length, slab, halo), out_sh...]
    pallas_call x1, Pallas kernels: 5.56 us -> 2.77 us  [shards(): pl.pallas_call(functools.partial(combine_body, length, slab, halo), out_s...]
    unnamed x17 -> x23, local copies, waits for them, and re-layouts: 5.95 us -> 4.84 us
where the time goes in v2:
time: 139 us; the launch traced here: 138 us
  waiting for transfers between devices  76.9 us (55%)
  starting transfers between devices  31.2 us (22%)
  Pallas kernels  13 us (9%)
  local copies, waits for them, and re-layouts  9.61 us (7%)
  other arithmetic  3.87 us (3%)
  blocking collectives  2.45 us (2%)
    all_to_all x1, waiting for transfers between devices, shards(): lax.all_to_all(pieces, 'tm', split_axis=0, concat_axis=0, tiled=True)  34.6 us
    all_to_all x1, waiting for transfers between devices, shards(): lax.all_to_all(corrected, 'tm', split_axis=0, concat_axis=0, tiled=True)  20 us
    ppermute x1, waiting for transfers between devices, from_behind(): lax.ppermute(value, axis, [(source, source + steps) for source in range(i...  10.8 us
    ppermute x4, waiting for transfers between devices, shards(): moments = moments + lax.ppermute(moments, axis, pairs)  10.7 us
    pallas_call x1, Pallas kernels, shards(): pl.pallas_call(functools.partial(krylov_body, length, slab, halo), out_sh...  10.2 us
    ppermute x3, starting transfers between devices, extended(): lax.ppermute(lax.slice_in_dim(block, block.shape[dim] - width, None, axis...  8.43 us
    all_to_all x1, starting transfers between devices, shards(): lax.all_to_all(pieces, 'tm', split_axis=0, concat_axis=0, tiled=True)  7.97 us
    ppermute x1, starting transfers between devices, from_behind(): lax.ppermute(value, axis, [(source, source + steps) for source in range(i...  5.05 us
  transfers between devices with their start and end apart: 13, of which 8 were waited for; matrix products, arithmetic and copies ran while one was open for 3% of the time, Pallas kernels for 0%

profile of v2, /device:TPU:0, one launch (start us, length us, event | category | flops | bytes accessed | tf_op | source)
XLA Modules:
  0.0 138.0 jit_solution(9050339055080886451)
XLA Ops:
  0.6 0.0 copy-start.6
  0.6 0.8 fusion.26
  1.5 2.4 %collective-permute-start.3 = (f32[2,1,512]{2,1,0:T(1,128)S(1)}, f32[2,1,512]{2,1,0:T(1,128)S(1)}, u32[]{:S(2)}, u32[]{:S(2)}) collective-permute-start(f32[2,1,512]{2,1,0:T(1,128)S(1)} %get-tuple-element.35), channel_id=1, source_target_pairs={{0,1},{2,3},{4,5},{6,7},{8,9},{10,11},{12,13},{14,15},{16,17},{18,... | collective-permute-start | bytes 12296 | tf_op jit(solution)/shard_map/ppermute | solution.py:27
  3.9 1.3 collective-permute-start.4
  5.2 0.7 fusion.29
  5.9 3.0 %collective-permute-start.1 = (f32[6,512]{1,0:T(8,128)S(1)}, f32[6,512]{1,0:T(8,128)S(1)}, u32[]{:S(2)}, u32[]{:S(2)}) collective-permute-start(f32[6,512]{1,0:T(8,128)S(1)} %get-tuple-element.41), channel_id=1, source_target_pairs={{0,1},{2,3},{4,5},{6,7},{8,9},{10,11},{12,13},{14,15},{16,17},{18,... | collective-permute-start | bytes 36872 | tf_op jit(solution)/shard_map/ppermute | solution.py:27
  8.9 1.3 collective-permute-start.2
  10.2 2.1 %slice_bitcast_fusion = (f32[256,512]{1,0:T(8,128)}, f32[1,256,512]{2,1,0:T(8,128)S(1)}) fusion(f32[2,256,512]{2,1,0:T(8,128)} %param.8), kind=kLoop, calls=%fused_computation.32 | loop fusion | bytes 2097152 | tf_op jit(solution)/shard_map/squeeze | solution.py:337
  12.3 5.0 %collective-permute-start = (f32[256,512]{1,0:T(8,128)}, f32[256,512]{1,0:T(8,128)}, u32[]{:S(2)}, u32[]{:S(2)}) collective-permute-start(f32[256,512]{1,0:T(8,128)} %get-tuple-element.33), channel_id=1, source_target_pairs={{0,2},{2,4},{4,6},{6,8},{8,10},{10,12},{12,14},{1,3},{3,5},{5,7},{... | collective-permute-start | bytes 1572872 | tf_op jit(solution)/shard_map/ppermute | solution.py:38
  17.4 0.2 fusion.11
  17.6 0.1 fusion.27
  17.7 0.0 copy-start.7
  17.8 0.5 add_add_fusion
  18.2 10.8 %collective-permute-done = f32[256,512]{1,0:T(8,128)} collective-permute-done((f32[256,512]{1,0:T(8,128)}, f32[256,512]{1,0:T(8,128)}, u32[]{:S(2)}, u32[]{:S(2)}) %collective-permute-start) | collective-permute-done | bytes 524320 | tf_op jit(solution)/shard_map/ppermute | solution.py:38
  29.0 0.1 select_bitcast_fusion
  29.1 1.2 multiply_reduce_fusion
  30.3 1.3 collective-permute-start.6
  31.6 3.0 %collective-permute-start.5 = (f32[2,6,512]{2,1,0:T(8,128)S(1)}, f32[2,6,512]{2,1,0:T(8,128)S(1)}, u32[]{:S(2)}, u32[]{:S(2)}) collective-permute-start(f32[2,6,512]{2,1,0:T(8,128)S(1)} %get-tuple-element.32), channel_id=1, source_target_pairs={{0,1},{2,3},{4,5},{6,7},{8,9},{10,11},{12,13},{14,15},{16,17},{18,... | collective-permute-start | bytes 73736 | tf_op jit(solution)/shard_map/ppermute | solution.py:27
  34.7 0.8 collective-permute-done.5
  35.5 0.2 pad_maximum_fusion.4
  35.9 0.7 constant_dynamic-update-slice_fusion.7
  36.6 0.7 constant_dynamic-update-slice_fusion.6
  37.3 0.7 constant_dynamic-update-slice_fusion.5
  38.0 0.7 constant_dynamic-update-slice_fusion.4
  38.7 0.7 constant_dynamic-update-slice_fusion.3
  39.3 0.7 constant_dynamic-update-slice_fusion.2
  40.0 0.7 constant_dynamic-update-slice_fusion.1
  40.7 0.7 constant_dynamic-update-slice_fusion
  41.4 8.0 %all-to-all-start = ((f32[8,88,512]{2,1,0:T(8,128)}), f32[8,88,512]{2,1,0:T(8,128)S(1)}, u32[]{:S(2)}, u32[]{:S(2)}) async-start(f32[8,88,512]{2,1,0:T(8,128)} %constant_dynamic-update-slice_fusion), calls=%async_computation | async-start | bytes 2883584 | tf_op jit(solution)/shard_map/all_to_all | solution.py:356
  49.4 0.0 copy-start.2
  49.4 0.0 copy-start.3
  49.4 0.1 pad_add_fusion.place_ref
  49.5 34.6 %all-to-all-done.pieces_ref = f32[8,88,512]{2,1,0:T(8,128)S(1)} async-done(((f32[8,88,512]{2,1,0:T(8,128)}), f32[8,88,512]{2,1,0:T(8,128)S(1)}, u32[]{:S(2)}, u32[]{:S(2)}) %all-to-all-start) | async-done | bytes 1441824 | tf_op jit(solution)/shard_map/all_to_all | solution.py:356
  84.1 10.2 %krylov.1 = (f32[704,512]{1,0:T(8,128)S(1)}, f32[704,512]{1,0:T(8,128)S(1)}, f32[704,512]{1,0:T(8,128)S(1)}, f32[704,512]{1,0:T(8,128)S(1)}, f32[704,512]{1,0:T(...) custom-call(s32[2]{0:T(128)S(1)} %pad_add_fusion.place_ref, f32[8,88,512]{2,1,0:T(8,128)S(1)} %all-to-all-done.pieces_ref, ...), custom_call_target="tpu_custom_call" | custom-call | tf_op jit(solution)/shard_map/krylov/pallas_call | solution.py:365
  94.3 0.0 collective-permute-start.7
  94.3 1.2 collective-permute-done.7
  95.5 1.5 %collective-permute-start.8 = (f32[16,128]{1,0:T(8,128)S(1)}, f32[16,128]{1,0:T(8,128)S(1)}, u32[]{:S(2)}, u32[]{:S(2)}) collective-permute-start(f32[16,128]{1,0:T(8,128)S(1)} %add.63), channel_id=1, source_target_pairs={{0,2},{2,0},{4,6},{6,4},{8,10},{10,8},{12,14},{14,12},{1,3},{3,1},... | collective-permute-start | bytes 24584 | tf_op jit(solution)/shard_map/ppermute | solution.py:387
  96.9 2.2 %collective-permute-done.8 = f32[16,128]{1,0:T(8,128)S(1)} collective-permute-done((f32[16,128]{1,0:T(8,128)S(1)}, f32[16,128]{1,0:T(8,128)S(1)}, u32[]{:S(2)}, u32[]{:S(2)}) %collective-permute-start.8) | collective-permute-done | bytes 8224 | tf_op jit(solution)/shard_map/ppermute | solution.py:387
  99.1 3.6 %collective-permute-done.9 = f32[16,128]{1,0:T(8,128)S(1)} collective-permute-done((f32[16,128]{1,0:T(8,128)S(1)}, f32[16,128]{1,0:T(8,128)S(1)}, u32[]{:S(2)}, u32[]{:S(2)}) %collective-permute-start.9) | collective-permute-done | bytes 8224 | tf_op jit(solution)/shard_map/ppermute | solution.py:387
  102.8 0.8 collective-permute-start.10
  103.6 3.7 %collective-permute-done.10 = f32[16,128]{1,0:T(8,128)S(1)} collective-permute-done((f32[16,128]{1,0:T(8,128)S(1)}, f32[16,128]{1,0:T(8,128)S(1)}, u32[]{:S(2)}, u32[]{:S(2)}) %collective-permute-start.10) | collective-permute-done | bytes 8224 | tf_op jit(solution)/shard_map/ppermute | solution.py:387
  107.3 2.8 %combine.1 = f32[8,64,512]{2,1,0:T(8,128)} custom-call(f32[16,128]{1,0:T(8,128)S(1)} %add.66.moments_ref, f32[7,16,128]{2,1,0:T(8,128)S(1)} %copy-done.2, f32[2,16,128]{2,1,0:T(8,128)S(1)} %copy-done.3, f32[128,128]{1,0:T(8,128)S(1)} %copy-done, f32[704,512]{1,0:T(8,128)S(1)} %get-tuple-element.10.rest_0_, f32[704,512]{1,0:T(8,128)S(1)} %get-tuple-element.11.rest_1_, ...), custom_call_target="tpu_custom_call" | custom-call | tf_op jit(solution)/shard_map/combine/pallas_call | solution.py:394
  110.1 3.6 %all-to-all-start.1 = ((f32[8,64,512]{2,1,0:T(8,128)}), f32[8,64,512]{2,1,0:T(8,128)S(1)}, u32[]{:S(2)}, u32[]{:S(2)}) async-start(f32[8,64,512]{2,1,0:T(8,128)} %combine.1), calls=%async_computation.1 | async-start | bytes 2097152 | tf_op jit(solution)/shard_map/all_to_all | solution.py:408
  113.7 2.5 %psum.7 = f32[2]{0:T(128)S(1)} all-reduce(f32[2]{0:T(128)S(1)} %get-tuple-element.16), channel_id=1, replica_groups=mesh['groups'=2,'tm'=8,'rows'=2] {'rows'}, use_global_device_ids=true, to_apply=%region_1.2 | all-reduce | flops 2 | bytes 16 | tf_op jit(solution)/shard_map/psum | solution.py:344
  116.2 0.5 add_sqrt_fusion
  116.7 20.0 %all-to-all-done.1 = f32[8,64,512]{2,1,0:T(8,128)S(1)} async-done(((f32[8,64,512]{2,1,0:T(8,128)}), f32[8,64,512]{2,1,0:T(8,128)S(1)}, u32[]{:S(2)}, u32[]{:S(2)}) %all-to-all-start.1) | async-done | bytes 1048608 | tf_op jit(solution)/shard_map/all_to_all | solution.py:408
  136.7 0.1 copy.11
  136.8 1.2 bitcast_add_fusion
  (35 shorter events, 0.3 us)
Async XLA Ops:
  0.6 16.7 %copy-start.6 = (f32[256,512]{1,0:T(8,128)S(1)}, f32[256,512]{1,0:T(8,128)}, u32[]{:S(2)}) copy-start(f32[256,512]{1,0:T(8,128)} %param.11) | copy-start | bytes 1572868
  1.5 27.6 %collective-permute-start.3 = (f32[2,1,512]{2,1,0:T(1,128)S(1)}, f32[2,1,512]{2,1,0:T(1,128)S(1)}, u32[]{:S(2)}, u32[]{:S(2)}) collective-permute-start(f32[2,1,512]{2,1,0:T(1,128)S(1)} %get-tuple-element.35), channel_id=1, source_target_pairs={{0,1},{2,3},{4,5},{6,7},{8,9},{10,11},{12,13},{14,15},{16,17},{18,... | collective-permute-start | bytes 12296 | tf_op jit(solution)/shard_map/ppermute | solution.py:27
  3.9 25.2 %collective-permute-start.4 = (f32[2,1,512]{2,1,0:T(1,128)S(1)}, f32[2,1,512]{2,1,0:T(1,128)S(1)}, u32[]{:S(2)}, u32[]{:S(2)}) collective-permute-start(f32[2,1,512]{2,1,0:T(1,128)S(1)} %get-tuple-element.36), channel_id=1, source_target_pairs={{1,0},{3,2},{5,4},{7,6},{9,8},{11,10},{13,12},{15,14},{17,16},{19,... | collective-permute-start | bytes 12296 | tf_op jit(solution)/shard_map/ppermute | solution.py:30
  5.9 11.5 %collective-permute-start.1 = (f32[6,512]{1,0:T(8,128)S(1)}, f32[6,512]{1,0:T(8,128)S(1)}, u32[]{:S(2)}, u32[]{:S(2)}) collective-permute-start(f32[6,512]{1,0:T(8,128)S(1)} %get-tuple-element.41), channel_id=1, source_target_pairs={{0,1},{2,3},{4,5},{6,7},{8,9},{10,11},{12,13},{14,15},{16,17},{18,... | collective-permute-start | bytes 36872 | tf_op jit(solution)/shard_map/ppermute | solution.py:27
  8.9 8.5 %collective-permute-start.2 = (f32[6,512]{1,0:T(8,128)S(1)}, f32[6,512]{1,0:T(8,128)S(1)}, u32[]{:S(2)}, u32[]{:S(2)}) collective-permute-start(f32[6,512]{1,0:T(8,128)S(1)} %get-tuple-element.42), channel_id=1, source_target_pairs={{1,0},{3,2},{5,4},{7,6},{9,8},{11,10},{13,12},{15,14},{17,16},{19,... | collective-permute-start | bytes 36872 | tf_op jit(solution)/shard_map/ppermute | solution.py:30
  12.3 16.7 %collective-permute-start = (f32[256,512]{1,0:T(8,128)}, f32[256,512]{1,0:T(8,128)}, u32[]{:S(2)}, u32[]{:S(2)}) collective-permute-start(f32[256,512]{1,0:T(8,128)} %get-tuple-element.33), channel_id=1, source_target_pairs={{0,2},{2,4},{4,6},{6,8},{8,10},{10,12},{12,14},{1,3},{3,5},{5,7},{... | collective-permute-start | bytes 1572872 | tf_op jit(solution)/shard_map/ppermute | solution.py:38
  17.7 11.3 %copy-start.7 = (f32[256,512]{1,0:T(8,128)S(1)}, f32[256,512]{1,0:T(8,128)}, u32[]{:S(2)}) copy-start(f32[256,512]{1,0:T(8,128)} %param.10) | copy-start | bytes 1572868
  17.7 11.4 %copy-start.5 = (f32[2,256,512]{2,1,0:T(8,128)S(1)}, f32[2,256,512]{2,1,0:T(8,128)}, u32[]{:S(2)}) copy-start(f32[2,256,512]{2,1,0:T(8,128)} %param.9) | copy-start | bytes 3145732
  18.2 10.9 %copy-start.4 = (f32[2,256,512]{2,1,0:T(8,128)S(1)}, f32[2,256,512]{2,1,0:T(8,128)}, u32[]{:S(2)}) copy-start(f32[2,256,512]{2,1,0:T(8,128)} %param.8) | copy-start | bytes 3145732
  30.3 4.3 %collective-permute-start.6 = (f32[2,6,512]{2,1,0:T(8,128)S(1)}, f32[2,6,512]{2,1,0:T(8,128)S(1)}, u32[]{:S(2)}, u32[]{:S(2)}) collective-permute-start(f32[2,6,512]{2,1,0:T(8,128)S(1)} %get-tuple-element.31), channel_id=1, source_target_pairs={{1,0},{3,2},{5,4},{7,6},{9,8},{11,10},{13,12},{15,14},{17,16},{19,... | collective-permute-start | bytes 73736 | tf_op jit(solution)/shard_map/ppermute | solution.py:30
  31.6 3.9 %collective-permute-start.5 = (f32[2,6,512]{2,1,0:T(8,128)S(1)}, f32[2,6,512]{2,1,0:T(8,128)S(1)}, u32[]{:S(2)}, u32[]{:S(2)}) collective-permute-start(f32[2,6,512]{2,1,0:T(8,128)S(1)} %get-tuple-element.32), channel_id=1, source_target_pairs={{0,1},{2,3},{4,5},{6,7},{8,9},{10,11},{12,13},{14,15},{16,17},{18,... | collective-permute-start | bytes 73736 | tf_op jit(solution)/shard_map/ppermute | solution.py:27
  41.4 42.7 %copy-start.1 = (f32[128,128]{1,0:T(8,128)S(1)}, f32[128,128]{1,0:T(8,128)}, u32[]{:S(2)}) copy-start(f32[128,128]{1,0:T(8,128)} %constant.46.clone.mix_ref) | copy-start | bytes 196612
  41.4 42.7 %all-to-all-start = ((f32[8,88,512]{2,1,0:T(8,128)}), f32[8,88,512]{2,1,0:T(8,128)S(1)}, u32[]{:S(2)}, u32[]{:S(2)}) async-start(f32[8,88,512]{2,1,0:T(8,128)} %constant_dynamic-update-slice_fusion), calls=%async_computation | async-start | bytes 2883584 | tf_op jit(solution)/shard_map/all_to_all | solution.py:356
  49.4 57.9 %copy-start = (f32[128,128]{1,0:T(8,128)S(1)}, f32[128,128]{1,0:T(8,128)}, u32[]{:S(2)}) copy-start(f32[128,128]{1,0:T(8,128)} %constant.49.clone.mix_ref) | copy-start | bytes 196612
  49.4 57.9 %copy-start.2 = (f32[7,16,128]{2,1,0:T(8,128)S(1)}, f32[7,16,128]{2,1,0:T(8,128)}, u32[]{:S(2)}) copy-start(f32[7,16,128]{2,1,0:T(8,128)} %constant.47.clone.table_ref) | copy-start | bytes 172036
  49.4 57.9 %copy-start.3 = (f32[2,16,128]{2,1,0:T(8,128)S(1)}, f32[2,16,128]{2,1,0:T(8,128)}, u32[]{:S(2)}) copy-start(f32[2,16,128]{2,1,0:T(8,128)} %constant.48.clone.shift_ref) | copy-start | bytes 49156
  94.3 1.2 collective-permute-start.7
  95.5 3.7 %collective-permute-start.8 = (f32[16,128]{1,0:T(8,128)S(1)}, f32[16,128]{1,0:T(8,128)S(1)}, u32[]{:S(2)}, u32[]{:S(2)}) collective-permute-start(f32[16,128]{1,0:T(8,128)S(1)} %add.63), channel_id=1, source_target_pairs={{0,2},{2,0},{4,6},{6,4},{8,10},{10,8},{12,14},{14,12},{1,3},{3,1},... | collective-permute-start | bytes 24584 | tf_op jit(solution)/shard_map/ppermute | solution.py:387
  99.1 3.7 %collective-permute-start.9 = (f32[16,128]{1,0:T(8,128)S(1)}, f32[16,128]{1,0:T(8,128)S(1)}, u32[]{:S(2)}, u32[]{:S(2)}) collective-permute-start(f32[16,128]{1,0:T(8,128)S(1)} %add.64), channel_id=1, source_target_pairs={{0,4},{2,6},{4,0},{6,2},{8,12},{10,14},{12,8},{14,10},{1,5},{3,7},... | collective-permute-start | bytes 24584 | tf_op jit(solution)/shard_map/ppermute | solution.py:387
  102.8 4.5 %collective-permute-start.10 = (f32[16,128]{1,0:T(8,128)S(1)}, f32[16,128]{1,0:T(8,128)S(1)}, u32[]{:S(2)}, u32[]{:S(2)}) collective-permute-start(f32[16,128]{1,0:T(8,128)S(1)} %add.65), channel_id=1, source_target_pairs={{0,8},{2,10},{4,12},{6,14},{8,0},{10,2},{12,4},{14,6},{1,9},{3,11}... | collective-permute-start | bytes 24584 | tf_op jit(solution)/shard_map/ppermute | solution.py:387
  110.1 26.6 %all-to-all-start.1 = ((f32[8,64,512]{2,1,0:T(8,128)}), f32[8,64,512]{2,1,0:T(8,128)S(1)}, u32[]{:S(2)}, u32[]{:S(2)}) async-start(f32[8,64,512]{2,1,0:T(8,128)} %combine.1), calls=%async_computation.1 | async-start | bytes 2097152 | tf_op jit(solution)/shard_map/all_to_all | solution.py:408

commit v3 on v2

--- a/solution.py
+++ b/solution.py
@@ -9,27 +9,16 @@
 from jax.experimental.pallas import tpu as pltpu
 from jax.sharding import PartitionSpec as P
 
+
 CG_ITERS = 3
 DEPTH = 2 * CG_ITERS
 MOMENTS = 2 * DEPTH + 1
 UNROLL = 16
+PAD = 8
 
 circulant_alpha = 0.05
 time_step = 0.5
 rms_eps = 1e-06
-
-
-def extended(block, sides, width):
-    for axis, dim in sides:
-        count = lax.axis_size(axis)
-        forward = [(i, i + 1) for i in range(count - 1)]
-        backward = [(target, source) for source, target in forward]
-        low = lax.ppermute(
-            lax.slice_in_dim(block, block.shape[dim] - width, None, axis=dim), axis, forward
-        )
-        high = lax.ppermute(lax.slice_in_dim(block, 0, width, axis=dim), axis, backward)
-        block = jnp.concatenate([low, block, high], axis=dim)
-    return block
 
 
 def from_behind(value, axis, steps):
@@ -38,27 +27,22 @@
     return lax.ppermute(value, axis, [(source, source + steps) for source in range(initial, last)])
 
 
-def faces_from(padded_rows):
-    centre = padded_rows[1:-1]
-    columns = jnp.pad(centre, ((0, 0), (1, 1)), mode="edge")
-    north_face = 0.5 * (centre + padded_rows[:-2])
-    south_face = 0.5 * (centre + padded_rows[2:])
-    west_face = 0.5 * (centre + columns[:, :-2])
-    east_face = 0.5 * (centre + columns[:, 2:])
-    return (north_face, south_face, west_face, east_face)
-
-
-def apply_faces(padded_rows, weights):
-    north_face, south_face, west_face, east_face = weights
-    centre = padded_rows[..., 1:-1, :]
-    lead_pad = [(0, 0)] * (centre.ndim - 1)
-    columns = jnp.pad(centre, lead_pad + [(1, 1)])
+def border_rows(blocks, axis, width):
+    count = lax.axis_size(axis)
+    if count == 2:
+        first = lax.axis_index(axis) == 0
+
+        def edge(block):
+            return jnp.where(first, block[..., -width:, :], block[..., :width, :])
+
+        mine = jnp.concatenate([edge(block).reshape(-1, block.shape[-1]) for block in blocks])
+        got = lax.ppermute(mine, axis, [(0, 1), (1, 0)])
+        return got, got
+    low = jnp.concatenate([b[..., -width:, :].reshape(-1, b.shape[-1]) for b in blocks])
+    high = jnp.concatenate([b[..., :width, :].reshape(-1, b.shape[-1]) for b in blocks])
     return (
-        (north_face + south_face + west_face + east_face) * centre
-        - north_face * padded_rows[..., :-2, :]
-        - south_face * padded_rows[..., 2:, :]
-        - west_face * columns[..., :-2]
-        - east_face * columns[..., 2:]
+        lax.ppermute(low, axis, [(i, i + 1) for i in range(count - 1)]),
+        lax.ppermute(high, axis, [(i + 1, i) for i in range(count - 1)]),
     )
 
 
@@ -127,14 +111,150 @@
     return np.stack(powers)
 
 
-def krylov_body(length, slab, halo, place_ref, pieces_ref, diff_ref, mix_ref, *rest):
+def flux_terms(here, under_first, east_weight, south_weight, west_weight, north, masks):
+    is_first, is_last, is_top, is_bottom = masks
+    tiles = len(here)
+    south = []
+    for t in range(tiles):
+        under = jnp.where(
+            is_bottom, pltpu.roll(under_first[t], 7, 0), pltpu.roll(here[t], 7, 0)
+        )
+        south.append(south_weight[t] * (under - here[t]))
+    turned = [pltpu.roll(v, 127, 1) for v in here] + [0.0]
+    east = [
+        east_weight[t] * (jnp.where(is_last, turned[t + 1], turned[t]) - here[t])
+        for t in range(tiles)
+    ]
+    moved = [west_weight * here[0]] + [pltpu.roll(f, 1, 1) for f in east]
+    value = []
+    for t in range(tiles):
+        from_north = jnp.where(is_top, pltpu.roll(north[t], 1, 0), pltpu.roll(south[t], 1, 0))
+        value.append(
+            (jnp.where(is_first, moved[t], moved[t + 1]) - east[t]) + (from_north - south[t])
+        )
+    return value, south
+
+
+def pack(out_ref, at, source_ref, slab, halo):
+    rows = slab + 2 * halo
+    for target in range(out_ref.shape[0]):
+        first = slab * target + PAD - halo
+        for t in range(source_ref.shape[-1] // 128):
+            out_ref[target, at + rows * t : at + rows * (t + 1), :] = source_ref[
+                first : first + rows, 128 * t : 128 * (t + 1)
+            ]
+
+
+def residual_body(slab, halo, rank_ref, iterate_ref, forcing_ref, diff_ref, low_ref, high_ref,
+                  pieces_ref, partial_ref, squares_ref, *scratch):
+    steps, rows_dev, columns = iterate_ref.shape
+    tiles = columns // 128
+    blocks = rows_dev // 8 + 2
+    lane8 = lax.broadcasted_iota(jnp.int32, (8, 128), 1)
+    sub8 = lax.broadcasted_iota(jnp.int32, (8, 128), 0)
+    masks = (lane8 == 0, lane8 == 127, sub8 == 0, sub8 == 7)
+    is_low_edge = rank_ref[0] == 0
+    is_high_edge = rank_ref[0] == rank_ref[1] - 1
+    keep_low = jnp.where(is_low_edge, 0.0, 1.0)
+    keep_high = jnp.where(is_high_edge, 0.0, 1.0)
+
+    def cut(ref, at, lead=()):
+        return [ref[lead + (slice(at, at + 8), slice(128 * t, 128 * t + 128))] for t in range(tiles)]
+
+    def block_of(ref, step, slot, b):
+        if b == 0:
+            return [v * keep_low for v in cut(low_ref, 8 * slot)]
+        if b == blocks - 1:
+            return [v * keep_high for v in cut(high_ref, 8 * slot)]
+        return cut(ref, 8 * (b - 1), (step,))
+
+    def diff_of(b):
+        if b == 0:
+            mine = [
+                jnp.broadcast_to(diff_ref[0:1, 128 * t : 128 * t + 128], (8, 128))
+                for t in range(tiles)
+            ]
+            got = cut(low_ref, 16 * steps)
+            return [jnp.where(is_low_edge, m, g) for m, g in zip(mine, got)]
+        if b == blocks - 1:
+            mine = [
+                jnp.broadcast_to(diff_ref[rows_dev - 1 :, 128 * t : 128 * t + 128], (8, 128))
+                for t in range(tiles)
+            ]
+            got = cut(high_ref, 16 * steps)
+            return [jnp.where(is_high_edge, m, g) for m, g in zip(mine, got)]
+        return cut(diff_ref, 8 * (b - 1))
+
+    quarter = 0.5 * time_step
+    zeros = [jnp.zeros((8, 128), jnp.float32)] * tiles
+    diff = diff_of(0)
+    here = [block_of(iterate_ref, s, s, 0) for s in range(steps)]
+    north = [zeros] * steps
+    squares = [jnp.zeros((8, 128), jnp.float32)] * steps
+    for b in range(blocks):
+        last = b + 1 == blocks
+        diff_next = diff if last else diff_of(b + 1)
+        next_here = here if last else [block_of(iterate_ref, s, s, b + 1) for s in range(steps)]
+        below = [
+            jnp.where(masks[3], pltpu.roll(diff_next[t], 7, 0), pltpu.roll(diff[t], 7, 0))
+            for t in range(tiles)
+        ]
+        turned = [pltpu.roll(v, 127, 1) for v in diff] + [diff[-1]]
+        after = [jnp.where(masks[1], turned[t + 1], turned[t]) for t in range(tiles)]
+        south_weight = [quarter * (diff[t] + below[t]) for t in range(tiles)]
+        east_weight = [quarter * (diff[t] + after[t]) for t in range(tiles)]
+        west_weight = (2.0 * quarter) * diff[0]
+        for s in range(steps):
+            value, north[s] = flux_terms(
+                here[s], next_here[s], east_weight, south_weight, west_weight, north[s], masks
+            )
+            force = block_of(forcing_ref, s, steps + s, b)
+            for t in range(tiles):
+                left = time_step * force[t] - here[s][t] - value[t]
+                if b == 0:
+                    left = left * keep_low
+                elif last:
+                    left = left * keep_high
+                if s == 0:
+                    partial_ref[8 * b : 8 * b + 8, 128 * t : 128 * t + 128] = left
+                else:
+                    left = left + here[s - 1][t]
+                    scratch[s - 1][8 * b : 8 * b + 8, 128 * t : 128 * t + 128] = left
+                    if 0 < b < blocks - 1:
+                        squares[s] = squares[s] + left * left
+        diff, here = diff_next, next_here
+    for s in range(1, steps):
+        squares_ref[s - 1] = squares[s]
+        pack(pieces_ref, (s - 1) * tiles * (slab + 2 * halo), scratch[s - 1], slab, halo)
+
+
+def first_step_body(slab, halo, rank_ref, partial_ref, previous_ref, low_ref, high_ref,
+                    pieces_ref, squares_ref, whole_ref):
+    rows_dev, columns = previous_ref.shape
+    keep_low = jnp.where(rank_ref[0] == 0, 0.0, 1.0)
+    keep_high = jnp.where(rank_ref[0] == rank_ref[1] - 1, 0.0, 1.0)
+    whole_ref[:PAD, :] = partial_ref[:PAD, :] + keep_low * low_ref[...]
+    whole_ref[PAD + rows_dev :, :] = partial_ref[PAD + rows_dev :, :] + keep_high * high_ref[...]
+    squares = jnp.zeros((8, columns), jnp.float32)
+    for at in range(0, rows_dev, 8):
+        value = partial_ref[PAD + at : PAD + at + 8, :] + previous_ref[at : at + 8, :]
+        whole_ref[PAD + at : PAD + at + 8, :] = value
+        squares = squares + value * value
+    total = squares[:, :128]
+    for t in range(1, columns // 128):
+        total = total + squares[:, 128 * t : 128 * t + 128]
+    squares_ref[0] = total
+    pack(pieces_ref, 0, whole_ref, slab, halo)
+
+
+def krylov_body(length, slab, halo, place_ref, early_ref, late_ref, diff_ref, mix_ref, *rest):
     vectors = rest[:DEPTH]
     moments_ref, south_ref, east_ref, west_ref = rest[DEPTH:]
     rows = slab + 2 * halo
     columns = diff_ref.shape[-1]
     groups = length // 8
     tiles = columns // 128
-    steps_dev = pieces_ref.shape[1] // rows
+    steps_dev = early_ref.shape[1] // (rows * tiles) + 1
 
     centre = diff_ref[...]
     below = jnp.concatenate([centre[1:], centre[-1:]], axis=0)
@@ -158,15 +278,19 @@
     if starts[-1] + 8 < rows:
         starts.append(rows - 8)
     for start in starts:
-        cells = []
-        for source in range(length // steps_dev):
-            for step in range(steps_dev):
-                at = step * rows + start
-                cells.append(pieces_ref[source, at : at + 8, :])
-        block = jnp.concatenate(cells, axis=0)
-        vectors[0][start * length : (start + 8) * length, :] = jnp.dot(
-            mix, block, precision=lax.Precision.HIGHEST, preferred_element_type=jnp.float32
-        )
+        for t in range(tiles):
+            cells = []
+            for source in range(length // steps_dev):
+                for step in range(steps_dev):
+                    ref = late_ref if step == 0 else early_ref
+                    at = (max(step - 1, 0) * tiles + t) * rows + start
+                    cells.append(ref[source, at : at + 8, :])
+            vectors[0][start * length : (start + 8) * length, 128 * t : 128 * t + 128] = jnp.dot(
+                mix,
+                jnp.concatenate(cells, axis=0),
+                precision=lax.Precision.HIGHEST,
+                preferred_element_type=jnp.float32,
+            )
 
     lane8 = lax.broadcasted_iota(jnp.int32, (8, 128), 1)
     is_first = lane8 == 0
@@ -315,7 +439,7 @@
             out_ref[step // steps_dev, at : at + 8, :] = result[step * 8 : step * 8 + 8]
 
 
-def shards(iterate, forcing, initial_state, diffusivity):
+def iteration(iterate, forcing, initial_state, diffusivity):
     steps_dev, rows_dev, columns_dev = iterate.shape
     time_devices = lax.axis_size("tm")
     row_devices = lax.axis_size("rows")
@@ -327,54 +451,73 @@
     halo = DEPTH
     rows = slab + 2 * halo
 
-    rimmed = extended(diffusivity, (("rows", 0),), halo)
-    here = lax.broadcasted_iota(jnp.int32, (rimmed.shape[0], 1), 0)
-    rimmed = jnp.where((row_rank == 0) & (here < halo), diffusivity[:1], rimmed)
-    rimmed = jnp.where(
-        (row_rank == row_devices - 1) & (here >= halo + rows_dev), diffusivity[-1:], rimmed
-    )
-    local_faces = faces_from(rimmed[halo - 1 : halo + rows_dev + 1])
+    tiles = columns_dev // 128
+    vmem = pl.BlockSpec(memory_space=pltpu.VMEM)
+    smem = pl.BlockSpec(memory_space=pltpu.SMEM)
+    params = pltpu.CompilerParams(vmem_limit_bytes=24 * 2**20)
+    rank = jnp.stack([row_rank, jnp.int32(row_devices)]).astype(jnp.int32)
+
     arriving = from_behind(iterate[-1], "tm", 1)
-    first_previous = jnp.where(time_rank == 0, initial_state, arriving)
-    previous = jnp.concatenate([first_previous[None], iterate[:-1]], axis=0)
-    iterate_rim = extended(iterate, (("rows", 1),), 1)
-    residual = (
-        time_step * forcing + previous - iterate - time_step * apply_faces(iterate_rim, local_faces)
-    )
-    squares = lax.psum(jnp.sum(residual * residual, axis=(1, 2)), "rows")
-    residual_rms = jnp.sqrt(squares / cell_count + rms_eps)
-
-    wide = extended(residual, (("rows", 1),), halo)
-    pieces = jnp.stack(
-        [
-            lax.slice_in_dim(wide, slab * k, slab * k + rows, axis=1).reshape(
-                steps_dev * rows, columns_dev
-            )
-            for k in range(time_devices)
-        ]
-    )
-    by_cells = lax.all_to_all(pieces, "tm", split_axis=0, concat_axis=0, tiled=True)
-    diff_slab = lax.dynamic_slice_in_dim(rimmed, slab * time_rank, rows, axis=0)
+    low, high = border_rows((iterate, forcing, diffusivity), "rows", PAD)
+    padded = rows_dev + 2 * PAD
+    early, partial, squares_late = pl.pallas_call(
+        functools.partial(residual_body, slab, halo),
+        out_shape=[
+            jax.ShapeDtypeStruct(
+                (time_devices, (steps_dev - 1) * tiles * rows, 128), jnp.float32
+            ),
+            pltpu.VMEM((padded, columns_dev), jnp.float32),
+            jax.ShapeDtypeStruct((steps_dev - 1, 8, 128), jnp.float32),
+        ],
+        in_specs=[smem] + [vmem] * 5,
+        out_specs=[vmem] * 3,
+        scratch_shapes=[pltpu.VMEM((padded, columns_dev), jnp.float32)] * (steps_dev - 1),
+        compiler_params=params,
+        name="residual",
+    )(rank, iterate, forcing, diffusivity, low, high)
+    early = lax.all_to_all(early, "tm", split_axis=0, concat_axis=0, tiled=True)
+
+    previous = jnp.where(time_rank == 0, initial_state, arriving)
+    before_low, before_high = border_rows((previous,), "rows", PAD)
+    late, squares_first = pl.pallas_call(
+        functools.partial(first_step_body, slab, halo),
+        out_shape=[
+            jax.ShapeDtypeStruct((time_devices, tiles * rows, 128), jnp.float32),
+            jax.ShapeDtypeStruct((1, 8, 128), jnp.float32),
+        ],
+        in_specs=[smem] + [vmem] * 4,
+        out_specs=[vmem] * 2,
+        scratch_shapes=[pltpu.VMEM((padded, columns_dev), jnp.float32)],
+        compiler_params=params,
+        name="first_step",
+    )(rank, partial, previous, before_low, before_high)
+    late = lax.all_to_all(late, "tm", split_axis=0, concat_axis=0, tiled=True)
+
+    squares = jnp.sum(jnp.concatenate([squares_first, squares_late]), axis=(1, 2))
+    residual_rms = jnp.sqrt(lax.psum(squares, "rows") / cell_count + rms_eps)
+
+    diff_low = jnp.where(row_rank == 0, diffusivity[:1], low[-PAD:])
+    diff_high = jnp.where(row_rank == row_devices - 1, diffusivity[-1:], high[-PAD:])
+    rimmed = jnp.concatenate([diff_low, diffusivity, diff_high])
+    diff_slab = lax.dynamic_slice_in_dim(rimmed, slab * time_rank + PAD - halo, rows, axis=0)
     place = jnp.stack(
         [row_rank * rows_dev + time_rank * slab - halo, jnp.int32(rows_dev * row_devices)]
     ).astype(jnp.int32)
 
-    vmem = pl.BlockSpec(memory_space=pltpu.VMEM)
-    smem = pl.BlockSpec(memory_space=pltpu.SMEM)
     vector = pltpu.VMEM((rows * length, columns_dev), jnp.float32)
     *powers, moments = pl.pallas_call(
         functools.partial(krylov_body, length, slab, halo),
         out_shape=[vector] * DEPTH + [jax.ShapeDtypeStruct((length, 128), jnp.float32)],
-        in_specs=[smem, vmem, vmem, vmem],
+        in_specs=[smem] + [vmem] * 4,
         out_specs=[vmem] * (DEPTH + 1),
         scratch_shapes=[
             pltpu.VMEM((rows * 8, columns_dev), jnp.float32),
             pltpu.VMEM((rows * 8, columns_dev), jnp.float32),
             pltpu.VMEM((rows * 8, 128), jnp.float32),
         ],
-        compiler_params=pltpu.CompilerParams(vmem_limit_bytes=24 * 2**20),
+        compiler_params=params,
         name="krylov",
-    )(place, by_cells, diff_slab, jnp.asarray(block_forward(length, 8)))
+    )(place, early, late, diff_slab, jnp.asarray(block_forward(length, 8)))
 
     for axis in ("rows", "tm"):
         count = lax.axis_size(axis)
@@ -396,7 +539,7 @@
         out_shape=jax.ShapeDtypeStruct((time_devices, steps_dev * slab, columns_dev), jnp.float32),
         in_specs=[vmem] * (4 + DEPTH),
         out_specs=vmem,
-        compiler_params=pltpu.CompilerParams(vmem_limit_bytes=24 * 2**20),
+        compiler_params=params,
         name="combine",
     )(
         moments,
@@ -420,7 +563,7 @@
         P(("groups", "rows"), None),
     )
     return jax.shard_map(
-        shards,
+        iteration,
         mesh=mesh,
         in_specs=placed,
         out_specs=(P(("groups", "tm"), "rows", None), P(("groups", "tm"))),

time: 139 us -> 131 us (0.942)
  waiting for transfers between devices: 76.9 us -> 66.2 us
  Pallas kernels: 13 us -> 19.1 us
  local copies, waits for them, and re-layouts: 9.61 us -> 5.31 us
  starting transfers between devices: 31.2 us -> 32.6 us
    all_to_all x2 -> x3, waiting for transfers between devices: 54.6 us -> 38.8 us  [the longest x1 19.9 us: iteration(): lax.all_to_all(corrected, 'tm', split_axis=0, concat_axis=0, tiled=True)]
    all_to_all x2 -> x3, starting transfers between devices: 11.6 us -> 25.3 us  [the longest x1 14.4 us: iteration(): late = lax.all_to_all(late, 'tm', split_axis=0, concat_axis=0, tiled=True)]
    ppermute x10 -> x6, starting transfers between devices: 14.6 us -> 2.52 us  [the longest x4 1.89 us: iteration(): moments = moments + lax.ppermute(moments, axis, pairs)]
    pallas_call x2 -> x4, Pallas kernels: 13 us -> 19.1 us  [the longest x1 10.1 us: iteration(): pl.pallas_call(functools.partial(krylov_body, length, slab, halo), out_sh...]
    ppermute x1, waiting for transfers between devices: 10.8 us -> 14.2 us  [from_behind(): lax.ppermute(value, axis, [(source, source + steps) for source in range(i...]
    slice x6 -> x1, local copies, waits for them, and re-layouts: 1.75 us -> 0.01 us  [iteration(): diffusivity[-1:]]
    ppermute x10 -> x6, waiting for transfers between devices: 11.6 us -> 13.1 us  [the longest x4 11.1 us: iteration(): moments = moments + lax.ppermute(moments, axis, pairs)]
    reshape x0 -> x2, other arithmetic: none -> 1.56 us  [border_rows(): edge(block).reshape(-1, block.shape[-1])]
  transfers between devices with their start and end apart: 13 -> 10, of which waited for: 8 -> 9; matrix products, arithmetic and copies ran while one was open for 3% -> 1% of each run, Pallas kernels for 0% -> 0%
where the time goes in v3:
time: 131 us
  waiting for transfers between devices  66.2 us (51%)
  starting transfers between devices  32.6 us (25%)
  Pallas kernels  19.1 us (15%)
  local copies, waits for them, and re-layouts  5.31 us (4%)
  other arithmetic  4.42 us (3%)
  blocking collectives  2.45 us (2%)
    all_to_all x1, waiting for transfers between devices, iteration(): lax.all_to_all(corrected, 'tm', split_axis=0, concat_axis=0, tiled=True)  19.9 us
    all_to_all x1, waiting for transfers between devices, iteration(): late = lax.all_to_all(late, 'tm', split_axis=0, concat_axis=0, tiled=True)  18.9 us
    all_to_all x1, starting transfers between devices, iteration(): late = lax.all_to_all(late, 'tm', split_axis=0, concat_axis=0, tiled=True)  14.4 us
    ppermute x1, waiting for transfers between devices, from_behind(): lax.ppermute(value, axis, [(source, source + steps) for source in range(i...  14.2 us
    ppermute x4, waiting for transfers between devices, iteration(): moments = moments + lax.ppermute(moments, axis, pairs)  11.1 us
    pallas_call x1, Pallas kernels, iteration(): pl.pallas_call(functools.partial(krylov_body, length, slab, halo), out_sh...  10.1 us
    all_to_all x1, starting transfers between devices, iteration(): early = lax.all_to_all(early, 'tm', split_axis=0, concat_axis=0, tiled=True)  7.3 us
    pallas_call x1, Pallas kernels, iteration(): pl.pallas_call(functools.partial(residual_body, slab, halo), out_shape=[j...  5.73 us
  transfers between devices with their start and end apart: 10, of which 9 were waited for; matrix products, arithmetic and copies ran while one was open for 1% of the time, Pallas kernels for 0%

profile of v3, /device:TPU:0, one launch (start us, length us, event | category | flops | bytes accessed | tf_op | source)
XLA Modules:
  0.0 130.8 jit_solution(15031828817021753312)
XLA Ops:
  0.6 0.7 slice_select_fusion.1
  1.4 0.8 select_bitcast_fusion
  2.2 0.8 select_bitcast_fusion.1
  3.0 0.6 collective-permute-start
  3.5 0.1 pad_add_fusion.1.rank_ref
  3.6 0.8 collective-permute-done.low_ref.high_ref
  4.4 1.2 copy-done
  5.7 1.0 copy-done.2
  6.7 1.2 copy-done.4
  7.9 5.7 %residual.1 = (f32[8,176,128]{2,1,0:T(8,128)}, f32[272,512]{1,0:T(8,128)S(1)}, f32[1,8,128]{2,1,0:T(8,128)S(1)}) custom-call(s32[2]{0:T(128)S(1)} %pad_add_fusion.1.rank_ref, f32[2,256,512]{2,1,0:T(8,128)S(1)} %copy-done, f32[2,256,512]{2,1,0:T(8,128)S(1)} %copy-done.4, f32[256,512]{1,0:T(8,128)S(1)} %copy-done.2, ...), custom_call_target="tpu_custom_call" | custom-call | tf_op jit(solution)/shard_map/residual/pallas_call | solution.py:463
  13.7 7.3 %all-to-all-start = ((f32[8,176,128]{2,1,0:T(8,128)}), f32[8,176,128]{2,1,0:T(8,128)S(1)}, u32[]{:S(2)}, u32[]{:S(2)}) async-start(f32[8,176,128]{2,1,0:T(8,128)} %get-tuple-element.14), calls=%async_computation | async-start | bytes 1441792 | tf_op jit(solution)/shard_map/all_to_all | solution.py:478
  21.0 0.0 copy-done.1
  21.0 0.8 slice_bitcast_fusion
  21.8 4.7 %collective-permute-start.1 = (f32[256,512]{1,0:T(8,128)}, f32[256,512]{1,0:T(8,128)}, u32[]{:S(2)}, u32[]{:S(2)}) collective-permute-start(f32[256,512]{1,0:T(8,128)} %slice_bitcast_fusion), channel_id=1, source_target_pairs={{0,2},{2,4},{4,6},{6,8},{8,10},{10,12},{12,14},{1,3},{3,5},{5,7},{... | collective-permute-start | bytes 1572872 | tf_op jit(solution)/shard_map/ppermute | solution.py:27
  26.5 14.2 %collective-permute-done.1 = f32[256,512]{1,0:T(8,128)} collective-permute-done((f32[256,512]{1,0:T(8,128)}, f32[256,512]{1,0:T(8,128)}, u32[]{:S(2)}, u32[]{:S(2)}) %collective-permute-start.1) | collective-permute-done | bytes 524320 | tf_op jit(solution)/shard_map/ppermute | solution.py:27
  40.7 0.0 copy-done.10
  40.7 0.1 broadcast_select_fusion.previous_ref
  40.8 0.0 copy-start.3
  40.8 0.1 collective-permute-start.2
  40.9 1.2 collective-permute-done.2.low_ref.high_ref
  42.1 0.6 first_step.1
  42.7 0.0 copy-start.5
  42.7 0.9 copy-done.5
  43.6 0.0 all-to-all-done.early_ref
  43.6 14.4 %all-to-all-start.1 = ((f32[8,176,128]{2,1,0:T(8,128)}), f32[8,176,128]{2,1,0:T(8,128)S(1)}, u32[]{:S(2)}, u32[]{:S(2)}) async-start(f32[8,176,128]{2,1,0:T(8,128)} %copy-done.5), calls=%async_computation.1 | async-start | bytes 1441792 | tf_op jit(solution)/shard_map/all_to_all | solution.py:494
  58.0 0.0 copy-start.8
  58.1 0.0 copy-start.9
  58.1 0.1 pad_add_fusion.place_ref
  58.2 0.0 copy-done.3
  58.2 18.9 %all-to-all-done.1.late_ref = f32[8,176,128]{2,1,0:T(8,128)S(1)} async-done(((f32[8,176,128]{2,1,0:T(8,128)}), f32[8,176,128]{2,1,0:T(8,128)S(1)}, u32[]{:S(2)}, u32[]{:S(2)}) %all-to-all-start.1) | async-done | bytes 720928 | tf_op jit(solution)/shard_map/all_to_all | solution.py:494
  77.1 10.1 %krylov.1 = (f32[704,512]{1,0:T(8,128)S(1)}, f32[704,512]{1,0:T(8,128)S(1)}, f32[704,512]{1,0:T(8,128)S(1)}, f32[704,512]{1,0:T(8,128)S(1)}, f32[704,512]{1,0:T(...) custom-call(s32[2]{0:T(128)S(1)} %pad_add_fusion.place_ref, f32[8,176,128]{2,1,0:T(8,128)S(1)} %all-to-all-done.early_ref, ...), custom_call_target="tpu_custom_call" | custom-call | tf_op jit(solution)/shard_map/krylov/pallas_call | solution.py:508
  87.2 0.0 collective-permute-start.3
  87.2 1.2 collective-permute-done.3
  88.4 1.4 %collective-permute-start.4 = (f32[16,128]{1,0:T(8,128)S(1)}, f32[16,128]{1,0:T(8,128)S(1)}, u32[]{:S(2)}, u32[]{:S(2)}) collective-permute-start(f32[16,128]{1,0:T(8,128)S(1)} %add.35), channel_id=1, source_target_pairs={{0,2},{2,0},{4,6},{6,4},{8,10},{10,8},{12,14},{14,12},{1,3},{3,1},... | collective-permute-start | bytes 24584 | tf_op jit(solution)/shard_map/ppermute | solution.py:530
  89.8 2.2 %collective-permute-done.4 = f32[16,128]{1,0:T(8,128)S(1)} collective-permute-done((f32[16,128]{1,0:T(8,128)S(1)}, f32[16,128]{1,0:T(8,128)S(1)}, u32[]{:S(2)}, u32[]{:S(2)}) %collective-permute-start.4) | collective-permute-done | bytes 8224 | tf_op jit(solution)/shard_map/ppermute | solution.py:530
  92.0 0.5 collective-permute-start.5
  92.5 3.2 %collective-permute-done.5 = f32[16,128]{1,0:T(8,128)S(1)} collective-permute-done((f32[16,128]{1,0:T(8,128)S(1)}, f32[16,128]{1,0:T(8,128)S(1)}, u32[]{:S(2)}, u32[]{:S(2)}) %collective-permute-start.5) | collective-permute-done | bytes 8224 | tf_op jit(solution)/shard_map/ppermute | solution.py:530
  95.7 0.0 collective-permute-start.6
  95.7 4.5 %collective-permute-done.6 = f32[16,128]{1,0:T(8,128)S(1)} collective-permute-done((f32[16,128]{1,0:T(8,128)S(1)}, f32[16,128]{1,0:T(8,128)S(1)}, u32[]{:S(2)}, u32[]{:S(2)}) %collective-permute-start.6) | collective-permute-done | bytes 8224 | tf_op jit(solution)/shard_map/ppermute | solution.py:530
  100.2 0.0 copy-done.6
  100.2 2.6 %combine.1 = f32[8,64,512]{2,1,0:T(8,128)} custom-call(f32[16,128]{1,0:T(8,128)S(1)} %add.38.moments_ref, f32[7,16,128]{2,1,0:T(8,128)S(1)} %copy-done.8, f32[2,16,128]{2,1,0:T(8,128)S(1)} %copy-done.9, f32[128,128]{1,0:T(8,128)S(1)} %copy-done.6, f32[704,512]{1,0:T(8,128)S(1)} %get-tuple-element.18.rest_0_, f32[704,512]{1,0:T(8,128)S(1)} %get-tuple-element.19.rest_1_, ...), custom_call_target="tpu_custom_call" | custom-call | tf_op jit(solution)/shard_map/combine/pallas_call | solution.py:537
  102.9 3.6 %all-to-all-start.2 = ((f32[8,64,512]{2,1,0:T(8,128)}), f32[8,64,512]{2,1,0:T(8,128)S(1)}, u32[]{:S(2)}, u32[]{:S(2)}) async-start(f32[8,64,512]{2,1,0:T(8,128)} %combine.1), calls=%async_computation.2 | async-start | bytes 2097152 | tf_op jit(solution)/shard_map/all_to_all | solution.py:551
  106.5 0.1 maximum_reduce_fusion
  106.6 2.4 %psum.7 = f32[2]{0:T(128)S(1)} all-reduce(f32[2]{0:T(128)S(1)} %maximum_reduce_fusion), channel_id=1, replica_groups=mesh['groups'=2,'tm'=8,'rows'=2] {'rows'}, use_global_device_ids=true, to_apply=%region_1.2 | all-reduce | flops 2 | bytes 16 | tf_op jit(solution)/shard_map/psum | solution.py:497
  109.0 0.5 add_sqrt_fusion
  109.5 19.9 %all-to-all-done.2 = f32[8,64,512]{2,1,0:T(8,128)S(1)} async-done(((f32[8,64,512]{2,1,0:T(8,128)}), f32[8,64,512]{2,1,0:T(8,128)S(1)}, u32[]{:S(2)}, u32[]{:S(2)}) %all-to-all-start.2) | async-done | bytes 1048608 | tf_op jit(solution)/shard_map/all_to_all | solution.py:551
  129.5 0.1 copy.10
  129.6 1.2 bitcast_add_fusion
  (19 shorter events, 0.1 us)
Async XLA Ops:
  3.0 1.5 %collective-permute-start = (f32[40,512]{1,0:T(8,128)S(1)}, f32[40,512]{1,0:T(8,128)S(1)}, u32[]{:S(2)}, u32[]{:S(2)}) collective-permute-start(f32[40,512]{1,0:T(8,128)S(1)} %pad_maximum_fusion), channel_id=1, source_target_pairs={{0,1},{1,0},{2,3},{3,2},{4,5},{5,4},{6,7},{7,6},{8,9},{9,8},{10,11... | collective-permute-start | bytes 245768 | tf_op jit(solution)/shard_map/ppermute | solution.py:39
  4.4 1.2 copy-start
  5.7 1.0 copy-start.2
  6.7 1.2 copy-start.4
  7.9 13.0 %copy-start.1 = (f32[2,256,512]{2,1,0:T(8,128)S(1)}, f32[2,256,512]{2,1,0:T(8,128)}, u32[]{:S(2)}) copy-start(f32[2,256,512]{2,1,0:T(8,128)} %iterate_ref.1) | copy-start | bytes 3145732
  13.7 27.1 %copy-start.10 = (f32[256,512]{1,0:T(8,128)S(1)}, f32[256,512]{1,0:T(8,128)}, u32[]{:S(2)}) copy-start(f32[256,512]{1,0:T(8,128)} %param.10) | copy-start | bytes 1572868
  13.7 29.9 %all-to-all-start = ((f32[8,176,128]{2,1,0:T(8,128)}), f32[8,176,128]{2,1,0:T(8,128)S(1)}, u32[]{:S(2)}, u32[]{:S(2)}) async-start(f32[8,176,128]{2,1,0:T(8,128)} %get-tuple-element.14), calls=%async_computation | async-start | bytes 1441792 | tf_op jit(solution)/shard_map/all_to_all | solution.py:478
  21.8 18.9 %collective-permute-start.1 = (f32[256,512]{1,0:T(8,128)}, f32[256,512]{1,0:T(8,128)}, u32[]{:S(2)}, u32[]{:S(2)}) collective-permute-start(f32[256,512]{1,0:T(8,128)} %slice_bitcast_fusion), channel_id=1, source_target_pairs={{0,2},{2,4},{4,6},{6,8},{8,10},{10,12},{12,14},{1,3},{3,5},{5,7},{... | collective-permute-start | bytes 1572872 | tf_op jit(solution)/shard_map/ppermute | solution.py:27
  40.8 17.4 %copy-start.3 = (f32[256,512]{1,0:T(8,128)S(1)}, f32[256,512]{1,0:T(8,128)}, u32[]{:S(2)}) copy-start(f32[256,512]{1,0:T(8,128)} %diff_ref.1) | copy-start | bytes 1572868
  40.8 1.2 collective-permute-start.2
  42.1 35.0 %copy-start.7 = (f32[128,128]{1,0:T(8,128)S(1)}, f32[128,128]{1,0:T(8,128)}, u32[]{:S(2)}) copy-start(f32[128,128]{1,0:T(8,128)} %constant.45.clone.mix_ref) | copy-start | bytes 196612
  42.7 0.9 copy-start.5
  43.6 33.5 %all-to-all-start.1 = ((f32[8,176,128]{2,1,0:T(8,128)}), f32[8,176,128]{2,1,0:T(8,128)S(1)}, u32[]{:S(2)}, u32[]{:S(2)}) async-start(f32[8,176,128]{2,1,0:T(8,128)} %copy-done.5), calls=%async_computation.1 | async-start | bytes 1441792 | tf_op jit(solution)/shard_map/all_to_all | solution.py:494
  58.0 42.2 %copy-start.6 = (f32[128,128]{1,0:T(8,128)S(1)}, f32[128,128]{1,0:T(8,128)}, u32[]{:S(2)}) copy-start(f32[128,128]{1,0:T(8,128)} %constant.48.clone.mix_ref) | copy-start | bytes 196612
  58.0 42.2 %copy-start.8 = (f32[7,16,128]{2,1,0:T(8,128)S(1)}, f32[7,16,128]{2,1,0:T(8,128)}, u32[]{:S(2)}) copy-start(f32[7,16,128]{2,1,0:T(8,128)} %constant.46.clone.table_ref) | copy-start | bytes 172036
  58.1 42.2 %copy-start.9 = (f32[2,16,128]{2,1,0:T(8,128)S(1)}, f32[2,16,128]{2,1,0:T(8,128)}, u32[]{:S(2)}) copy-start(f32[2,16,128]{2,1,0:T(8,128)} %constant.47.clone.shift_ref) | copy-start | bytes 49156
  87.2 1.2 collective-permute-start.3
  88.4 3.7 %collective-permute-start.4 = (f32[16,128]{1,0:T(8,128)S(1)}, f32[16,128]{1,0:T(8,128)S(1)}, u32[]{:S(2)}, u32[]{:S(2)}) collective-permute-start(f32[16,128]{1,0:T(8,128)S(1)} %add.35), channel_id=1, source_target_pairs={{0,2},{2,0},{4,6},{6,4},{8,10},{10,8},{12,14},{14,12},{1,3},{3,1},... | collective-permute-start | bytes 24584 | tf_op jit(solution)/shard_map/ppermute | solution.py:530
  92.0 3.7 %collective-permute-start.5 = (f32[16,128]{1,0:T(8,128)S(1)}, f32[16,128]{1,0:T(8,128)S(1)}, u32[]{:S(2)}, u32[]{:S(2)}) collective-permute-start(f32[16,128]{1,0:T(8,128)S(1)} %add.36), channel_id=1, source_target_pairs={{0,4},{2,6},{4,0},{6,2},{8,12},{10,14},{12,8},{14,10},{1,5},{3,7},... | collective-permute-start | bytes 24584 | tf_op jit(solution)/shard_map/ppermute | solution.py:530
  95.7 4.5 %collective-permute-start.6 = (f32[16,128]{1,0:T(8,128)S(1)}, f32[16,128]{1,0:T(8,128)S(1)}, u32[]{:S(2)}, u32[]{:S(2)}) collective-permute-start(f32[16,128]{1,0:T(8,128)S(1)} %add.37), channel_id=1, source_target_pairs={{0,8},{2,10},{4,12},{6,14},{8,0},{10,2},{12,4},{14,6},{1,9},{3,11}... | collective-permute-start | bytes 24584 | tf_op jit(solution)/shard_map/ppermute | solution.py:530
  102.9 26.6 %all-to-all-start.2 = ((f32[8,64,512]{2,1,0:T(8,128)}), f32[8,64,512]{2,1,0:T(8,128)S(1)}, u32[]{:S(2)}, u32[]{:S(2)}) async-start(f32[8,64,512]{2,1,0:T(8,128)} %combine.1), calls=%async_computation.2 | async-start | bytes 2097152 | tf_op jit(solution)/shard_map/all_to_all | solution.py:551

commit v4 on v3

--- a/solution.py
+++ b/solution.py
@@ -25,6 +25,14 @@
     count = lax.axis_size(axis)
     initial, last = (max(0, -steps), min(count, count - steps))
     return lax.ppermute(value, axis, [(source, source + steps) for source in range(initial, last)])
+
+
+def exchanged(pieces):
+    count = pieces.shape[0]
+    got = [pieces[0]] + [None] * (count - 1)
+    for k in reversed(range(1, count)):
+        got[k] = lax.ppermute(pieces[k], "tm", [(i, i ^ k) for i in range(count)])
+    return got
 
 
 def border_rows(blocks, axis, width):
@@ -111,121 +119,63 @@
     return np.stack(powers)
 
 
-def flux_terms(here, under_first, east_weight, south_weight, west_weight, north, masks):
-    is_first, is_last, is_top, is_bottom = masks
-    tiles = len(here)
-    south = []
-    for t in range(tiles):
-        under = jnp.where(
-            is_bottom, pltpu.roll(under_first[t], 7, 0), pltpu.roll(here[t], 7, 0)
-        )
-        south.append(south_weight[t] * (under - here[t]))
-    turned = [pltpu.roll(v, 127, 1) for v in here] + [0.0]
-    east = [
-        east_weight[t] * (jnp.where(is_last, turned[t + 1], turned[t]) - here[t])
-        for t in range(tiles)
-    ]
-    moved = [west_weight * here[0]] + [pltpu.roll(f, 1, 1) for f in east]
-    value = []
-    for t in range(tiles):
-        from_north = jnp.where(is_top, pltpu.roll(north[t], 1, 0), pltpu.roll(south[t], 1, 0))
-        value.append(
-            (jnp.where(is_first, moved[t], moved[t + 1]) - east[t]) + (from_north - south[t])
-        )
-    return value, south
-
-
-def pack(out_ref, at, source_ref, slab, halo):
+def face_weights(padded_rows):
+    centre = padded_rows[1:-1]
+    columns = jnp.pad(centre, ((0, 0), (1, 1)), mode="edge")
+    return (
+        0.5 * (centre + padded_rows[:-2]),
+        0.5 * (centre + padded_rows[2:]),
+        0.5 * (centre + columns[:, :-2]),
+        0.5 * (centre + columns[:, 2:]),
+    )
+
+
+def apply_faces(padded_rows, weights):
+    north, south, west, east = weights
+    centre = padded_rows[..., 1:-1, :]
+    columns = jnp.pad(centre, [(0, 0)] * (centre.ndim - 1) + [(1, 1)])
+    return (
+        (north + south + west + east) * centre
+        - north * padded_rows[..., :-2, :]
+        - south * padded_rows[..., 2:, :]
+        - west * columns[..., :-2]
+        - east * columns[..., 2:]
+    )
+
+
+def borders_body(rank_ref, iterate_ref, forcing_ref, diff_ref, mine_ref, last_ref, done):
+    steps, rows_dev, _ = iterate_ref.shape
+    start = pl.multiple_of(jnp.where(rank_ref[0] == 0, rows_dev - PAD, 0), 8)
+    copies = []
+    for s in range(steps):
+        copies.append((iterate_ref.at[s, pl.ds(start, PAD)], mine_ref.at[pl.ds(PAD * s, PAD)]))
+        at = PAD * (steps + s)
+        copies.append((forcing_ref.at[s, pl.ds(start, PAD)], mine_ref.at[pl.ds(at, PAD)]))
+    copies.append((diff_ref.at[pl.ds(start, PAD)], mine_ref.at[pl.ds(2 * PAD * steps, PAD)]))
+    copies.append((iterate_ref.at[steps - 1], last_ref))
+    started = []
+    for index, (source, target) in enumerate(copies):
+        started.append(pltpu.make_async_copy(source, target, done.at[index]))
+        started[-1].start()
+    for copy in started:
+        copy.wait()
+
+
+def pack(out_ref, at, source_ref, slab, halo, flip=0):
     rows = slab + 2 * halo
     for target in range(out_ref.shape[0]):
         first = slab * target + PAD - halo
         for t in range(source_ref.shape[-1] // 128):
-            out_ref[target, at + rows * t : at + rows * (t + 1), :] = source_ref[
+            out_ref[target ^ flip, at + rows * t : at + rows * (t + 1), :] = source_ref[
                 first : first + rows, 128 * t : 128 * (t + 1)
             ]
 
 
-def residual_body(slab, halo, rank_ref, iterate_ref, forcing_ref, diff_ref, low_ref, high_ref,
-                  pieces_ref, partial_ref, squares_ref, *scratch):
-    steps, rows_dev, columns = iterate_ref.shape
-    tiles = columns // 128
-    blocks = rows_dev // 8 + 2
-    lane8 = lax.broadcasted_iota(jnp.int32, (8, 128), 1)
-    sub8 = lax.broadcasted_iota(jnp.int32, (8, 128), 0)
-    masks = (lane8 == 0, lane8 == 127, sub8 == 0, sub8 == 7)
-    is_low_edge = rank_ref[0] == 0
-    is_high_edge = rank_ref[0] == rank_ref[1] - 1
-    keep_low = jnp.where(is_low_edge, 0.0, 1.0)
-    keep_high = jnp.where(is_high_edge, 0.0, 1.0)
-
-    def cut(ref, at, lead=()):
-        return [ref[lead + (slice(at, at + 8), slice(128 * t, 128 * t + 128))] for t in range(tiles)]
-
-    def block_of(ref, step, slot, b):
-        if b == 0:
-            return [v * keep_low for v in cut(low_ref, 8 * slot)]
-        if b == blocks - 1:
-            return [v * keep_high for v in cut(high_ref, 8 * slot)]
-        return cut(ref, 8 * (b - 1), (step,))
-
-    def diff_of(b):
-        if b == 0:
-            mine = [
-                jnp.broadcast_to(diff_ref[0:1, 128 * t : 128 * t + 128], (8, 128))
-                for t in range(tiles)
-            ]
-            got = cut(low_ref, 16 * steps)
-            return [jnp.where(is_low_edge, m, g) for m, g in zip(mine, got)]
-        if b == blocks - 1:
-            mine = [
-                jnp.broadcast_to(diff_ref[rows_dev - 1 :, 128 * t : 128 * t + 128], (8, 128))
-                for t in range(tiles)
-            ]
-            got = cut(high_ref, 16 * steps)
-            return [jnp.where(is_high_edge, m, g) for m, g in zip(mine, got)]
-        return cut(diff_ref, 8 * (b - 1))
-
-    quarter = 0.5 * time_step
-    zeros = [jnp.zeros((8, 128), jnp.float32)] * tiles
-    diff = diff_of(0)
-    here = [block_of(iterate_ref, s, s, 0) for s in range(steps)]
-    north = [zeros] * steps
-    squares = [jnp.zeros((8, 128), jnp.float32)] * steps
-    for b in range(blocks):
-        last = b + 1 == blocks
-        diff_next = diff if last else diff_of(b + 1)
-        next_here = here if last else [block_of(iterate_ref, s, s, b + 1) for s in range(steps)]
-        below = [
-            jnp.where(masks[3], pltpu.roll(diff_next[t], 7, 0), pltpu.roll(diff[t], 7, 0))
-            for t in range(tiles)
-        ]
-        turned = [pltpu.roll(v, 127, 1) for v in diff] + [diff[-1]]
-        after = [jnp.where(masks[1], turned[t + 1], turned[t]) for t in range(tiles)]
-        south_weight = [quarter * (diff[t] + below[t]) for t in range(tiles)]
-        east_weight = [quarter * (diff[t] + after[t]) for t in range(tiles)]
-        west_weight = (2.0 * quarter) * diff[0]
-        for s in range(steps):
-            value, north[s] = flux_terms(
-                here[s], next_here[s], east_weight, south_weight, west_weight, north[s], masks
-            )
-            force = block_of(forcing_ref, s, steps + s, b)
-            for t in range(tiles):
-                left = time_step * force[t] - here[s][t] - value[t]
-                if b == 0:
-                    left = left * keep_low
-                elif last:
-                    left = left * keep_high
-                if s == 0:
-                    partial_ref[8 * b : 8 * b + 8, 128 * t : 128 * t + 128] = left
-                else:
-                    left = left + here[s - 1][t]
-                    scratch[s - 1][8 * b : 8 * b + 8, 128 * t : 128 * t + 128] = left
-                    if 0 < b < blocks - 1:
-                        squares[s] = squares[s] + left * left
-        diff, here = diff_next, next_here
+def later_steps_body(slab, halo, rank_ref, wide_ref, pieces_ref):
+    steps, _, columns = wide_ref.shape
     for s in range(1, steps):
-        squares_ref[s - 1] = squares[s]
-        pack(pieces_ref, (s - 1) * tiles * (slab + 2 * halo), scratch[s - 1], slab, halo)
+        at = (s - 1) * (columns // 128) * (slab + 2 * halo)
+        pack(pieces_ref, at, wide_ref.at[s], slab, halo, rank_ref[2])
 
 
 def first_step_body(slab, halo, rank_ref, partial_ref, previous_ref, low_ref, high_ref,
@@ -233,11 +183,11 @@
     rows_dev, columns = previous_ref.shape
     keep_low = jnp.where(rank_ref[0] == 0, 0.0, 1.0)
     keep_high = jnp.where(rank_ref[0] == rank_ref[1] - 1, 0.0, 1.0)
-    whole_ref[:PAD, :] = partial_ref[:PAD, :] + keep_low * low_ref[...]
-    whole_ref[PAD + rows_dev :, :] = partial_ref[PAD + rows_dev :, :] + keep_high * high_ref[...]
+    whole_ref[:PAD, :] = partial_ref[0, :PAD, :] + keep_low * low_ref[...]
+    whole_ref[PAD + rows_dev :, :] = partial_ref[0, PAD + rows_dev :, :] + keep_high * high_ref[...]
     squares = jnp.zeros((8, columns), jnp.float32)
     for at in range(0, rows_dev, 8):
-        value = partial_ref[PAD + at : PAD + at + 8, :] + previous_ref[at : at + 8, :]
+        value = partial_ref[0, PAD + at : PAD + at + 8, :] + previous_ref[at : at + 8, :]
         whole_ref[PAD + at : PAD + at + 8, :] = value
         squares = squares + value * value
     total = squares[:, :128]
@@ -247,15 +197,8 @@
     pack(pieces_ref, 0, whole_ref, slab, halo)
 
 
-def krylov_body(length, slab, halo, place_ref, early_ref, late_ref, diff_ref, mix_ref, *rest):
-    vectors = rest[:DEPTH]
-    moments_ref, south_ref, east_ref, west_ref = rest[DEPTH:]
-    rows = slab + 2 * halo
-    columns = diff_ref.shape[-1]
-    groups = length // 8
-    tiles = columns // 128
-    steps_dev = early_ref.shape[1] // (rows * tiles) + 1
-
+def put_weights(diff_ref, south_ref, east_ref, west_ref):
+    rows, columns = diff_ref.shape
     centre = diff_ref[...]
     below = jnp.concatenate([centre[1:], centre[-1:]], axis=0)
     lane = lax.broadcasted_iota(jnp.int32, (rows, columns), 1)
@@ -268,29 +211,46 @@
         south_ref[8 * r : 8 * r + 8, :] = jnp.broadcast_to(south[r : r + 1], (8, columns))
         east_ref[8 * r : 8 * r + 8, :] = jnp.broadcast_to(east[r : r + 1], (8, columns))
         west_ref[8 * r : 8 * r + 8, :] = jnp.broadcast_to(west[r : r + 1], (8, 128))
-    first_row = place_ref[0] + halo == 0
-    last_row = place_ref[0] + halo + slab == place_ref[1]
-    keep_above = jnp.where(first_row, 0.0, 1.0)
-    keep_below = jnp.where(last_row, 0.0, 1.0)
-
-    mix = mix_ref[...]
+
+
+def transform(target, early_ref, late_ref, mix, rows, length, tiles):
+    sources = early_ref.shape[0]
+    steps_dev = length // sources
     starts = list(range(0, rows - 7, 8))
     if starts[-1] + 8 < rows:
         starts.append(rows - 8)
     for start in starts:
         for t in range(tiles):
             cells = []
-            for source in range(length // steps_dev):
+            for source in range(sources):
                 for step in range(steps_dev):
                     ref = late_ref if step == 0 else early_ref
                     at = (max(step - 1, 0) * tiles + t) * rows + start
                     cells.append(ref[source, at : at + 8, :])
-            vectors[0][start * length : (start + 8) * length, 128 * t : 128 * t + 128] = jnp.dot(
+            target[start * length : (start + 8) * length, 128 * t : 128 * t + 128] = jnp.dot(
                 mix,
                 jnp.concatenate(cells, axis=0),
                 precision=lax.Precision.HIGHEST,
                 preferred_element_type=jnp.float32,
             )
+
+
+def krylov_body(length, slab, halo, sources, place_ref, late_ref, diff_ref, mix_ref, *rest):
+    pieces = rest[:sources]
+    vectors = rest[sources : sources + DEPTH]
+    moments_ref, early_ref, south_ref, east_ref, west_ref = rest[sources + DEPTH :]
+    rows = slab + 2 * halo
+    columns = diff_ref.shape[-1]
+    groups = length // 8
+    tiles = columns // 128
+    first_row = place_ref[0] + halo == 0
+    last_row = place_ref[0] + halo + slab == place_ref[1]
+    keep_above = jnp.where(first_row, 0.0, 1.0)
+    keep_below = jnp.where(last_row, 0.0, 1.0)
+    put_weights(diff_ref, south_ref, east_ref, west_ref)
+    for index, piece in enumerate(pieces):
+        early_ref[index ^ place_ref[2]] = piece[...]
+    transform(vectors[0], early_ref, late_ref, mix_ref[...], rows, length, tiles)
 
     lane8 = lax.broadcasted_iota(jnp.int32, (8, 128), 1)
     is_first = lane8 == 0
@@ -455,27 +415,63 @@
     vmem = pl.BlockSpec(memory_space=pltpu.VMEM)
     smem = pl.BlockSpec(memory_space=pltpu.SMEM)
     params = pltpu.CompilerParams(vmem_limit_bytes=24 * 2**20)
-    rank = jnp.stack([row_rank, jnp.int32(row_devices)]).astype(jnp.int32)
-
-    arriving = from_behind(iterate[-1], "tm", 1)
-    low, high = border_rows((iterate, forcing, diffusivity), "rows", PAD)
+    rank = jnp.stack([row_rank, jnp.int32(row_devices), time_rank]).astype(jnp.int32)
+
+    if row_devices == 2:
+        mine, last = pl.pallas_call(
+            borders_body,
+            out_shape=[
+                pltpu.VMEM(((2 * steps_dev + 1) * PAD, columns_dev), jnp.float32),
+                pltpu.VMEM((rows_dev, columns_dev), jnp.float32),
+            ],
+            in_specs=[smem] + [pl.BlockSpec(memory_space=pltpu.HBM)] * 3,
+            out_specs=[vmem] * 2,
+            scratch_shapes=[pltpu.SemaphoreType.DMA((2 * steps_dev + 2,))],
+            compiler_params=pltpu.CompilerParams(vmem_limit_bytes=2**26 - 3 * 2**18),
+            name="borders",
+        )(rank, iterate, forcing, diffusivity)
+        low = high = lax.ppermute(mine, "rows", [(0, 1), (1, 0)])
+    else:
+        last = iterate[-1]
+        low, high = border_rows((iterate, forcing, diffusivity), "rows", PAD)
+    arriving = from_behind(last, "tm", 1)
+
+    keep_low = jnp.where(row_rank == 0, 0.0, 1.0)
+    keep_high = jnp.where(row_rank == row_devices - 1, 0.0, 1.0)
+
+    def widened(block, slot):
+        shape = (steps_dev, PAD, columns_dev)
+        at = slice(slot * PAD, (slot + steps_dev) * PAD)
+        return jnp.concatenate(
+            [keep_low * low[at].reshape(shape), block, keep_high * high[at].reshape(shape)], axis=1
+        )
+
+    diff_low = jnp.where(row_rank == 0, diffusivity[:1], low[-PAD:])
+    diff_high = jnp.where(row_rank == row_devices - 1, diffusivity[-1:], high[-PAD:])
+    rimmed = jnp.concatenate([diff_low, diffusivity, diff_high])
+    wide_iterate = widened(iterate, 0)
+    faces = face_weights(jnp.pad(rimmed, ((1, 1), (0, 0)), mode="edge"))
+    wide_rows = jnp.pad(wide_iterate, ((0, 0), (1, 1), (0, 0)))
+    wide = time_step * (widened(forcing, steps_dev) - apply_faces(wide_rows, faces)) - wide_iterate
+    wide = wide + jnp.concatenate([jnp.zeros_like(wide_iterate[:1]), wide_iterate[:-1]])
+    at_row = lax.broadcasted_iota(jnp.int32, (1, rows_dev + 2 * PAD, 1), 1)
+    keep = jnp.where(at_row < PAD, keep_low, jnp.where(at_row < PAD + rows_dev, 1.0, keep_high))
+    wide = wide * keep
+    own = wide[1:, PAD : PAD + rows_dev]
+    squares_late = jnp.sum(own * own, axis=(1, 2))
+
     padded = rows_dev + 2 * PAD
-    early, partial, squares_late = pl.pallas_call(
-        functools.partial(residual_body, slab, halo),
-        out_shape=[
-            jax.ShapeDtypeStruct(
-                (time_devices, (steps_dev - 1) * tiles * rows, 128), jnp.float32
-            ),
-            pltpu.VMEM((padded, columns_dev), jnp.float32),
-            jax.ShapeDtypeStruct((steps_dev - 1, 8, 128), jnp.float32),
-        ],
-        in_specs=[smem] + [vmem] * 5,
-        out_specs=[vmem] * 3,
-        scratch_shapes=[pltpu.VMEM((padded, columns_dev), jnp.float32)] * (steps_dev - 1),
+    early = pl.pallas_call(
+        functools.partial(later_steps_body, slab, halo),
+        out_shape=jax.ShapeDtypeStruct(
+            (time_devices, (steps_dev - 1) * tiles * rows, 128), jnp.float32
+        ),
+        in_specs=[smem, vmem],
+        out_specs=vmem,
         compiler_params=params,
-        name="residual",
-    )(rank, iterate, forcing, diffusivity, low, high)
-    early = lax.all_to_all(early, "tm", split_axis=0, concat_axis=0, tiled=True)
+        name="later_steps",
+    )(rank, wide)
+    early = exchanged(early)
 
     previous = jnp.where(time_rank == 0, initial_state, arriving)
     before_low, before_high = border_rows((previous,), "rows", PAD)
@@ -490,34 +486,36 @@
         scratch_shapes=[pltpu.VMEM((padded, columns_dev), jnp.float32)],
         compiler_params=params,
         name="first_step",
-    )(rank, partial, previous, before_low, before_high)
+    )(rank, wide, previous, before_low, before_high)
     late = lax.all_to_all(late, "tm", split_axis=0, concat_axis=0, tiled=True)
 
-    squares = jnp.sum(jnp.concatenate([squares_first, squares_late]), axis=(1, 2))
+    squares = jnp.concatenate([jnp.sum(squares_first, axis=(1, 2)), squares_late])
     residual_rms = jnp.sqrt(lax.psum(squares, "rows") / cell_count + rms_eps)
 
-    diff_low = jnp.where(row_rank == 0, diffusivity[:1], low[-PAD:])
-    diff_high = jnp.where(row_rank == row_devices - 1, diffusivity[-1:], high[-PAD:])
-    rimmed = jnp.concatenate([diff_low, diffusivity, diff_high])
     diff_slab = lax.dynamic_slice_in_dim(rimmed, slab * time_rank + PAD - halo, rows, axis=0)
     place = jnp.stack(
-        [row_rank * rows_dev + time_rank * slab - halo, jnp.int32(rows_dev * row_devices)]
+        [
+            row_rank * rows_dev + time_rank * slab - halo,
+            jnp.int32(rows_dev * row_devices),
+            time_rank,
+        ]
     ).astype(jnp.int32)
 
     vector = pltpu.VMEM((rows * length, columns_dev), jnp.float32)
     *powers, moments = pl.pallas_call(
-        functools.partial(krylov_body, length, slab, halo),
+        functools.partial(krylov_body, length, slab, halo, time_devices),
         out_shape=[vector] * DEPTH + [jax.ShapeDtypeStruct((length, 128), jnp.float32)],
-        in_specs=[smem] + [vmem] * 4,
+        in_specs=[smem] + [vmem] * (3 + time_devices),
         out_specs=[vmem] * (DEPTH + 1),
         scratch_shapes=[
+            pltpu.VMEM((time_devices, (steps_dev - 1) * tiles * rows, 128), jnp.float32),
             pltpu.VMEM((rows * 8, columns_dev), jnp.float32),
             pltpu.VMEM((rows * 8, columns_dev), jnp.float32),
             pltpu.VMEM((rows * 8, 128), jnp.float32),
         ],
         compiler_params=params,
         name="krylov",
-    )(place, early, late, diff_slab, jnp.asarray(block_forward(length, 8)))
+    )(place, late, diff_slab, jnp.asarray(block_forward(length, 8)), *early)
 
     for axis in ("rows", "tm"):
         count = lax.axis_size(axis)

time: 131 us -> 120 us (0.916)
  waiting for transfers between devices: 66.2 us -> 48.3 us
  starting transfers between devices: 32.6 us -> 40 us
  other arithmetic: 4.42 us -> 8.04 us
  Pallas kernels: 19.1 us -> 16.7 us
  local copies, waits for them, and re-layouts: 5.31 us -> 3.01 us
    ppermute x0 -> x8, starting transfers between devices: none -> 22.4 us  [the longest x7 21.9 us: exchanged(): got[k] = lax.ppermute(pieces[k], 'tm', [(i, i ^ k) for i in range(count)])]
    all_to_all x1, waiting for transfers between devices: 18.9 us -> 0.01 us  [iteration(): late = lax.all_to_all(late, 'tm', split_axis=0, concat_axis=0, tiled=True)]
    ppermute x0 -> x8, waiting for transfers between devices: none -> 12.5 us  [the longest x7 12.5 us: exchanged(): got[k] = lax.ppermute(pieces[k], 'tm', [(i, i ^ k) for i in range(count)])]
    all_to_all x1, starting transfers between devices: 14.4 us -> 6.8 us  [iteration(): late = lax.all_to_all(late, 'tm', split_axis=0, concat_axis=0, tiled=True)]
    all_to_all x1 -> x0, starting transfers between devices: 7.3 us -> none  [iteration(): early = lax.all_to_all(early, 'tm', split_axis=0, concat_axis=0, tiled=True)]
    ppermute x1, waiting for transfers between devices: 14.2 us -> 7.84 us  [from_behind(): lax.ppermute(value, axis, [(source, source + steps) for source in range(i...]
    unnamed x22 -> x24, local copies, waits for them, and re-layouts: 4.38 us -> 1.11 us
    pallas_call x2 -> x3, Pallas kernels: 15.8 us -> 12.6 us  [the longest x1 10.1 us: iteration(): pl.pallas_call(functools.partial(krylov_body, length, slab, halo, time_de...]
  transfers between devices with their start and end apart: 10 -> 16, of which waited for: 9 -> 11; matrix products, arithmetic and copies ran while one was open for 1% -> 7% of each run, Pallas kernels for 0% -> 0%
where the time goes in v4:
time: 120 us; the launch traced here: 119 us
  waiting for transfers between devices  48.3 us (40%)
  starting transfers between devices  40 us (33%)
  Pallas kernels  16.7 us (14%)
  other arithmetic  8.04 us (7%)
  local copies, waits for them, and re-layouts  3.01 us (3%)
  blocking collectives  2.45 us (2%)
    ppermute x7, starting transfers between devices, exchanged(): got[k] = lax.ppermute(pieces[k], 'tm', [(i, i ^ k) for i in range(count)])  21.9 us
    all_to_all x1, waiting for transfers between devices, iteration(): lax.all_to_all(corrected, 'tm', split_axis=0, concat_axis=0, tiled=True)  17.3 us
    ppermute x7, waiting for transfers between devices, exchanged(): got[k] = lax.ppermute(pieces[k], 'tm', [(i, i ^ k) for i in range(count)])  12.5 us
    ppermute x4, waiting for transfers between devices, iteration(): moments = moments + lax.ppermute(moments, axis, pairs)  10.6 us
    pallas_call x1, Pallas kernels, iteration(): pl.pallas_call(functools.partial(krylov_body, length, slab, halo, time_de...  10.1 us
    ppermute x1, waiting for transfers between devices, from_behind(): lax.ppermute(value, axis, [(source, source + steps) for source in range(i...  7.84 us
    all_to_all x1, starting transfers between devices, iteration(): late = lax.all_to_all(late, 'tm', split_axis=0, concat_axis=0, tiled=True)  6.8 us
    ppermute x1, starting transfers between devices, from_behind(): lax.ppermute(value, axis, [(source, source + steps) for source in range(i...  4.45 us
  transfers between devices with their start and end apart: 16, of which 11 were waited for; matrix products, arithmetic and copies ran while one was open for 7% of the time, Pallas kernels for 0%

profile of v4, /device:TPU:0, one launch (start us, length us, event | category | flops | bytes accessed | tf_op | source)
XLA Modules:
  0.0 119.4 jit_solution(5326226273090903688)
XLA Ops:
  0.6 0.6 add_add_fusion.2.rank_ref
  1.2 1.8 %borders.1 = (f32[40,512]{1,0:T(8,128)S(1)}, f32[256,512]{1,0:T(8,128)S(1)}) custom-call(s32[3]{0:T(128)} %add_add_fusion.2.rank_ref, f32[2,256,512]{2,1,0:T(8,128)} %iterate_ref.1, f32[2,256,512]{2,1,0:T(8,128)} %forcing_ref.1, f32[256,512]{1,0:T(8,128)} %diff_ref.1), custom_call_target="tpu_custom_call" | custom-call | tf_op jit(solution)/shard_map/borders/pallas_call | solution.py:421
  3.1 0.6 collective-permute-start
  3.6 4.5 %collective-permute-start.1 = (f32[256,512]{1,0:T(8,128)S(1)}, f32[256,512]{1,0:T(8,128)S(1)}, u32[]{:S(2)}, u32[]{:S(2)}) collective-permute-start(f32[256,512]{1,0:T(8,128)S(1)} %get-tuple-element.14), channel_id=1, source_target_pairs={{0,2},{2,4},{4,6},{6,8},{8,10},{10,12},{12,14},{1,3},{3,5},{5,7},{... | collective-permute-start | bytes 1572872 | tf_op jit(solution)/shard_map/ppermute | solution.py:27
  8.1 0.7 fusion.23
  8.9 1.4 %pad_maximum_fusion = f32[2,272,512]{2,1,0:T(8,128)S(1)} fusion(f32[2,8,512]{2,1,0:T(8,128)S(1)} %get-tuple-element.45, f32[2,256,512]{2,1,0:T(8,128)} %iterate_ref.1, f32[2,8,512]{2,1,0:T(8,128)S(1)} %get-tuple-element.46), kind=kLoop, calls=%fused_computation.11 | loop fusion | flops 557056 | bytes 2228224 | tf_op jit(solution)/shard_map/concatenate | solution.py:445
  10.4 0.1 fusion.22
  10.5 0.8 copy-done.6
  11.3 0.2 copy-done.10
  11.5 0.5 add_add_fusion
  12.0 7.8 %collective-permute-done.1 = f32[256,512]{1,0:T(8,128)S(1)} collective-permute-done((f32[256,512]{1,0:T(8,128)S(1)}, f32[256,512]{1,0:T(8,128)S(1)}, u32[]{:S(2)}, u32[]{:S(2)}) %collective-permute-start.1) | collective-permute-done | bytes 524320 | tf_op jit(solution)/shard_map/ppermute | solution.py:27
  19.9 0.1 broadcast_select_fusion.previous_ref
  20.0 0.1 collective-permute-start.2
  20.1 1.1 fusion.7.partial_ref.wide_ref
  21.2 1.5 %first_step.1 = (f32[8,176,128]{2,1,0:T(8,128)}, f32[1,8,128]{2,1,0:T(8,128)S(1)}) custom-call(s32[3]{0:T(128)S(1)} %copy-done.4, f32[2,272,512]{2,1,0:T(8,128)S(1)} %fusion.7.partial_ref.wide_ref, f32[256,512]{1,0:T(8,128)S(1)} %broadcast_select_fusion.previous_ref, f32[8,512]{1,0:T(8,128)S(1)} %collective-permute-done.2.low_ref.high_ref, ...), custom_call_target="tpu_custom_call" | custom-call | tf_op jit(solution)/shard_map/first_step/pallas_call | solution.py:478
  22.8 6.8 %all-to-all-start = ((f32[8,176,128]{2,1,0:T(8,128)}), f32[8,176,128]{2,1,0:T(8,128)S(1)}, u32[]{:S(2)}, u32[]{:S(2)}) async-start(f32[8,176,128]{2,1,0:T(8,128)} %get-tuple-element.15), calls=%async_computation | async-start | bytes 1441792 | tf_op jit(solution)/shard_map/all_to_all | solution.py:490
  29.6 0.6 later_steps.1
  30.3 4.8 %collective-permute-start.9 = (f32[176,128]{1,0:T(8,128)S(1)}, f32[176,128]{1,0:T(8,128)S(1)}, u32[]{:S(2)}, u32[]{:S(2)}) collective-permute-start(f32[176,128]{1,0:T(8,128)S(1)} %get-tuple-element.29), channel_id=1, source_target_pairs={{0,14},{2,12},{4,10},{6,8},{8,6},{10,4},{12,2},{14,0},{1,15},{3,13... | collective-permute-start | bytes 270344 | tf_op jit(solution)/shard_map/ppermute | solution.py:34
  35.1 0.6 collective-permute-start.8
  35.6 0.1 add_add_fusion.1.place_ref
  35.7 0.6 collective-permute-start.7
  36.3 1.9 %collective-permute-start.6 = (f32[176,128]{1,0:T(8,128)S(1)}, f32[176,128]{1,0:T(8,128)S(1)}, u32[]{:S(2)}, u32[]{:S(2)}) collective-permute-start(f32[176,128]{1,0:T(8,128)S(1)} %get-tuple-element.32), channel_id=1, source_target_pairs={{0,8},{2,10},{4,12},{6,14},{8,0},{10,2},{12,4},{14,6},{1,9},{3,11}... | collective-permute-start | bytes 270344 | tf_op jit(solution)/shard_map/ppermute | solution.py:34
  38.1 2.3 %collective-permute-start.5 = (f32[176,128]{1,0:T(8,128)S(1)}, f32[176,128]{1,0:T(8,128)S(1)}, u32[]{:S(2)}, u32[]{:S(2)}) collective-permute-start(f32[176,128]{1,0:T(8,128)S(1)} %get-tuple-element.33), channel_id=1, source_target_pairs={{0,6},{2,4},{4,2},{6,0},{8,14},{10,12},{12,10},{14,8},{1,7},{3,5},... | collective-permute-start | bytes 270344 | tf_op jit(solution)/shard_map/ppermute | solution.py:34
  40.4 9.2 %collective-permute-done.9.rest_7_ = f32[176,128]{1,0:T(8,128)S(1)} collective-permute-done((f32[176,128]{1,0:T(8,128)S(1)}, f32[176,128]{1,0:T(8,128)S(1)}, u32[]{:S(2)}, u32[]{:S(2)}) %collective-permute-start.9) | collective-permute-done | bytes 90144 | tf_op jit(solution)/shard_map/ppermute | solution.py:34
  49.6 11.2 %collective-permute-start.4 = (f32[176,128]{1,0:T(8,128)S(1)}, f32[176,128]{1,0:T(8,128)S(1)}, u32[]{:S(2)}, u32[]{:S(2)}) collective-permute-start(f32[176,128]{1,0:T(8,128)S(1)} %get-tuple-element.34), channel_id=1, source_target_pairs={{0,4},{2,6},{4,0},{6,2},{8,12},{10,14},{12,8},{14,10},{1,5},{3,7},... | collective-permute-start | bytes 270344 | tf_op jit(solution)/shard_map/ppermute | solution.py:34
  60.8 0.6 collective-permute-start.3
  61.4 0.9 constant_dynamic-slice_fusion.diff_ref
  62.3 1.9 %collective-permute-done.7.rest_5_ = f32[176,128]{1,0:T(8,128)S(1)} collective-permute-done((f32[176,128]{1,0:T(8,128)S(1)}, f32[176,128]{1,0:T(8,128)S(1)}, u32[]{:S(2)}, u32[]{:S(2)}) %collective-permute-start.7) | collective-permute-done | bytes 90144 | tf_op jit(solution)/shard_map/ppermute | solution.py:34
  64.2 0.3 collective-permute-done.6.rest_4_
  64.4 1.2 %collective-permute-done.4.rest_2_ = f32[176,128]{1,0:T(8,128)S(1)} collective-permute-done((f32[176,128]{1,0:T(8,128)S(1)}, f32[176,128]{1,0:T(8,128)S(1)}, u32[]{:S(2)}, u32[]{:S(2)}) %collective-permute-start.4) | collective-permute-done | bytes 90144 | tf_op jit(solution)/shard_map/ppermute | solution.py:34
  65.7 10.1 %krylov.1 = (f32[704,512]{1,0:T(8,128)S(1)}, f32[704,512]{1,0:T(8,128)S(1)}, f32[704,512]{1,0:T(8,128)S(1)}, f32[704,512]{1,0:T(8,128)S(1)}, f32[704,512]{1,0:T(...) custom-call(s32[3]{0:T(128)S(1)} %add_add_fusion.1.place_ref, f32[8,176,128]{2,1,0:T(8,128)S(1)} %all-to-all-done.late_ref, ...), custom_call_target="tpu_custom_call" | custom-call | tf_op jit(solution)/shard_map/krylov/pallas_call | solution.py:505
  75.8 1.2 collective-permute-done.10
  77.0 1.1 collective-permute-start.11
  78.1 2.6 %collective-permute-done.11 = f32[16,128]{1,0:T(8,128)S(1)} collective-permute-done((f32[16,128]{1,0:T(8,128)S(1)}, f32[16,128]{1,0:T(8,128)S(1)}, u32[]{:S(2)}, u32[]{:S(2)}) %collective-permute-start.11) | collective-permute-done | bytes 8224 | tf_op jit(solution)/shard_map/ppermute | solution.py:528
  80.7 0.7 collective-permute-start.12
  81.4 2.9 %collective-permute-done.12 = f32[16,128]{1,0:T(8,128)S(1)} collective-permute-done((f32[16,128]{1,0:T(8,128)S(1)}, f32[16,128]{1,0:T(8,128)S(1)}, u32[]{:S(2)}, u32[]{:S(2)}) %collective-permute-start.12) | collective-permute-done | bytes 8224 | tf_op jit(solution)/shard_map/ppermute | solution.py:528
  84.3 0.6 collective-permute-start.13
  84.9 3.9 %collective-permute-done.13 = f32[16,128]{1,0:T(8,128)S(1)} collective-permute-done((f32[16,128]{1,0:T(8,128)S(1)}, f32[16,128]{1,0:T(8,128)S(1)}, u32[]{:S(2)}, u32[]{:S(2)}) %collective-permute-start.13) | collective-permute-done | bytes 8224 | tf_op jit(solution)/shard_map/ppermute | solution.py:528
  88.9 2.6 %combine.1 = f32[8,64,512]{2,1,0:T(8,128)} custom-call(f32[16,128]{1,0:T(8,128)S(1)} %add.76.moments_ref, f32[7,16,128]{2,1,0:T(8,128)S(1)} %copy-done.2, f32[2,16,128]{2,1,0:T(8,128)S(1)} %copy-done.3, f32[128,128]{1,0:T(8,128)S(1)} %copy-done, f32[704,512]{1,0:T(8,128)S(1)} %get-tuple-element.17.rest_0_, f32[704,512]{1,0:T(8,128)S(1)} %get-tuple-element.18.rest_1_, ...), custom_call_target="tpu_custom_call" | custom-call | tf_op jit(solution)/shard_map/combine/pallas_call | solution.py:535
  91.5 3.8 %all-to-all-start.1 = ((f32[8,64,512]{2,1,0:T(8,128)}), f32[8,64,512]{2,1,0:T(8,128)S(1)}, u32[]{:S(2)}, u32[]{:S(2)}) async-start(f32[8,64,512]{2,1,0:T(8,128)} %combine.1), calls=%async_computation.1 | async-start | bytes 2097152 | tf_op jit(solution)/shard_map/all_to_all | solution.py:549
  95.3 0.7 fusion.17
  96.0 0.6 reduce_sum.22
  96.6 1.3 %pad_maximum_fusion.14 = f32[2]{0:T(128)S(1)} fusion(f32[1]{0:T(128)} %bitcast.21, f32[1]{0:T(128)} %bitcast.20), kind=kLoop, calls=%fused_computation.58 | loop fusion | flops 2 | bytes 16 | tf_op jit(solution)/shard_map/concatenate | solution.py:492
  97.9 2.4 %psum.7 = f32[2]{0:T(128)S(1)} all-reduce(f32[2]{0:T(128)S(1)} %pad_maximum_fusion.14), channel_id=1, replica_groups=mesh['groups'=2,'tm'=8,'rows'=2] {'rows'}, use_global_device_ids=true, to_apply=%region_2.3 | all-reduce | flops 2 | bytes 16 | tf_op jit(solution)/shard_map/psum | solution.py:493
  100.3 0.5 add_sqrt_fusion
  100.9 17.3 %all-to-all-done.1 = f32[8,64,512]{2,1,0:T(8,128)S(1)} async-done(((f32[8,64,512]{2,1,0:T(8,128)}), f32[8,64,512]{2,1,0:T(8,128)S(1)}, u32[]{:S(2)}, u32[]{:S(2)}) %all-to-all-start.1) | async-done | bytes 1048608 | tf_op jit(solution)/shard_map/all_to_all | solution.py:549
  118.2 0.1 copy.10
  118.3 1.2 bitcast_add_fusion
  (43 shorter events, 0.3 us)
Async XLA Ops:
  3.1 5.8 %collective-permute-start = (f32[40,512]{1,0:T(8,128)S(1)}, f32[40,512]{1,0:T(8,128)S(1)}, u32[]{:S(2)}, u32[]{:S(2)}) collective-permute-start(f32[40,512]{1,0:T(8,128)S(1)} %get-tuple-element.13), channel_id=1, source_target_pairs={{0,1},{1,0},{2,3},{3,2},{4,5},{5,4},{6,7},{7,6},{8,9},{9,8},{10,11... | collective-permute-start | bytes 245768 | tf_op jit(solution)/shard_map/ppermute | solution.py:433
  3.6 16.2 %collective-permute-start.1 = (f32[256,512]{1,0:T(8,128)S(1)}, f32[256,512]{1,0:T(8,128)S(1)}, u32[]{:S(2)}, u32[]{:S(2)}) collective-permute-start(f32[256,512]{1,0:T(8,128)S(1)} %get-tuple-element.14), channel_id=1, source_target_pairs={{0,2},{2,4},{4,6},{6,8},{8,10},{10,12},{12,14},{1,3},{3,5},{5,7},{... | collective-permute-start | bytes 1572872 | tf_op jit(solution)/shard_map/ppermute | solution.py:27
  8.9 1.4 %copy-start.8 = (f32[256,512]{1,0:T(8,128)S(1)}, f32[256,512]{1,0:T(8,128)}, u32[]{:S(2)}) copy-start(f32[256,512]{1,0:T(8,128)} %diff_ref.1) | copy-start | bytes 1572868
  10.3 1.0 copy-start.6
  10.4 1.2 copy-start.10
  11.5 8.4 %copy-start.11 = (f32[256,512]{1,0:T(8,128)S(1)}, f32[256,512]{1,0:T(8,128)}, u32[]{:S(2)}) copy-start(f32[256,512]{1,0:T(8,128)} %param.10) | copy-start | bytes 1572868
  11.5 8.5 %copy-start.7 = (f32[2,272,512]{2,1,0:T(8,128)S(1)}, f32[2,272,512]{2,1,0:T(8,128)}, u32[]{:S(2)}) copy-start(f32[2,272,512]{2,1,0:T(8,128)} %copy-done.6) | copy-start | bytes 3342340
  12.0 8.1 %slice-start = ((f32[2,272,512]{2,1,0:T(8,128)}), f32[1,272,512]{2,1,0:T(8,128)S(1)}, s32[]{:S(2)}) async-start(f32[2,272,512]{2,1,0:T(8,128)} %copy-done.6), calls=%async_computation.2 | async-start | bytes 1114112 | tf_op jit(solution)/shard_map/slice | solution.py:456
  12.0 8.1 %copy-start.9 = (f32[2,256,512]{2,1,0:T(8,128)S(1)}, f32[2,256,512]{2,1,0:T(8,128)}, u32[]{:S(2)}) copy-start(f32[2,256,512]{2,1,0:T(8,128)} %forcing_ref.1) | copy-start | bytes 3145732
  20.0 1.2 %collective-permute-start.2 = (f32[8,512]{1,0:T(8,128)S(1)}, f32[8,512]{1,0:T(8,128)S(1)}, u32[]{:S(2)}, u32[]{:S(2)}) collective-permute-start(f32[8,512]{1,0:T(8,128)S(1)} %slice_select_fusion), channel_id=1, source_target_pairs={{0,1},{1,0},{2,3},{3,2},{4,5},{5,4},{6,7},{7,6},{8,9},{9,8},{10,11... | collective-permute-start | bytes 49160 | tf_op jit(solution)/shard_map/ppermute | solution.py:47
  20.1 1.1 copy-start.4
  22.8 42.9 %all-to-all-start = ((f32[8,176,128]{2,1,0:T(8,128)}), f32[8,176,128]{2,1,0:T(8,128)S(1)}, u32[]{:S(2)}, u32[]{:S(2)}) async-start(f32[8,176,128]{2,1,0:T(8,128)} %get-tuple-element.15), calls=%async_computation | async-start | bytes 1441792 | tf_op jit(solution)/shard_map/all_to_all | solution.py:490
  30.2 35.5 %copy-start.1 = (f32[128,128]{1,0:T(8,128)S(1)}, f32[128,128]{1,0:T(8,128)}, u32[]{:S(2)}) copy-start(f32[128,128]{1,0:T(8,128)} %constant.56.clone.mix_ref) | copy-start | bytes 196612
  30.2 58.6 %copy-start = (f32[128,128]{1,0:T(8,128)S(1)}, f32[128,128]{1,0:T(8,128)}, u32[]{:S(2)}) copy-start(f32[128,128]{1,0:T(8,128)} %constant.59.clone.mix_ref) | copy-start | bytes 196612
  30.2 58.6 %copy-start.2 = (f32[7,16,128]{2,1,0:T(8,128)S(1)}, f32[7,16,128]{2,1,0:T(8,128)}, u32[]{:S(2)}) copy-start(f32[7,16,128]{2,1,0:T(8,128)} %constant.57.clone.table_ref) | copy-start | bytes 172036
  30.3 58.6 %copy-start.3 = (f32[2,16,128]{2,1,0:T(8,128)S(1)}, f32[2,16,128]{2,1,0:T(8,128)}, u32[]{:S(2)}) copy-start(f32[2,16,128]{2,1,0:T(8,128)} %constant.58.clone.shift_ref) | copy-start | bytes 49156
  30.3 19.3 %collective-permute-start.9 = (f32[176,128]{1,0:T(8,128)S(1)}, f32[176,128]{1,0:T(8,128)S(1)}, u32[]{:S(2)}, u32[]{:S(2)}) collective-permute-start(f32[176,128]{1,0:T(8,128)S(1)} %get-tuple-element.29), channel_id=1, source_target_pairs={{0,14},{2,12},{4,10},{6,8},{8,6},{10,4},{12,2},{14,0},{1,15},{3,13... | collective-permute-start | bytes 270344 | tf_op jit(solution)/shard_map/ppermute | solution.py:34
  35.1 25.7 %collective-permute-start.8 = (f32[176,128]{1,0:T(8,128)S(1)}, f32[176,128]{1,0:T(8,128)S(1)}, u32[]{:S(2)}, u32[]{:S(2)}) collective-permute-start(f32[176,128]{1,0:T(8,128)S(1)} %get-tuple-element.30), channel_id=1, source_target_pairs={{0,12},{2,14},{4,8},{6,10},{8,4},{10,6},{12,0},{14,2},{1,13},{3,15... | collective-permute-start | bytes 270344 | tf_op jit(solution)/shard_map/ppermute | solution.py:34
  35.7 28.5 %collective-permute-start.7 = (f32[176,128]{1,0:T(8,128)S(1)}, f32[176,128]{1,0:T(8,128)S(1)}, u32[]{:S(2)}, u32[]{:S(2)}) collective-permute-start(f32[176,128]{1,0:T(8,128)S(1)} %get-tuple-element.31), channel_id=1, source_target_pairs={{0,10},{2,8},{4,14},{6,12},{8,2},{10,0},{12,6},{14,4},{1,11},{3,9}... | collective-permute-start | bytes 270344 | tf_op jit(solution)/shard_map/ppermute | solution.py:34
  36.3 28.2 %collective-permute-start.6 = (f32[176,128]{1,0:T(8,128)S(1)}, f32[176,128]{1,0:T(8,128)S(1)}, u32[]{:S(2)}, u32[]{:S(2)}) collective-permute-start(f32[176,128]{1,0:T(8,128)S(1)} %get-tuple-element.32), channel_id=1, source_target_pairs={{0,8},{2,10},{4,12},{6,14},{8,0},{10,2},{12,4},{14,6},{1,9},{3,11}... | collective-permute-start | bytes 270344 | tf_op jit(solution)/shard_map/ppermute | solution.py:34
  38.1 26.3 %collective-permute-start.5 = (f32[176,128]{1,0:T(8,128)S(1)}, f32[176,128]{1,0:T(8,128)S(1)}, u32[]{:S(2)}, u32[]{:S(2)}) collective-permute-start(f32[176,128]{1,0:T(8,128)S(1)} %get-tuple-element.33), channel_id=1, source_target_pairs={{0,6},{2,4},{4,2},{6,0},{8,14},{10,12},{12,10},{14,8},{1,7},{3,5},... | collective-permute-start | bytes 270344 | tf_op jit(solution)/shard_map/ppermute | solution.py:34
  49.6 16.1 %collective-permute-start.4 = (f32[176,128]{1,0:T(8,128)S(1)}, f32[176,128]{1,0:T(8,128)S(1)}, u32[]{:S(2)}, u32[]{:S(2)}) collective-permute-start(f32[176,128]{1,0:T(8,128)S(1)} %get-tuple-element.34), channel_id=1, source_target_pairs={{0,4},{2,6},{4,0},{6,2},{8,12},{10,14},{12,8},{14,10},{1,5},{3,7},... | collective-permute-start | bytes 270344 | tf_op jit(solution)/shard_map/ppermute | solution.py:34
  60.8 4.9 %collective-permute-start.3 = (f32[176,128]{1,0:T(8,128)S(1)}, f32[176,128]{1,0:T(8,128)S(1)}, u32[]{:S(2)}, u32[]{:S(2)}) collective-permute-start(f32[176,128]{1,0:T(8,128)S(1)} %get-tuple-element.35), channel_id=1, source_target_pairs={{0,2},{2,0},{4,6},{6,4},{8,10},{10,8},{12,14},{14,12},{1,3},{3,1},... | collective-permute-start | bytes 270344 | tf_op jit(solution)/shard_map/ppermute | solution.py:34
  75.8 1.2 collective-permute-start.10
  77.0 3.7 %collective-permute-start.11 = (f32[16,128]{1,0:T(8,128)S(1)}, f32[16,128]{1,0:T(8,128)S(1)}, u32[]{:S(2)}, u32[]{:S(2)}) collective-permute-start(f32[16,128]{1,0:T(8,128)S(1)} %add.73), channel_id=1, source_target_pairs={{0,2},{2,0},{4,6},{6,4},{8,10},{10,8},{12,14},{14,12},{1,3},{3,1},... | collective-permute-start | bytes 24584 | tf_op jit(solution)/shard_map/ppermute | solution.py:528
  80.7 3.7 %collective-permute-start.12 = (f32[16,128]{1,0:T(8,128)S(1)}, f32[16,128]{1,0:T(8,128)S(1)}, u32[]{:S(2)}, u32[]{:S(2)}) collective-permute-start(f32[16,128]{1,0:T(8,128)S(1)} %add.74), channel_id=1, source_target_pairs={{0,4},{2,6},{4,0},{6,2},{8,12},{10,14},{12,8},{14,10},{1,5},{3,7},... | collective-permute-start | bytes 24584 | tf_op jit(solution)/shard_map/ppermute | solution.py:528
  84.3 4.5 %collective-permute-start.13 = (f32[16,128]{1,0:T(8,128)S(1)}, f32[16,128]{1,0:T(8,128)S(1)}, u32[]{:S(2)}, u32[]{:S(2)}) collective-permute-start(f32[16,128]{1,0:T(8,128)S(1)} %add.75), channel_id=1, source_target_pairs={{0,8},{2,10},{4,12},{6,14},{8,0},{10,2},{12,4},{14,6},{1,9},{3,11}... | collective-permute-start | bytes 24584 | tf_op jit(solution)/shard_map/ppermute | solution.py:528
  91.5 26.6 %all-to-all-start.1 = ((f32[8,64,512]{2,1,0:T(8,128)}), f32[8,64,512]{2,1,0:T(8,128)S(1)}, u32[]{:S(2)}, u32[]{:S(2)}) async-start(f32[8,64,512]{2,1,0:T(8,128)} %combine.1), calls=%async_computation.1 | async-start | bytes 2097152 | tf_op jit(solution)/shard_map/all_to_all | solution.py:549
  96.0 22.2 %copy-start.5 = (f32[2,256,512]{2,1,0:T(8,128)S(1)}, f32[2,256,512]{2,1,0:T(8,128)}, u32[]{:S(2)}) copy-start(f32[2,256,512]{2,1,0:T(8,128)} %iterate_ref.1) | copy-start | bytes 3145732

commit v5 on v4

--- a/solution.py
+++ b/solution.py
@@ -14,6 +14,7 @@
 DEPTH = 2 * CG_ITERS
 MOMENTS = 2 * DEPTH + 1
 UNROLL = 16
+LEAST_PIVOTS = (2e-2, 2e-3)
 PAD = 8
 
 circulant_alpha = 0.05
@@ -33,6 +34,111 @@
     for k in reversed(range(1, count)):
         got[k] = lax.ppermute(pieces[k], "tm", [(i, i ^ k) for i in range(count)])
     return got
+
+
+def summed_over_group(values):
+    for axis in ("rows", "tm"):
+        count = lax.axis_size(axis)
+        if count & (count - 1):
+            values = lax.psum(values, axis)
+        else:
+            step = 1
+            while step < count:
+                pairs = [(i, i ^ step) for i in range(count)]
+                values = values + lax.ppermute(values, axis, pairs)
+                step *= 2
+    return values
+
+
+def extended(block, axis, dim, width):
+    count = lax.axis_size(axis)
+    forward = [(i, i + 1) for i in range(count - 1)]
+    backward = [(target, source) for source, target in forward]
+    low = lax.slice_in_dim(block, block.shape[dim] - width, None, axis=dim)
+    high = lax.slice_in_dim(block, 0, width, axis=dim)
+    low, high = lax.ppermute(low, axis, forward), lax.ppermute(high, axis, backward)
+    return jnp.concatenate([low, block, high], axis=dim)
+
+
+def careful_correction(iterate, forcing, initial_state, diffusivity):
+    steps_dev, rows_dev, columns = iterate.shape
+    time_devices = lax.axis_size("tm")
+    row_devices = lax.axis_size("rows")
+    time_rank = lax.axis_index("tm")
+    row_rank = lax.axis_index("rows")
+    length = steps_dev * time_devices
+    half = length // 2
+    slab = rows_dev // time_devices
+    halo = -(-(DEPTH + 1) // 8) * 8
+    rows = slab + 2 * halo
+    rimmed = extended(diffusivity, "rows", 0, halo)
+    at = lax.broadcasted_iota(jnp.int32, (rows_dev + 2 * halo, 1), 0)
+    rimmed = jnp.where((row_rank == 0) & (at < halo), diffusivity[:1], rimmed)
+    beyond = (row_rank == row_devices - 1) & (at >= halo + rows_dev)
+    rimmed = jnp.where(beyond, diffusivity[-1:], rimmed)
+    arriving = from_behind(iterate[-1], "tm", 1)
+    first_previous = jnp.where(time_rank == 0, initial_state, arriving)
+    previous = jnp.concatenate([first_previous[None], iterate[:-1]], axis=0)
+    faces = face_weights(rimmed[halo - 1 : halo + rows_dev + 1])
+    spread = apply_faces(extended(iterate, "rows", 1, 1), faces)
+    residual = time_step * forcing + previous - iterate - time_step * spread
+    wide = extended(residual, "rows", 1, halo)
+    pieces = jnp.stack(
+        [lax.slice_in_dim(wide, slab * k, slab * k + rows, axis=1) for k in range(time_devices)]
+    )
+    pieces = lax.all_to_all(pieces, "tm", split_axis=0, concat_axis=0, tiled=True)
+    flat = pieces.reshape(length, rows * columns)
+    spectrum = jnp.dot(
+        jnp.asarray(forward_matrix(length), jnp.float32), flat, precision=lax.Precision.HIGHEST
+    ).reshape(length, rows, columns)
+
+    slab_faces = face_weights(
+        jnp.pad(
+            lax.dynamic_slice_in_dim(rimmed, slab * time_rank, rows, axis=0),
+            ((1, 1), (0, 0)),
+            mode="edge",
+        )
+    )
+    place = lax.broadcasted_iota(jnp.int32, (1, rows, 1), 1) - halo
+    grid_row = place + row_rank * rows_dev + time_rank * slab
+    inside = (grid_row >= 0) & (grid_row < rows_dev * row_devices)
+    own = (place >= 0) & (place < slab)
+    real, imag = channel_shifts(length)
+    real = jnp.asarray(real[:, None, None], jnp.float32)
+    imag = jnp.asarray(imag[:, None, None], jnp.float32)
+    channel = lax.broadcasted_iota(jnp.int32, (length, 1, 1), 0)
+    alone = (channel == 0) | (channel == half)
+
+    def operate(values, orientation):
+        padded = jnp.pad(values, ((0, 0), (1, 1), (0, 0)))
+        spread = time_step * apply_faces(padded, slab_faces)
+        swapped = jnp.concatenate([-values[half:], values[:half]])
+        return jnp.where(inside, real * values + orientation * imag * swapped + spread, 0.0)
+
+    def norm(values):
+        sums = jnp.sum(jnp.where(own, values * values, 0.0), axis=(1, 2), keepdims=True)
+        sums = summed_over_group(sums)
+        return jnp.where(alone, sums, sums + jnp.concatenate([sums[half:], sums[:half]]))
+
+    def iterated(_, state):
+        result, remain, search, gamma = state
+        image = operate(search, 1.0)
+        rate = gamma / norm(image)
+        result = result + rate * search
+        remain = remain - rate * image
+        normal = operate(remain, -1.0)
+        gamma_next = norm(normal)
+        search = normal + (gamma_next / gamma) * search
+        return result, remain, search, gamma_next
+
+    normal = operate(spectrum, -1.0)
+    state = (jnp.zeros_like(spectrum), spectrum, normal, norm(normal))
+    result = lax.fori_loop(0, CG_ITERS, iterated, state)[0]
+    result = result[:, halo : halo + slab].reshape(length, slab * columns)
+    corrected = jnp.dot(
+        jnp.asarray(inverse_matrix(length), jnp.float32), result, precision=lax.Precision.HIGHEST
+    ).reshape(time_devices, steps_dev * slab, columns)
+    return lax.all_to_all(corrected, "tm", split_axis=0, concat_axis=0, tiled=True)
 
 
 def border_rows(blocks, axis, width):
@@ -344,7 +450,7 @@
 
 def combine_body(length, slab, halo, moments_ref, table_ref, shift_ref, mix_ref, *rest):
     power_refs = rest[:DEPTH]
-    out_ref = rest[DEPTH]
+    out_ref, doubt_ref = rest[DEPTH:]
     steps_dev = out_ref.shape[1] // slab
     half = length // 2
     own = moments_ref[...]
@@ -364,6 +470,9 @@
     low3 = cross / pivot1
     pivot2 = pivot2 - low3 * cross
     right2 = right2 - low3 * right1
+    sound = (pivot1 > LEAST_PIVOTS[0] * mu[3]) & (pivot2 > LEAST_PIVOTS[1] * mu[5])
+    doubt = jnp.max(jnp.where(sound, 0.0, 1.0), axis=0, keepdims=True)
+    doubt_ref[...] = jnp.broadcast_to(doubt, doubt_ref.shape)
     c2 = right2 / pivot2
     c1 = (right1 - cross * c2) / pivot1
     c0 = (mu[0] - mu[2] * c1 - mu[3] * c2) / mu[1]
@@ -517,26 +626,20 @@
         name="krylov",
     )(place, late, diff_slab, jnp.asarray(block_forward(length, 8)), *early)
 
-    for axis in ("rows", "tm"):
-        count = lax.axis_size(axis)
-        if count & (count - 1):
-            moments = lax.psum(moments, axis)
-        else:
-            step = 1
-            while step < count:
-                pairs = [(i, i ^ step) for i in range(count)]
-                moments = moments + lax.ppermute(moments, axis, pairs)
-                step *= 2
+    moments = summed_over_group(moments)
 
     real, imag = channel_shifts(length)
     shift = np.broadcast_to(np.stack([real, imag])[:, :, None], (2, length, 128))
     table = np.zeros((DEPTH + 1, length, 128))
     table[:, :, :MOMENTS] = power_table(length)
-    corrected = pl.pallas_call(
+    corrected, doubt = pl.pallas_call(
         functools.partial(combine_body, length, slab, halo),
-        out_shape=jax.ShapeDtypeStruct((time_devices, steps_dev * slab, columns_dev), jnp.float32),
+        out_shape=[
+            jax.ShapeDtypeStruct((time_devices, steps_dev * slab, columns_dev), jnp.float32),
+            jax.ShapeDtypeStruct((8, 128), jnp.float32),
+        ],
         in_specs=[vmem] * (4 + DEPTH),
-        out_specs=vmem,
+        out_specs=[vmem] * 2,
         compiler_params=params,
         name="combine",
     )(
@@ -547,6 +650,12 @@
         *powers,
     )
     back = lax.all_to_all(corrected, "tm", split_axis=0, concat_axis=0, tiled=True)
+
+    def redone(trip, _):
+        inputs = (iterate, forcing, initial_state, diffusivity)
+        return careful_correction(*[jnp.where(trip < 2, value, 0.0) for value in inputs])
+
+    back = lax.fori_loop(0, doubt[0, 0].astype(jnp.int32), redone, back)
     own_steps = back.reshape(time_devices, steps_dev, slab, columns_dev)
     own_steps = jnp.swapaxes(own_steps, 0, 1).reshape(steps_dev, rows_dev, columns_dev)
     updated = iterate + own_steps

time: 120 us -> 126 us (1.050)
  other arithmetic: 8.04 us -> 11.6 us
  waiting for transfers between devices: 48.3 us -> 45.4 us
  local copies, waits for them, and re-layouts: 3.01 us -> 5.44 us
  starting transfers between devices: 40 us -> 41.6 us
    mul x1, other arithmetic: 1.05 us -> 4.5 us  [iteration(): wide = wide * keep]
    reshape x0 -> x1, local copies, waits for them, and re-layouts: none -> 1.31 us  [iteration(): own_steps = back.reshape(time_devices, steps_dev, slab, columns_dev)]
  transfers between devices with their start and end apart: 16 -> 16, of which waited for: 11 -> 11; matrix products, arithmetic and copies ran while one was open for 7% -> 10% of each run, Pallas kernels for 0% -> 0%
where the time goes in v5:
time: 126 us; the launch traced here: 125 us
  waiting for transfers between devices  45.4 us (36%)
  starting transfers between devices  41.6 us (33%)
  Pallas kernels  16.7 us (13%)
  other arithmetic  11.6 us (9%)
  local copies, waits for them, and re-layouts  5.44 us (4%)
  blocking collectives  2.45 us (2%)
  between operations  1.66 us (1%)
    ppermute x7, starting transfers between devices, exchanged(): got[k] = lax.ppermute(pieces[k], 'tm', [(i, i ^ k) for i in range(count)])  21.8 us
    all_to_all x1, waiting for transfers between devices, iteration(): lax.all_to_all(corrected, 'tm', split_axis=0, concat_axis=0, tiled=True)  16.1 us
    ppermute x7, waiting for transfers between devices, exchanged(): got[k] = lax.ppermute(pieces[k], 'tm', [(i, i ^ k) for i in range(count)])  11.7 us
    pallas_call x1, Pallas kernels, iteration(): pl.pallas_call(functools.partial(krylov_body, length, slab, halo, time_de...  10.1 us
    ppermute x4, waiting for transfers between devices, summed_over_group(): values = values + lax.ppermute(values, axis, pairs)  9.49 us
    ppermute x1, waiting for transfers between devices, from_behind(): lax.ppermute(value, axis, [(source, source + steps) for source in range(i...  8.1 us
    all_to_all x1, starting transfers between devices, iteration(): late = lax.all_to_all(late, 'tm', split_axis=0, concat_axis=0, tiled=True)  6.8 us
    mul x1, other arithmetic, iteration(): wide = wide * keep  4.5 us
  transfers between devices with their start and end apart: 16, of which 11 were waited for; matrix products, arithmetic and copies ran while one was open for 10% of the time, Pallas kernels for 0%

profile of v5, /device:TPU:0, one launch (start us, length us, event | category | flops | bytes accessed | tf_op | source)
XLA Modules:
  0.0 125.1 jit_solution(13988552885881972640)
XLA Ops:
  0.6 0.6 add_add_fusion.4.rank_ref
  1.2 1.8 %borders.1 = (f32[40,512]{1,0:T(8,128)S(1)}, f32[256,512]{1,0:T(8,128)S(1)}) custom-call(s32[3]{0:T(128)} %add_add_fusion.4.rank_ref, f32[2,256,512]{2,1,0:T(8,128)} %iterate_ref.1, f32[2,256,512]{2,1,0:T(8,128)} %forcing_ref.1, f32[256,512]{1,0:T(8,128)} %diff_ref.1), custom_call_target="tpu_custom_call" | custom-call | tf_op jit(solution)/shard_map/borders/pallas_call | solution.py:530
  3.1 0.6 collective-permute-start.19
  3.6 4.5 %collective-permute-start.20 = (f32[256,512]{1,0:T(8,128)S(1)}, f32[256,512]{1,0:T(8,128)S(1)}, u32[]{:S(2)}, u32[]{:S(2)}) collective-permute-start(f32[256,512]{1,0:T(8,128)S(1)} %get-tuple-element.438), channel_id=1, source_target_pairs={{0,2},{2,4},{4,6},{6,8},{8,10},{10,12},{12,14},{1,3},{3,5},{5,7},{... | collective-permute-start | bytes 1572872 | tf_op jit(solution)/shard_map/ppermute | solution.py:28
  8.1 0.7 fusion.125
  8.9 1.4 %pad_maximum_fusion.10 = f32[2,272,512]{2,1,0:T(8,128)S(1)} fusion(f32[2,8,512]{2,1,0:T(8,128)S(1)} %get-tuple-element.727, f32[2,256,512]{2,1,0:T(8,128)} %iterate_ref.1, f32[2,8,512]{2,1,0:T(8,128)S(1)} %get-tuple-element.728), kind=kLoop, calls=%fused_computation.162 | loop fusion | flops 557056 | bytes 2228224 | tf_op jit(solution)/shard_map/concatenate | solution.py:554
  10.4 0.1 fusion.124
  10.5 0.8 copy-done.17
  11.3 0.5 add_add_fusion.2
  11.8 8.1 %collective-permute-done.20 = f32[256,512]{1,0:T(8,128)S(1)} collective-permute-done((f32[256,512]{1,0:T(8,128)S(1)}, f32[256,512]{1,0:T(8,128)S(1)}, u32[]{:S(2)}, u32[]{:S(2)}) %collective-permute-start.20) | collective-permute-done | bytes 524320 | tf_op jit(solution)/shard_map/ppermute | solution.py:28
  20.1 0.9 slice-done
  20.9 4.5 %fusion.89.partial_ref.wide_ref = f32[2,272,512]{2,1,0:T(8,128)S(1)} fusion(f32[2,272,512]{2,1,0:T(8,128)} %copy-done.16, f32[2,8,512]{2,1,0:T(8,128)S(1)} %get-tuple-element.726, f32[2,256,512]{2,1,0:T(8,128)S(1)} %copy-done.9, f32[2,8,512]{2,1,0:T(8,128)S(1)} %get-tuple-element.725, f32[1,272,512]{2,1,0:T(8,128)S(1)} %slice-done, ...), kind=kLoop, calls=%fused_computation.160 | loop fusion | flops 4456448 | bytes 6685760 | tf_op jit(solution)/shard_map/mul | solution.py:568
  25.5 1.5 %first_step.1 = (f32[8,176,128]{2,1,0:T(8,128)}, f32[1,8,128]{2,1,0:T(8,128)S(1)}) custom-call(s32[3]{0:T(128)S(1)} %copy-done.4, f32[2,272,512]{2,1,0:T(8,128)S(1)} %fusion.89.partial_ref.wide_ref, f32[256,512]{1,0:T(8,128)S(1)} %broadcast_select_fusion.2.previous_ref, f32[8,512]{1,0:T(8,128)S(1)} %collective-permute-done.21.low_ref.high_ref, ...), custom_call_target="tpu_custom_call" | custom-call | tf_op jit(solution)/shard_map/first_step/pallas_call | solution.py:587
  27.0 6.8 %all-to-all-start.2 = ((f32[8,176,128]{2,1,0:T(8,128)}), f32[8,176,128]{2,1,0:T(8,128)S(1)}, u32[]{:S(2)}, u32[]{:S(2)}) async-start(f32[8,176,128]{2,1,0:T(8,128)} %get-tuple-element.439), calls=%async_computation.2 | async-start | bytes 1441792 | tf_op jit(solution)/shard_map/all_to_all | solution.py:599
  33.8 0.6 later_steps.1
  34.5 4.8 %collective-permute-start.28 = (f32[176,128]{1,0:T(8,128)S(1)}, f32[176,128]{1,0:T(8,128)S(1)}, u32[]{:S(2)}, u32[]{:S(2)}) collective-permute-start(f32[176,128]{1,0:T(8,128)S(1)} %get-tuple-element.711), channel_id=1, source_target_pairs={{0,14},{2,12},{4,10},{6,8},{8,6},{10,4},{12,2},{14,0},{1,15},{3,13... | collective-permute-start | bytes 270344 | tf_op jit(solution)/shard_map/ppermute | solution.py:35
  39.3 0.6 collective-permute-start.27
  39.9 0.6 collective-permute-start.26
  40.5 1.9 %collective-permute-start.25 = (f32[176,128]{1,0:T(8,128)S(1)}, f32[176,128]{1,0:T(8,128)S(1)}, u32[]{:S(2)}, u32[]{:S(2)}) collective-permute-start(f32[176,128]{1,0:T(8,128)S(1)} %get-tuple-element.714), channel_id=1, source_target_pairs={{0,8},{2,10},{4,12},{6,14},{8,0},{10,2},{12,4},{14,6},{1,9},{3,11}... | collective-permute-start | bytes 270344 | tf_op jit(solution)/shard_map/ppermute | solution.py:35
  42.4 2.3 %collective-permute-start.24 = (f32[176,128]{1,0:T(8,128)S(1)}, f32[176,128]{1,0:T(8,128)S(1)}, u32[]{:S(2)}, u32[]{:S(2)}) collective-permute-start(f32[176,128]{1,0:T(8,128)S(1)} %get-tuple-element.715), channel_id=1, source_target_pairs={{0,6},{2,4},{4,2},{6,0},{8,14},{10,12},{12,10},{14,8},{1,7},{3,5},... | collective-permute-start | bytes 270344 | tf_op jit(solution)/shard_map/ppermute | solution.py:35
  44.6 9.2 %collective-permute-done.28.rest_7_ = f32[176,128]{1,0:T(8,128)S(1)} collective-permute-done((f32[176,128]{1,0:T(8,128)S(1)}, f32[176,128]{1,0:T(8,128)S(1)}, u32[]{:S(2)}, u32[]{:S(2)}) %collective-permute-start.28) | collective-permute-done | bytes 90144 | tf_op jit(solution)/shard_map/ppermute | solution.py:35
  53.9 10.5 %collective-permute-start.23 = (f32[176,128]{1,0:T(8,128)S(1)}, f32[176,128]{1,0:T(8,128)S(1)}, u32[]{:S(2)}, u32[]{:S(2)}) collective-permute-start(f32[176,128]{1,0:T(8,128)S(1)} %get-tuple-element.716), channel_id=1, source_target_pairs={{0,4},{2,6},{4,0},{6,2},{8,12},{10,14},{12,8},{14,10},{1,5},{3,7},... | collective-permute-start | bytes 270344 | tf_op jit(solution)/shard_map/ppermute | solution.py:35
  64.4 1.2 collective-permute-start.22
  65.6 0.9 constant_dynamic-slice_fusion.4.diff_ref
  66.5 1.3 %collective-permute-done.26.rest_5_ = f32[176,128]{1,0:T(8,128)S(1)} collective-permute-done((f32[176,128]{1,0:T(8,128)S(1)}, f32[176,128]{1,0:T(8,128)S(1)}, u32[]{:S(2)}, u32[]{:S(2)}) %collective-permute-start.26) | collective-permute-done | bytes 90144 | tf_op jit(solution)/shard_map/ppermute | solution.py:35
  67.8 0.1 collective-permute-done.25.rest_4_
  67.9 0.9 collective-permute-done.23.rest_2_
  68.8 0.2 collective-permute-done.22.rest_1_
  68.9 10.1 %krylov.1 = (f32[704,512]{1,0:T(8,128)S(1)}, f32[704,512]{1,0:T(8,128)S(1)}, f32[704,512]{1,0:T(8,128)S(1)}, f32[704,512]{1,0:T(8,128)S(1)}, f32[704,512]{1,0:T(...) custom-call(s32[3]{0:T(128)S(1)} %add_add_fusion.3.place_ref, f32[8,176,128]{2,1,0:T(8,128)S(1)} %all-to-all-done.2.late_ref, ...), custom_call_target="tpu_custom_call" | custom-call | tf_op jit(solution)/shard_map/krylov/pallas_call | solution.py:614
  79.1 1.2 collective-permute-done.29
  80.3 1.2 collective-permute-start.30
  81.5 2.4 %collective-permute-done.30 = f32[16,128]{1,0:T(8,128)S(1)} collective-permute-done((f32[16,128]{1,0:T(8,128)S(1)}, f32[16,128]{1,0:T(8,128)S(1)}, u32[]{:S(2)}, u32[]{:S(2)}) %collective-permute-start.30) | collective-permute-done | bytes 8224 | tf_op jit(solution)/shard_map/ppermute | solution.py:48
  83.9 1.6 %collective-permute-start.31 = (f32[16,128]{1,0:T(8,128)S(1)}, f32[16,128]{1,0:T(8,128)S(1)}, u32[]{:S(2)}, u32[]{:S(2)}) collective-permute-start(f32[16,128]{1,0:T(8,128)S(1)} %add.488), channel_id=1, source_target_pairs={{0,4},{2,6},{4,0},{6,2},{8,12},{10,14},{12,8},{14,10},{1,5},{3,7},... | collective-permute-start | bytes 24584 | tf_op jit(solution)/shard_map/ppermute | solution.py:48
  85.6 2.0 %collective-permute-done.31 = f32[16,128]{1,0:T(8,128)S(1)} collective-permute-done((f32[16,128]{1,0:T(8,128)S(1)}, f32[16,128]{1,0:T(8,128)S(1)}, u32[]{:S(2)}, u32[]{:S(2)}) %collective-permute-start.31) | collective-permute-done | bytes 8224 | tf_op jit(solution)/shard_map/ppermute | solution.py:48
  87.6 0.6 collective-permute-start.32
  88.2 3.9 %collective-permute-done.32 = f32[16,128]{1,0:T(8,128)S(1)} collective-permute-done((f32[16,128]{1,0:T(8,128)S(1)}, f32[16,128]{1,0:T(8,128)S(1)}, u32[]{:S(2)}, u32[]{:S(2)}) %collective-permute-start.32) | collective-permute-done | bytes 8224 | tf_op jit(solution)/shard_map/ppermute | solution.py:48
  92.1 2.6 %combine.1 = (f32[8,64,512]{2,1,0:T(8,128)}, f32[8,128]{1,0:T(8,128)S(1)}) custom-call(f32[16,128]{1,0:T(8,128)S(1)} %add.490.moments_ref, f32[7,16,128]{2,1,0:T(8,128)S(1)} %copy-done.2, f32[2,16,128]{2,1,0:T(8,128)S(1)} %copy-done.3, f32[128,128]{1,0:T(8,128)S(1)} %copy-done, f32[704,512]{1,0:T(8,128)S(1)} %get-tuple-element.441.rest_0_, ...), custom_call_target="tpu_custom_call" | custom-call | tf_op jit(solution)/shard_map/combine/pallas_call | solution.py:635
  94.8 4.4 %all-to-all-start.3 = ((f32[8,64,512]{2,1,0:T(8,128)}), f32[8,64,512]{2,1,0:T(8,128)}, u32[]{:S(2)}, u32[]{:S(2)}) async-start(f32[8,64,512]{2,1,0:T(8,128)} %get-tuple-element.447), calls=%async_computation.3 | async-start | bytes 2097152 | tf_op jit(solution)/shard_map/all_to_all | solution.py:652
  99.2 0.7 fusion.99
  99.9 0.7 reduce_sum.61
  100.6 1.3 %pad_maximum_fusion.24 = f32[2]{0:T(128)S(1)} fusion(f32[1]{0:T(128)} %bitcast.22, f32[1]{0:T(128)} %bitcast.21), kind=kLoop, calls=%fused_computation.209 | loop fusion | flops 2 | bytes 16 | tf_op jit(solution)/shard_map/concatenate | solution.py:601
  101.9 2.4 %psum.7 = f32[2]{0:T(128)S(1)} all-reduce(f32[2]{0:T(128)S(1)} %pad_maximum_fusion.24), channel_id=1, replica_groups=mesh['groups'=2,'tm'=8,'rows'=2] {'rows'}, use_global_device_ids=true, to_apply=%region_9.10 | all-reduce | flops 2 | bytes 16 | tf_op jit(solution)/shard_map/psum | solution.py:602
  104.4 0.5 add_sqrt_fusion
  104.9 0.6 slice.600
  106.2 16.1 %all-to-all-done.3 = f32[8,64,512]{2,1,0:T(8,128)} async-done(((f32[8,64,512]{2,1,0:T(8,128)}), f32[8,64,512]{2,1,0:T(8,128)}, u32[]{:S(2)}, u32[]{:S(2)}) %all-to-all-start.3) | async-done | bytes 1048608 | tf_op jit(solution)/shard_map/all_to_all | solution.py:652
  122.3 0.2 while.48
  122.6 1.3 %copy.16 = f32[8,2,32,512]{3,2,0,1:T(8,128)S(1)} copy(f32[8,2,32,512]{3,2,1,0:T(8,128)} %bitcast.18) | data formatting | bytes 2097152 | tf_op jit(solution)/shard_map/reshape | solution.py:659
  123.9 1.2 bitcast_add_fusion.3
  (51 shorter events, 0.5 us)
Async XLA Ops:
  3.1 5.8 %collective-permute-start.19 = (f32[40,512]{1,0:T(8,128)S(1)}, f32[40,512]{1,0:T(8,128)S(1)}, u32[]{:S(2)}, u32[]{:S(2)}) collective-permute-start(f32[40,512]{1,0:T(8,128)S(1)} %get-tuple-element.437), channel_id=1, source_target_pairs={{0,1},{1,0},{2,3},{3,2},{4,5},{5,4},{6,7},{7,6},{8,9},{9,8},{10,11... | collective-permute-start | bytes 245768 | tf_op jit(solution)/shard_map/ppermute | solution.py:542
  3.6 16.2 %collective-permute-start.20 = (f32[256,512]{1,0:T(8,128)S(1)}, f32[256,512]{1,0:T(8,128)S(1)}, u32[]{:S(2)}, u32[]{:S(2)}) collective-permute-start(f32[256,512]{1,0:T(8,128)S(1)} %get-tuple-element.438), channel_id=1, source_target_pairs={{0,2},{2,4},{4,6},{6,8},{8,10},{10,12},{12,14},{1,3},{3,5},{5,7},{... | collective-permute-start | bytes 1572872 | tf_op jit(solution)/shard_map/ppermute | solution.py:28
  8.9 1.4 %copy-start.11 = (f32[256,512]{1,0:T(8,128)S(1)}, f32[256,512]{1,0:T(8,128)}, u32[]{:S(2)}) copy-start(f32[256,512]{1,0:T(8,128)} %diff_ref.1) | copy-start | bytes 1572868
  10.3 1.5 %copy-start.16 = (f32[2,272,512]{2,1,0:T(8,128)}, f32[2,272,512]{2,1,0:T(8,128)S(1)}, u32[]{:S(2)}) copy-start(f32[2,272,512]{2,1,0:T(8,128)S(1)} %pad_maximum_fusion.10) | copy-start | bytes 3342340
  10.4 0.9 copy-start.17
  11.3 8.6 %copy-start.14 = (f32[256,512]{1,0:T(8,128)S(1)}, f32[256,512]{1,0:T(8,128)}, u32[]{:S(2)}) copy-start(f32[256,512]{1,0:T(8,128)} %param.18) | copy-start | bytes 1572868
  11.8 8.3 %copy-start.9 = (f32[2,256,512]{2,1,0:T(8,128)S(1)}, f32[2,256,512]{2,1,0:T(8,128)}, u32[]{:S(2)}) copy-start(f32[2,256,512]{2,1,0:T(8,128)} %forcing_ref.1) | copy-start | bytes 3145732
  19.9 1.1 slice-start
  20.0 5.5 %collective-permute-start.21 = (f32[8,512]{1,0:T(8,128)S(1)}, f32[8,512]{1,0:T(8,128)S(1)}, u32[]{:S(2)}, u32[]{:S(2)}) collective-permute-start(f32[8,512]{1,0:T(8,128)S(1)} %slice_select_fusion), channel_id=1, source_target_pairs={{0,1},{1,0},{2,3},{3,2},{4,5},{5,4},{6,7},{7,6},{8,9},{9,8},{10,11... | collective-permute-start | bytes 49160 | tf_op jit(solution)/shard_map/ppermute | solution.py:153
  20.9 4.5 %copy-start.4 = (s32[3]{0:T(128)S(1)}, s32[3]{0:T(128)}, u32[]{:S(2)}) copy-start(s32[3]{0:T(128)} %add_add_fusion.4.rank_ref) | copy-start | bytes 40
  27.0 41.9 %all-to-all-start.2 = ((f32[8,176,128]{2,1,0:T(8,128)}), f32[8,176,128]{2,1,0:T(8,128)S(1)}, u32[]{:S(2)}, u32[]{:S(2)}) async-start(f32[8,176,128]{2,1,0:T(8,128)} %get-tuple-element.439), calls=%async_computation.2 | async-start | bytes 1441792 | tf_op jit(solution)/shard_map/all_to_all | solution.py:599
  33.8 35.2 %copy-start.1 = (f32[128,128]{1,0:T(8,128)S(1)}, f32[128,128]{1,0:T(8,128)}, u32[]{:S(2)}) copy-start(f32[128,128]{1,0:T(8,128)} %constant.205.clone.mix_ref) | copy-start | bytes 196612
  34.4 57.7 %copy-start = (f32[128,128]{1,0:T(8,128)S(1)}, f32[128,128]{1,0:T(8,128)}, u32[]{:S(2)}) copy-start(f32[128,128]{1,0:T(8,128)} %constant.208.clone.mix_ref) | copy-start | bytes 196612
  34.4 57.7 %copy-start.2 = (f32[7,16,128]{2,1,0:T(8,128)S(1)}, f32[7,16,128]{2,1,0:T(8,128)}, u32[]{:S(2)}) copy-start(f32[7,16,128]{2,1,0:T(8,128)} %constant.206.clone.table_ref) | copy-start | bytes 172036
  34.4 57.7 %copy-start.3 = (f32[2,16,128]{2,1,0:T(8,128)S(1)}, f32[2,16,128]{2,1,0:T(8,128)}, u32[]{:S(2)}) copy-start(f32[2,16,128]{2,1,0:T(8,128)} %constant.207.clone.shift_ref) | copy-start | bytes 49156
  34.5 19.4 %collective-permute-start.28 = (f32[176,128]{1,0:T(8,128)S(1)}, f32[176,128]{1,0:T(8,128)S(1)}, u32[]{:S(2)}, u32[]{:S(2)}) collective-permute-start(f32[176,128]{1,0:T(8,128)S(1)} %get-tuple-element.711), channel_id=1, source_target_pairs={{0,14},{2,12},{4,10},{6,8},{8,6},{10,4},{12,2},{14,0},{1,15},{3,13... | collective-permute-start | bytes 270344 | tf_op jit(solution)/shard_map/ppermute | solution.py:35
  39.3 25.1 %collective-permute-start.27 = (f32[176,128]{1,0:T(8,128)S(1)}, f32[176,128]{1,0:T(8,128)S(1)}, u32[]{:S(2)}, u32[]{:S(2)}) collective-permute-start(f32[176,128]{1,0:T(8,128)S(1)} %get-tuple-element.712), channel_id=1, source_target_pairs={{0,12},{2,14},{4,8},{6,10},{8,4},{10,6},{12,0},{14,2},{1,13},{3,15... | collective-permute-start | bytes 270344 | tf_op jit(solution)/shard_map/ppermute | solution.py:35
  39.9 27.9 %collective-permute-start.26 = (f32[176,128]{1,0:T(8,128)S(1)}, f32[176,128]{1,0:T(8,128)S(1)}, u32[]{:S(2)}, u32[]{:S(2)}) collective-permute-start(f32[176,128]{1,0:T(8,128)S(1)} %get-tuple-element.713), channel_id=1, source_target_pairs={{0,10},{2,8},{4,14},{6,12},{8,2},{10,0},{12,6},{14,4},{1,11},{3,9}... | collective-permute-start | bytes 270344 | tf_op jit(solution)/shard_map/ppermute | solution.py:35
  40.5 27.4 %collective-permute-start.25 = (f32[176,128]{1,0:T(8,128)S(1)}, f32[176,128]{1,0:T(8,128)S(1)}, u32[]{:S(2)}, u32[]{:S(2)}) collective-permute-start(f32[176,128]{1,0:T(8,128)S(1)} %get-tuple-element.714), channel_id=1, source_target_pairs={{0,8},{2,10},{4,12},{6,14},{8,0},{10,2},{12,4},{14,6},{1,9},{3,11}... | collective-permute-start | bytes 270344 | tf_op jit(solution)/shard_map/ppermute | solution.py:35
  42.4 25.5 %collective-permute-start.24 = (f32[176,128]{1,0:T(8,128)S(1)}, f32[176,128]{1,0:T(8,128)S(1)}, u32[]{:S(2)}, u32[]{:S(2)}) collective-permute-start(f32[176,128]{1,0:T(8,128)S(1)} %get-tuple-element.715), channel_id=1, source_target_pairs={{0,6},{2,4},{4,2},{6,0},{8,14},{10,12},{12,10},{14,8},{1,7},{3,5},... | collective-permute-start | bytes 270344 | tf_op jit(solution)/shard_map/ppermute | solution.py:35
  53.9 14.9 %collective-permute-start.23 = (f32[176,128]{1,0:T(8,128)S(1)}, f32[176,128]{1,0:T(8,128)S(1)}, u32[]{:S(2)}, u32[]{:S(2)}) collective-permute-start(f32[176,128]{1,0:T(8,128)S(1)} %get-tuple-element.716), channel_id=1, source_target_pairs={{0,4},{2,6},{4,0},{6,2},{8,12},{10,14},{12,8},{14,10},{1,5},{3,7},... | collective-permute-start | bytes 270344 | tf_op jit(solution)/shard_map/ppermute | solution.py:35
  64.4 4.5 %collective-permute-start.22 = (f32[176,128]{1,0:T(8,128)S(1)}, f32[176,128]{1,0:T(8,128)S(1)}, u32[]{:S(2)}, u32[]{:S(2)}) collective-permute-start(f32[176,128]{1,0:T(8,128)S(1)} %get-tuple-element.717), channel_id=1, source_target_pairs={{0,2},{2,0},{4,6},{6,4},{8,10},{10,8},{12,14},{14,12},{1,3},{3,1},... | collective-permute-start | bytes 270344 | tf_op jit(solution)/shard_map/ppermute | solution.py:35
  79.1 1.2 collective-permute-start.29
  80.3 3.7 %collective-permute-start.30 = (f32[16,128]{1,0:T(8,128)S(1)}, f32[16,128]{1,0:T(8,128)S(1)}, u32[]{:S(2)}, u32[]{:S(2)}) collective-permute-start(f32[16,128]{1,0:T(8,128)S(1)} %add.487), channel_id=1, source_target_pairs={{0,2},{2,0},{4,6},{6,4},{8,10},{10,8},{12,14},{14,12},{1,3},{3,1},... | collective-permute-start | bytes 24584 | tf_op jit(solution)/shard_map/ppermute | solution.py:48
  83.9 3.7 %collective-permute-start.31 = (f32[16,128]{1,0:T(8,128)S(1)}, f32[16,128]{1,0:T(8,128)S(1)}, u32[]{:S(2)}, u32[]{:S(2)}) collective-permute-start(f32[16,128]{1,0:T(8,128)S(1)} %add.488), channel_id=1, source_target_pairs={{0,4},{2,6},{4,0},{6,2},{8,12},{10,14},{12,8},{14,10},{1,5},{3,7},... | collective-permute-start | bytes 24584 | tf_op jit(solution)/shard_map/ppermute | solution.py:48
  87.6 4.5 %collective-permute-start.32 = (f32[16,128]{1,0:T(8,128)S(1)}, f32[16,128]{1,0:T(8,128)S(1)}, u32[]{:S(2)}, u32[]{:S(2)}) collective-permute-start(f32[16,128]{1,0:T(8,128)S(1)} %add.489), channel_id=1, source_target_pairs={{0,8},{2,10},{4,12},{6,14},{8,0},{10,2},{12,4},{14,6},{1,9},{3,11}... | collective-permute-start | bytes 24584 | tf_op jit(solution)/shard_map/ppermute | solution.py:48
  94.8 27.5 %copy-start.7 = (f32[2,256,512]{2,1,0:T(8,128)S(1)}, f32[2,256,512]{2,1,0:T(8,128)}, u32[]{:S(2)}) copy-start(f32[2,256,512]{2,1,0:T(8,128)} %iterate_ref.1) | copy-start | bytes 3145732
  94.8 27.5 %copy-start.12 = (f32[256,512]{1,0:T(8,128)S(1)}, f32[256,512]{1,0:T(8,128)}, u32[]{:S(2)}) copy-start(f32[256,512]{1,0:T(8,128)} %diff_ref.1) | copy-start | bytes 1572868
  94.8 27.5 %copy-start.18 = (f32[16]{0:T(128)S(1)}, f32[16]{0:T(128)}, u32[]{:S(2)}) copy-start(f32[16]{0:T(128)} %constant.483) | copy-start | bytes 196
  94.8 27.5 %copy-start.19 = (f32[16]{0:T(128)S(1)}, f32[16]{0:T(128)}, u32[]{:S(2)}) copy-start(f32[16]{0:T(128)} %constant.482) | copy-start | bytes 196
  94.8 27.5 %copy-start.20 = (f32[16,16]{1,0:T(8,128)S(1)}, f32[16,16]{1,0:T(8,128)}, u32[]{:S(2)}) copy-start(f32[16,16]{1,0:T(8,128)} %constant.209.clone..sunk.2) | copy-start | bytes 3076
  94.8 27.5 %all-to-all-start.3 = ((f32[8,64,512]{2,1,0:T(8,128)}), f32[8,64,512]{2,1,0:T(8,128)}, u32[]{:S(2)}, u32[]{:S(2)}) async-start(f32[8,64,512]{2,1,0:T(8,128)} %get-tuple-element.447), calls=%async_computation.3 | async-start | bytes 2097152 | tf_op jit(solution)/shard_map/all_to_all | solution.py:652

commit v6 on v5

--- a/solution.py
+++ b/solution.py
@@ -58,6 +58,27 @@
     high = lax.slice_in_dim(block, 0, width, axis=dim)
     low, high = lax.ppermute(low, axis, forward), lax.ppermute(high, axis, backward)
     return jnp.concatenate([low, block, high], axis=dim)
+
+
+def finish_body(slab, iterate_ref, back_ref, out_ref, got_ref, sum_ref, arrived, left):
+    chunks = back_ref.shape[0]
+    copies = [
+        pltpu.make_async_copy(back_ref.at[k], got_ref.at[k], arrived.at[k]) for k in range(chunks)
+    ]
+    for copy in copies:
+        copy.start()
+    leaving = []
+    for k in range(chunks):
+        copies[k].wait()
+        at = slice(slab * k, slab * (k + 1))
+        for s in range(iterate_ref.shape[0]):
+            sum_ref[s, at, :] = iterate_ref[s, at, :] + got_ref[k, slab * s : slab * (s + 1), :]
+        leaving.append(
+            pltpu.make_async_copy(sum_ref.at[:, at, :], out_ref.at[:, at, :], left.at[k])
+        )
+        leaving[-1].start()
+    for copy in leaving:
+        copy.wait()
 
 
 def careful_correction(iterate, forcing, initial_state, diffusivity):
@@ -249,15 +270,17 @@
     )
 
 
-def borders_body(rank_ref, iterate_ref, forcing_ref, diff_ref, mine_ref, last_ref, done):
+def borders_body(iterate_ref, forcing_ref, diff_ref, mine_ref, last_ref, rim_ref, done):
     steps, rows_dev, _ = iterate_ref.shape
-    start = pl.multiple_of(jnp.where(rank_ref[0] == 0, rows_dev - PAD, 0), 8)
+    start = pl.multiple_of(jnp.where(lax.axis_index("rows") == 0, rows_dev - PAD, 0), 8)
     copies = []
     for s in range(steps):
         copies.append((iterate_ref.at[s, pl.ds(start, PAD)], mine_ref.at[pl.ds(PAD * s, PAD)]))
         at = PAD * (steps + s)
         copies.append((forcing_ref.at[s, pl.ds(start, PAD)], mine_ref.at[pl.ds(at, PAD)]))
     copies.append((diff_ref.at[pl.ds(start, PAD)], mine_ref.at[pl.ds(2 * PAD * steps, PAD)]))
+    copies.append((diff_ref.at[pl.ds(0, PAD)], rim_ref.at[pl.ds(0, PAD)]))
+    copies.append((diff_ref.at[pl.ds(rows_dev - PAD, PAD)], rim_ref.at[pl.ds(PAD, PAD)]))
     copies.append((iterate_ref.at[steps - 1], last_ref))
     started = []
     for index, (source, target) in enumerate(copies):
@@ -277,11 +300,11 @@
             ]
 
 
-def later_steps_body(slab, halo, rank_ref, wide_ref, pieces_ref):
+def later_steps_body(slab, halo, wide_ref, pieces_ref):
     steps, _, columns = wide_ref.shape
     for s in range(1, steps):
         at = (s - 1) * (columns // 128) * (slab + 2 * halo)
-        pack(pieces_ref, at, wide_ref.at[s], slab, halo, rank_ref[2])
+        pack(pieces_ref, at, wide_ref.at[s], slab, halo)
 
 
 def first_step_body(slab, halo, rank_ref, partial_ref, previous_ref, low_ref, high_ref,
@@ -300,7 +323,7 @@
     for t in range(1, columns // 128):
         total = total + squares[:, 128 * t : 128 * t + 128]
     squares_ref[0] = total
-    pack(pieces_ref, 0, whole_ref, slab, halo)
+    pack(pieces_ref, 0, whole_ref, slab, halo, rank_ref[2])
 
 
 def put_weights(diff_ref, south_ref, east_ref, west_ref):
@@ -336,15 +359,15 @@
             target[start * length : (start + 8) * length, 128 * t : 128 * t + 128] = jnp.dot(
                 mix,
                 jnp.concatenate(cells, axis=0),
-                precision=lax.Precision.HIGHEST,
+                precision=lax.Precision.HIGH,
                 preferred_element_type=jnp.float32,
             )
 
 
-def krylov_body(length, slab, halo, sources, place_ref, late_ref, diff_ref, mix_ref, *rest):
+def krylov_body(length, slab, halo, sources, place_ref, early_ref, diff_ref, mix_ref, *rest):
     pieces = rest[:sources]
     vectors = rest[sources : sources + DEPTH]
-    moments_ref, early_ref, south_ref, east_ref, west_ref = rest[sources + DEPTH :]
+    moments_ref, late_ref, south_ref, east_ref, west_ref = rest[sources + DEPTH :]
     rows = slab + 2 * halo
     columns = diff_ref.shape[-1]
     groups = length // 8
@@ -355,7 +378,7 @@
     keep_below = jnp.where(last_row, 0.0, 1.0)
     put_weights(diff_ref, south_ref, east_ref, west_ref)
     for index, piece in enumerate(pieces):
-        early_ref[index ^ place_ref[2]] = piece[...]
+        late_ref[index ^ place_ref[2]] = piece[...]
     transform(vectors[0], early_ref, late_ref, mix_ref[...], rows, length, tiles)
 
     lane8 = lax.broadcasted_iota(jnp.int32, (8, 128), 1)
@@ -501,7 +524,7 @@
                 other = other + spread(crossed, power) * flipped
         block = (total + other).reshape(8 * length, columns)
         result = jnp.dot(
-            mix_ref[...], block, precision=lax.Precision.HIGHEST, preferred_element_type=jnp.float32
+            mix_ref[...], block, precision=lax.Precision.HIGH, preferred_element_type=jnp.float32
         )
         for step in range(length):
             at = (step % steps_dev) * slab + start
@@ -527,21 +550,23 @@
     rank = jnp.stack([row_rank, jnp.int32(row_devices), time_rank]).astype(jnp.int32)
 
     if row_devices == 2:
-        mine, last = pl.pallas_call(
+        mine, last, rim = pl.pallas_call(
             borders_body,
             out_shape=[
                 pltpu.VMEM(((2 * steps_dev + 1) * PAD, columns_dev), jnp.float32),
                 pltpu.VMEM((rows_dev, columns_dev), jnp.float32),
+                pltpu.VMEM((2 * PAD, columns_dev), jnp.float32),
             ],
-            in_specs=[smem] + [pl.BlockSpec(memory_space=pltpu.HBM)] * 3,
-            out_specs=[vmem] * 2,
-            scratch_shapes=[pltpu.SemaphoreType.DMA((2 * steps_dev + 2,))],
+            in_specs=[pl.BlockSpec(memory_space=pltpu.HBM)] * 3,
+            out_specs=[vmem] * 3,
+            scratch_shapes=[pltpu.SemaphoreType.DMA((2 * steps_dev + 4,))],
             compiler_params=pltpu.CompilerParams(vmem_limit_bytes=2**26 - 3 * 2**18),
             name="borders",
-        )(rank, iterate, forcing, diffusivity)
+        )(iterate, forcing, diffusivity)
         low = high = lax.ppermute(mine, "rows", [(0, 1), (1, 0)])
     else:
         last = iterate[-1]
+        rim = jnp.concatenate([diffusivity[:PAD], diffusivity[-PAD:]])
         low, high = border_rows((iterate, forcing, diffusivity), "rows", PAD)
     arriving = from_behind(last, "tm", 1)
 
@@ -555,8 +580,8 @@
             [keep_low * low[at].reshape(shape), block, keep_high * high[at].reshape(shape)], axis=1
         )
 
-    diff_low = jnp.where(row_rank == 0, diffusivity[:1], low[-PAD:])
-    diff_high = jnp.where(row_rank == row_devices - 1, diffusivity[-1:], high[-PAD:])
+    diff_low = jnp.where(row_rank == 0, rim[:1], low[-PAD:])
+    diff_high = jnp.where(row_rank == row_devices - 1, rim[-1:], high[-PAD:])
     rimmed = jnp.concatenate([diff_low, diffusivity, diff_high])
     wide_iterate = widened(iterate, 0)
     faces = face_weights(jnp.pad(rimmed, ((1, 1), (0, 0)), mode="edge"))
@@ -575,12 +600,12 @@
         out_shape=jax.ShapeDtypeStruct(
             (time_devices, (steps_dev - 1) * tiles * rows, 128), jnp.float32
         ),
-        in_specs=[smem, vmem],
+        in_specs=[vmem],
         out_specs=vmem,
         compiler_params=params,
         name="later_steps",
-    )(rank, wide)
-    early = exchanged(early)
+    )(wide)
+    early = lax.all_to_all(early, "tm", split_axis=0, concat_axis=0, tiled=True)
 
     previous = jnp.where(time_rank == 0, initial_state, arriving)
     before_low, before_high = border_rows((previous,), "rows", PAD)
@@ -596,7 +621,7 @@
         compiler_params=params,
         name="first_step",
     )(rank, wide, previous, before_low, before_high)
-    late = lax.all_to_all(late, "tm", split_axis=0, concat_axis=0, tiled=True)
+    late = exchanged(late)
 
     squares = jnp.concatenate([jnp.sum(squares_first, axis=(1, 2)), squares_late])
     residual_rms = jnp.sqrt(lax.psum(squares, "rows") / cell_count + rms_eps)
@@ -617,14 +642,14 @@
         in_specs=[smem] + [vmem] * (3 + time_devices),
         out_specs=[vmem] * (DEPTH + 1),
         scratch_shapes=[
-            pltpu.VMEM((time_devices, (steps_dev - 1) * tiles * rows, 128), jnp.float32),
+            pltpu.VMEM((time_devices, tiles * rows, 128), jnp.float32),
             pltpu.VMEM((rows * 8, columns_dev), jnp.float32),
             pltpu.VMEM((rows * 8, columns_dev), jnp.float32),
             pltpu.VMEM((rows * 8, 128), jnp.float32),
         ],
         compiler_params=params,
         name="krylov",
-    )(place, late, diff_slab, jnp.asarray(block_forward(length, 8)), *early)
+    )(place, early, diff_slab, jnp.asarray(block_forward(length, 8)), *late)
 
     moments = summed_over_group(moments)
 
@@ -656,9 +681,20 @@
         return careful_correction(*[jnp.where(trip < 2, value, 0.0) for value in inputs])
 
     back = lax.fori_loop(0, doubt[0, 0].astype(jnp.int32), redone, back)
-    own_steps = back.reshape(time_devices, steps_dev, slab, columns_dev)
-    own_steps = jnp.swapaxes(own_steps, 0, 1).reshape(steps_dev, rows_dev, columns_dev)
-    updated = iterate + own_steps
+    updated = pl.pallas_call(
+        functools.partial(finish_body, slab),
+        out_shape=jax.ShapeDtypeStruct(iterate.shape, jnp.float32),
+        in_specs=[vmem, pl.BlockSpec(memory_space=pl.ANY)],
+        out_specs=pl.BlockSpec(memory_space=pltpu.HBM),
+        scratch_shapes=[
+            pltpu.VMEM(back.shape, jnp.float32),
+            pltpu.VMEM(iterate.shape, jnp.float32),
+            pltpu.SemaphoreType.DMA((time_devices,)),
+            pltpu.SemaphoreType.DMA((time_devices,)),
+        ],
+        compiler_params=params,
+        name="finish",
+    )(iterate, back)
     return (updated, residual_rms)
 
 

time: 126 us -> 109 us (0.87)
  waiting for transfers between devices: 45.4 us -> 31.8 us
  other arithmetic: 11.6 us -> 7.31 us
  starting transfers between devices: 41.6 us -> 44.4 us
  local copies, waits for them, and re-layouts: 5.44 us -> 3.41 us
    ppermute x7, waiting for transfers between devices: 11.7 us -> 2.97 us  [exchanged(): got[k] = lax.ppermute(pieces[k], 'tm', [(i, i ^ k) for i in range(count)])]
    ppermute x1, waiting for transfers between devices: 8.1 us -> 1.78 us  [from_behind(): lax.ppermute(value, axis, [(source, source + steps) for source in range(i...]
    ppermute x7, starting transfers between devices: 21.8 us -> 26.7 us  [exchanged(): got[k] = lax.ppermute(pieces[k], 'tm', [(i, i ^ k) for i in range(count)])]
    mul x1, other arithmetic: 4.5 us -> 1.02 us  [iteration(): wide = wide * keep]
    all_to_all x1, starting transfers between devices: 6.8 us -> 4.08 us  [iteration(): early = lax.all_to_all(early, 'tm', split_axis=0, concat_axis=0, tiled=True)]
    pallas_call x0 -> x1, Pallas kernels: none -> 2.11 us  [iteration(): pl.pallas_call(functools.partial(finish_body, slab), out_shape=jax.ShapeD...]
    reshape x1 -> x0, local copies, waits for them, and re-layouts: 1.31 us -> none  [iteration(): own_steps = back.reshape(time_devices, steps_dev, slab, columns_dev)]
    concatenate x1, other arithmetic: 1.36 us -> 0.08 us  [widened(): jnp.concatenate([keep_low * low[at].reshape(shape), block, keep_high * hi...]
  transfers between devices with their start and end apart: 16 -> 16, of which waited for: 11 -> 12; matrix products, arithmetic and copies ran while one was open for 10% -> 8% of each run, Pallas kernels for 0% -> 1%
where the time goes in v6:
time: 109 us; the launch traced here: 108 us
  starting transfers between devices  44.4 us (41%)
  waiting for transfers between devices  31.8 us (29%)
  Pallas kernels  16.8 us (15%)
  other arithmetic  7.31 us (7%)
  local copies, waits for them, and re-layouts  3.41 us (3%)
  blocking collectives  2.45 us (2%)
  between operations  1.71 us (2%)
    ppermute x7, starting transfers between devices, exchanged(): got[k] = lax.ppermute(pieces[k], 'tm', [(i, i ^ k) for i in range(count)])  26.7 us
    all_to_all x1, waiting for transfers between devices, iteration(): lax.all_to_all(corrected, 'tm', split_axis=0, concat_axis=0, tiled=True)  16.2 us
    ppermute x4, waiting for transfers between devices, summed_over_group(): values = values + lax.ppermute(values, axis, pairs)  9.78 us
    pallas_call x1, Pallas kernels, iteration(): pl.pallas_call(functools.partial(krylov_body, length, slab, halo, time_de...  9.52 us
    ppermute x1, starting transfers between devices, from_behind(): lax.ppermute(value, axis, [(source, source + steps) for source in range(i...  5.39 us
    all_to_all x1, starting transfers between devices, iteration(): lax.all_to_all(corrected, 'tm', split_axis=0, concat_axis=0, tiled=True)  4.39 us
    all_to_all x1, starting transfers between devices, iteration(): early = lax.all_to_all(early, 'tm', split_axis=0, concat_axis=0, tiled=True)  4.08 us
    ppermute x4, starting transfers between devices, summed_over_group(): values = values + lax.ppermute(values, axis, pairs)  3.24 us
  transfers between devices with their start and end apart: 16, of which 12 were waited for; matrix products, arithmetic and copies ran while one was open for 8% of the time, Pallas kernels for 1%

profile of v6, /device:TPU:0, one launch (start us, length us, event | category | flops | bytes accessed | tf_op | source)
XLA Modules:
  0.0 108.1 jit_solution(15824354568175768298)
XLA Ops:
  0.6 1.2 %borders.1 = (f32[40,512]{1,0:T(8,128)S(1)}, f32[256,512]{1,0:T(8,128)S(1)}, f32[16,512]{1,0:T(8,128)S(1)}) custom-call(f32[2,256,512]{2,1,0:T(8,128)} %iterate_ref.3, f32[2,256,512]{2,1,0:T(8,128)} %forcing_ref.1, f32[256,512]{1,0:T(8,128)} %diff_ref.1), custom_call_target="tpu_custom_call" | custom-call | tf_op jit(solution)/shard_map/borders/pallas_call | solution.py:553
  1.9 0.6 collective-permute-start.19
  2.4 5.4 %collective-permute-start.20 = (f32[256,512]{1,0:T(8,128)S(1)}, f32[256,512]{1,0:T(8,128)}, u32[]{:S(2)}, u32[]{:S(2)}) collective-permute-start(f32[256,512]{1,0:T(8,128)S(1)} %get-tuple-element.440), channel_id=1, source_target_pairs={{0,2},{2,4},{4,6},{6,8},{8,10},{10,12},{12,14},{1,3},{3,5},{5,7},{... | collective-permute-start | bytes 1572872 | tf_op jit(solution)/shard_map/ppermute | solution.py:28
  7.9 1.1 %pad_maximum_fusion.23 = f32[272,512]{1,0:T(8,128)S(1)} fusion(f32[8,512]{1,0:T(8,128)S(1)} %get-tuple-element.724, f32[256,512]{1,0:T(8,128)} %diff_ref.1, f32[8,512]{1,0:T(8,128)S(1)} %get-tuple-element.723), kind=kLoop, calls=%fused_computation.183 | loop fusion | flops 278528 | bytes 1114112 | tf_op jit(solution)/shard_map/jit(_pad)/concatenate | solution.py:587
  9.0 0.1 fusion.124
  9.3 0.5 copy-done.15
  9.8 0.4 copy-done.11
  10.2 0.5 add_add_fusion.2
  10.7 0.7 copy-done.9
  11.5 1.0 fusion.89.wide_ref.partial_ref
  12.5 0.9 later_steps.1
  13.4 4.1 %all-to-all-start.2 = ((f32[8,176,128]{2,1,0:T(8,128)}), f32[8,176,128]{2,1,0:T(8,128)S(1)}, u32[]{:S(2)}, u32[]{:S(2)}) async-start(f32[8,176,128]{2,1,0:T(8,128)} %later_steps.1), calls=%async_computation.2 | async-start | bytes 1441792 | tf_op jit(solution)/shard_map/all_to_all | solution.py:608
  17.5 1.8 %collective-permute-done.20 = f32[256,512]{1,0:T(8,128)} collective-permute-done((f32[256,512]{1,0:T(8,128)S(1)}, f32[256,512]{1,0:T(8,128)}, u32[]{:S(2)}, u32[]{:S(2)}) %collective-permute-start.20) | collective-permute-done | bytes 524320 | tf_op jit(solution)/shard_map/ppermute | solution.py:28
  19.3 1.1 %broadcast_select_fusion.2.previous_ref = f32[256,512]{1,0:T(8,128)S(1)} fusion(f32[256,512]{1,0:T(8,128)} %param.18, f32[256,512]{1,0:T(8,128)} %collective-permute-done.20, pred[]{:T(512)S(6)} %eq.73), kind=kLoop, calls=%fused_computation.187 | loop fusion | flops 131072 | bytes 1572865 | tf_op jit(solution)/shard_map/jit(_where)/select_n | solution.py:610
  20.5 0.1 add_add_fusion.4.rank_ref
  20.6 1.1 %collective-permute-done.21.low_ref.high_ref = f32[8,512]{1,0:T(8,128)S(1)} collective-permute-done((f32[8,512]{1,0:T(8,128)S(1)}, f32[8,512]{1,0:T(8,128)S(1)}, u32[]{:S(2)}, u32[]{:S(2)}) %collective-permute-start.21) | collective-permute-done | bytes 16416 | tf_op jit(solution)/shard_map/ppermute | solution.py:174
  21.7 0.7 first_step.1
  22.4 9.6 %collective-permute-start.28 = (f32[176,128]{1,0:T(8,128)S(1)}, f32[176,128]{1,0:T(8,128)S(1)}, u32[]{:S(2)}, u32[]{:S(2)}) collective-permute-start(f32[176,128]{1,0:T(8,128)S(1)} %get-tuple-element.713), channel_id=1, source_target_pairs={{0,14},{2,12},{4,10},{6,8},{8,6},{10,4},{12,2},{14,0},{1,15},{3,13... | collective-permute-start | bytes 270344 | tf_op jit(solution)/shard_map/ppermute | solution.py:35
  32.1 1.9 %collective-permute-start.26 = (f32[176,128]{1,0:T(8,128)S(1)}, f32[176,128]{1,0:T(8,128)S(1)}, u32[]{:S(2)}, u32[]{:S(2)}) collective-permute-start(f32[176,128]{1,0:T(8,128)S(1)} %get-tuple-element.715), channel_id=1, source_target_pairs={{0,10},{2,8},{4,14},{6,12},{8,2},{10,0},{12,6},{14,4},{1,11},{3,9}... | collective-permute-start | bytes 270344 | tf_op jit(solution)/shard_map/ppermute | solution.py:35
  33.9 1.1 %collective-permute-start.25 = (f32[176,128]{1,0:T(8,128)S(1)}, f32[176,128]{1,0:T(8,128)S(1)}, u32[]{:S(2)}, u32[]{:S(2)}) collective-permute-start(f32[176,128]{1,0:T(8,128)S(1)} %get-tuple-element.716), channel_id=1, source_target_pairs={{0,8},{2,10},{4,12},{6,14},{8,0},{10,2},{12,4},{14,6},{1,9},{3,11}... | collective-permute-start | bytes 270344 | tf_op jit(solution)/shard_map/ppermute | solution.py:35
  35.1 2.3 %collective-permute-start.24 = (f32[176,128]{1,0:T(8,128)S(1)}, f32[176,128]{1,0:T(8,128)S(1)}, u32[]{:S(2)}, u32[]{:S(2)}) collective-permute-start(f32[176,128]{1,0:T(8,128)S(1)} %get-tuple-element.717), channel_id=1, source_target_pairs={{0,6},{2,4},{4,2},{6,0},{8,14},{10,12},{12,10},{14,8},{1,7},{3,5},... | collective-permute-start | bytes 270344 | tf_op jit(solution)/shard_map/ppermute | solution.py:35
  37.4 0.1 collective-permute-done.28.rest_7_
  37.5 11.1 %collective-permute-start.23 = (f32[176,128]{1,0:T(8,128)S(1)}, f32[176,128]{1,0:T(8,128)S(1)}, u32[]{:S(2)}, u32[]{:S(2)}) collective-permute-start(f32[176,128]{1,0:T(8,128)S(1)} %get-tuple-element.718), channel_id=1, source_target_pairs={{0,4},{2,6},{4,0},{6,2},{8,12},{10,14},{12,8},{14,10},{1,5},{3,7},... | collective-permute-start | bytes 270344 | tf_op jit(solution)/shard_map/ppermute | solution.py:35
  48.5 0.7 collective-permute-start.22
  49.3 0.9 constant_dynamic-slice_fusion.4.diff_ref
  50.2 1.7 %collective-permute-done.26.rest_5_ = f32[176,128]{1,0:T(8,128)S(1)} collective-permute-done((f32[176,128]{1,0:T(8,128)S(1)}, f32[176,128]{1,0:T(8,128)S(1)}, u32[]{:S(2)}, u32[]{:S(2)}) %collective-permute-start.26) | collective-permute-done | bytes 90144 | tf_op jit(solution)/shard_map/ppermute | solution.py:35
  51.9 0.1 collective-permute-done.25.rest_4_
  52.0 0.9 collective-permute-done.23.rest_2_
  52.9 0.2 collective-permute-done.22.rest_1_
  53.1 9.5 %krylov.1 = (f32[704,512]{1,0:T(8,128)S(1)}, f32[704,512]{1,0:T(8,128)S(1)}, f32[704,512]{1,0:T(8,128)S(1)}, f32[704,512]{1,0:T(8,128)S(1)}, f32[704,512]{1,0:T(...) custom-call(s32[3]{0:T(128)S(1)} %add_add_fusion.3.place_ref, f32[8,176,128]{2,1,0:T(8,128)S(1)} %all-to-all-done.2.early_ref, ...), custom_call_target="tpu_custom_call" | custom-call | tf_op jit(solution)/shard_map/krylov/pallas_call | solution.py:639
  62.6 1.2 %collective-permute-done.29 = f32[16,128]{1,0:T(8,128)S(1)} collective-permute-done((f32[16,128]{1,0:T(8,128)S(1)}, f32[16,128]{1,0:T(8,128)S(1)}, u32[]{:S(2)}, u32[]{:S(2)}) %collective-permute-start.29) | collective-permute-done | bytes 8224 | tf_op jit(solution)/shard_map/ppermute | solution.py:48
  63.8 1.2 %collective-permute-start.30 = (f32[16,128]{1,0:T(8,128)S(1)}, f32[16,128]{1,0:T(8,128)S(1)}, u32[]{:S(2)}, u32[]{:S(2)}) collective-permute-start(f32[16,128]{1,0:T(8,128)S(1)} %add.484), channel_id=1, source_target_pairs={{0,2},{2,0},{4,6},{6,4},{8,10},{10,8},{12,14},{14,12},{1,3},{3,1},... | collective-permute-start | bytes 24584 | tf_op jit(solution)/shard_map/ppermute | solution.py:48
  65.0 2.4 %collective-permute-done.30 = f32[16,128]{1,0:T(8,128)S(1)} collective-permute-done((f32[16,128]{1,0:T(8,128)S(1)}, f32[16,128]{1,0:T(8,128)S(1)}, u32[]{:S(2)}, u32[]{:S(2)}) %collective-permute-start.30) | collective-permute-done | bytes 8224 | tf_op jit(solution)/shard_map/ppermute | solution.py:48
  67.4 1.2 %collective-permute-start.31 = (f32[16,128]{1,0:T(8,128)S(1)}, f32[16,128]{1,0:T(8,128)S(1)}, u32[]{:S(2)}, u32[]{:S(2)}) collective-permute-start(f32[16,128]{1,0:T(8,128)S(1)} %add.485), channel_id=1, source_target_pairs={{0,4},{2,6},{4,0},{6,2},{8,12},{10,14},{12,8},{14,10},{1,5},{3,7},... | collective-permute-start | bytes 24584 | tf_op jit(solution)/shard_map/ppermute | solution.py:48
  68.6 2.4 %collective-permute-done.31 = f32[16,128]{1,0:T(8,128)S(1)} collective-permute-done((f32[16,128]{1,0:T(8,128)S(1)}, f32[16,128]{1,0:T(8,128)S(1)}, u32[]{:S(2)}, u32[]{:S(2)}) %collective-permute-start.31) | collective-permute-done | bytes 8224 | tf_op jit(solution)/shard_map/ppermute | solution.py:48
  71.1 0.8 collective-permute-start.32
  71.9 3.8 %collective-permute-done.32 = f32[16,128]{1,0:T(8,128)S(1)} collective-permute-done((f32[16,128]{1,0:T(8,128)S(1)}, f32[16,128]{1,0:T(8,128)S(1)}, u32[]{:S(2)}, u32[]{:S(2)}) %collective-permute-start.32) | collective-permute-done | bytes 8224 | tf_op jit(solution)/shard_map/ppermute | solution.py:48
  75.7 2.4 %combine.1 = (f32[8,64,512]{2,1,0:T(8,128)}, f32[8,128]{1,0:T(8,128)S(1)}) custom-call(f32[16,128]{1,0:T(8,128)S(1)} %add.487.moments_ref, f32[7,16,128]{2,1,0:T(8,128)S(1)} %copy-done.2, f32[2,16,128]{2,1,0:T(8,128)S(1)} %copy-done.3, f32[128,128]{1,0:T(8,128)S(1)} %copy-done, f32[704,512]{1,0:T(8,128)S(1)} %get-tuple-element.443.rest_0_, ...), custom_call_target="tpu_custom_call" | custom-call | tf_op jit(solution)/shard_map/combine/pallas_call | solution.py:660
  78.1 4.4 %all-to-all-start.3 = ((f32[8,64,512]{2,1,0:T(8,128)}), f32[8,64,512]{2,1,0:T(8,128)}, u32[]{:S(2)}, u32[]{:S(2)}) async-start(f32[8,64,512]{2,1,0:T(8,128)} %get-tuple-element.449), calls=%async_computation.3 | async-start | bytes 2097152 | tf_op jit(solution)/shard_map/all_to_all | solution.py:677
  82.5 0.7 fusion.99
  83.2 0.7 reduce_sum.61
  83.9 1.4 %pad_maximum_fusion.24 = f32[2]{0:T(128)S(1)} fusion(f32[1]{0:T(128)} %bitcast.19, f32[1]{0:T(128)} %bitcast.18), kind=kLoop, calls=%fused_computation.208 | loop fusion | flops 2 | bytes 16 | tf_op jit(solution)/shard_map/concatenate | solution.py:626
  85.3 2.4 %psum.7 = f32[2]{0:T(128)S(1)} all-reduce(f32[2]{0:T(128)S(1)} %pad_maximum_fusion.24), channel_id=1, replica_groups=mesh['groups'=2,'tm'=8,'rows'=2] {'rows'}, use_global_device_ids=true, to_apply=%region_9.10 | all-reduce | flops 2 | bytes 16 | tf_op jit(solution)/shard_map/psum | solution.py:627
  87.7 0.5 add_sqrt_fusion
  88.3 0.5 slice.600
  89.4 16.2 %all-to-all-done.3 = f32[8,64,512]{2,1,0:T(8,128)} async-done(((f32[8,64,512]{2,1,0:T(8,128)}), f32[8,64,512]{2,1,0:T(8,128)}, u32[]{:S(2)}, u32[]{:S(2)}) %all-to-all-start.3) | async-done | bytes 1048608 | tf_op jit(solution)/shard_map/all_to_all | solution.py:677
  105.6 0.2 while.48
  105.9 2.1 %finish.1 = f32[2,256,512]{2,1,0:T(8,128)} custom-call(f32[2,256,512]{2,1,0:T(8,128)S(1)} %get-tuple-element.1256, f32[8,64,512]{2,1,0:T(8,128)} %get-tuple-element.1252), custom_call_target="tpu_custom_call" | custom-call | tf_op jit(solution)/shard_map/finish/pallas_call | solution.py:684
  (45 shorter events, 0.4 us)
Async XLA Ops:
  1.9 7.2 %copy-start.6 = (f32[2,256,512]{2,1,0:T(8,128)S(1)}, f32[2,256,512]{2,1,0:T(8,128)}, u32[]{:S(2)}) copy-start(f32[2,256,512]{2,1,0:T(8,128)} %iterate_ref.3) | copy-start | bytes 3145732
  1.9 6.0 %collective-permute-start.19 = (f32[40,512]{1,0:T(8,128)S(1)}, f32[40,512]{1,0:T(8,128)S(1)}, u32[]{:S(2)}, u32[]{:S(2)}) collective-permute-start(f32[40,512]{1,0:T(8,128)S(1)} %get-tuple-element.438), channel_id=1, source_target_pairs={{0,1},{1,0},{2,3},{3,2},{4,5},{5,4},{6,7},{7,6},{8,9},{9,8},{10,11... | collective-permute-start | bytes 245768 | tf_op jit(solution)/shard_map/ppermute | solution.py:566
  2.4 16.8 %collective-permute-start.20 = (f32[256,512]{1,0:T(8,128)S(1)}, f32[256,512]{1,0:T(8,128)}, u32[]{:S(2)}, u32[]{:S(2)}) collective-permute-start(f32[256,512]{1,0:T(8,128)S(1)} %get-tuple-element.440), channel_id=1, source_target_pairs={{0,2},{2,4},{4,6},{6,8},{8,10},{10,12},{12,14},{1,3},{3,5},{5,7},{... | collective-permute-start | bytes 1572872 | tf_op jit(solution)/shard_map/ppermute | solution.py:28
  9.0 0.8 copy-start.15
  9.1 1.1 %copy-start.11 = (f32[256,512]{1,0:T(8,128)S(1)}, f32[256,512]{1,0:T(8,128)}, u32[]{:S(2)}) copy-start(f32[256,512]{1,0:T(8,128)} %diff_ref.1) | copy-start | bytes 1572868
  10.2 1.2 %copy-start.9 = (f32[2,256,512]{2,1,0:T(8,128)S(1)}, f32[2,256,512]{2,1,0:T(8,128)}, u32[]{:S(2)}) copy-start(f32[2,256,512]{2,1,0:T(8,128)} %forcing_ref.1) | copy-start | bytes 3145732
  13.4 39.7 %all-to-all-start.2 = ((f32[8,176,128]{2,1,0:T(8,128)}), f32[8,176,128]{2,1,0:T(8,128)S(1)}, u32[]{:S(2)}, u32[]{:S(2)}) async-start(f32[8,176,128]{2,1,0:T(8,128)} %later_steps.1), calls=%async_computation.2 | async-start | bytes 1441792 | tf_op jit(solution)/shard_map/all_to_all | solution.py:608
  20.4 1.2 %collective-permute-start.21 = (f32[8,512]{1,0:T(8,128)S(1)}, f32[8,512]{1,0:T(8,128)S(1)}, u32[]{:S(2)}, u32[]{:S(2)}) collective-permute-start(f32[8,512]{1,0:T(8,128)S(1)} %slice_select_fusion), channel_id=1, source_target_pairs={{0,1},{1,0},{2,3},{3,2},{4,5},{5,4},{6,7},{7,6},{8,9},{9,8},{10,11... | collective-permute-start | bytes 49160 | tf_op jit(solution)/shard_map/ppermute | solution.py:174
  20.6 32.5 %copy-start.1 = (f32[128,128]{1,0:T(8,128)S(1)}, f32[128,128]{1,0:T(8,128)}, u32[]{:S(2)}) copy-start(f32[128,128]{1,0:T(8,128)} %constant.205.clone.mix_ref) | copy-start | bytes 196612
  22.3 53.3 %copy-start = (f32[128,128]{1,0:T(8,128)S(1)}, f32[128,128]{1,0:T(8,128)}, u32[]{:S(2)}) copy-start(f32[128,128]{1,0:T(8,128)} %constant.208.clone.mix_ref) | copy-start | bytes 196612
  22.3 53.3 %copy-start.2 = (f32[7,16,128]{2,1,0:T(8,128)S(1)}, f32[7,16,128]{2,1,0:T(8,128)}, u32[]{:S(2)}) copy-start(f32[7,16,128]{2,1,0:T(8,128)} %constant.206.clone.table_ref) | copy-start | bytes 172036
  22.3 53.3 %copy-start.3 = (f32[2,16,128]{2,1,0:T(8,128)S(1)}, f32[2,16,128]{2,1,0:T(8,128)}, u32[]{:S(2)}) copy-start(f32[2,16,128]{2,1,0:T(8,128)} %constant.207.clone.shift_ref) | copy-start | bytes 49156
  22.4 15.1 %collective-permute-start.28 = (f32[176,128]{1,0:T(8,128)S(1)}, f32[176,128]{1,0:T(8,128)S(1)}, u32[]{:S(2)}, u32[]{:S(2)}) collective-permute-start(f32[176,128]{1,0:T(8,128)S(1)} %get-tuple-element.713), channel_id=1, source_target_pairs={{0,14},{2,12},{4,10},{6,8},{8,6},{10,4},{12,2},{14,0},{1,15},{3,13... | collective-permute-start | bytes 270344 | tf_op jit(solution)/shard_map/ppermute | solution.py:35
  32.0 16.5 %collective-permute-start.27 = (f32[176,128]{1,0:T(8,128)S(1)}, f32[176,128]{1,0:T(8,128)S(1)}, u32[]{:S(2)}, u32[]{:S(2)}) collective-permute-start(f32[176,128]{1,0:T(8,128)S(1)} %get-tuple-element.714), channel_id=1, source_target_pairs={{0,12},{2,14},{4,8},{6,10},{8,4},{10,6},{12,0},{14,2},{1,13},{3,15... | collective-permute-start | bytes 270344 | tf_op jit(solution)/shard_map/ppermute | solution.py:35
  32.1 19.8 %collective-permute-start.26 = (f32[176,128]{1,0:T(8,128)S(1)}, f32[176,128]{1,0:T(8,128)S(1)}, u32[]{:S(2)}, u32[]{:S(2)}) collective-permute-start(f32[176,128]{1,0:T(8,128)S(1)} %get-tuple-element.715), channel_id=1, source_target_pairs={{0,10},{2,8},{4,14},{6,12},{8,2},{10,0},{12,6},{14,4},{1,11},{3,9}... | collective-permute-start | bytes 270344 | tf_op jit(solution)/shard_map/ppermute | solution.py:35
  33.9 18.1 %collective-permute-start.25 = (f32[176,128]{1,0:T(8,128)S(1)}, f32[176,128]{1,0:T(8,128)S(1)}, u32[]{:S(2)}, u32[]{:S(2)}) collective-permute-start(f32[176,128]{1,0:T(8,128)S(1)} %get-tuple-element.716), channel_id=1, source_target_pairs={{0,8},{2,10},{4,12},{6,14},{8,0},{10,2},{12,4},{14,6},{1,9},{3,11}... | collective-permute-start | bytes 270344 | tf_op jit(solution)/shard_map/ppermute | solution.py:35
  35.1 16.9 %collective-permute-start.24 = (f32[176,128]{1,0:T(8,128)S(1)}, f32[176,128]{1,0:T(8,128)S(1)}, u32[]{:S(2)}, u32[]{:S(2)}) collective-permute-start(f32[176,128]{1,0:T(8,128)S(1)} %get-tuple-element.717), channel_id=1, source_target_pairs={{0,6},{2,4},{4,2},{6,0},{8,14},{10,12},{12,10},{14,8},{1,7},{3,5},... | collective-permute-start | bytes 270344 | tf_op jit(solution)/shard_map/ppermute | solution.py:35
  37.5 15.4 %collective-permute-start.23 = (f32[176,128]{1,0:T(8,128)S(1)}, f32[176,128]{1,0:T(8,128)S(1)}, u32[]{:S(2)}, u32[]{:S(2)}) collective-permute-start(f32[176,128]{1,0:T(8,128)S(1)} %get-tuple-element.718), channel_id=1, source_target_pairs={{0,4},{2,6},{4,0},{6,2},{8,12},{10,14},{12,8},{14,10},{1,5},{3,7},... | collective-permute-start | bytes 270344 | tf_op jit(solution)/shard_map/ppermute | solution.py:35
  48.5 4.5 %collective-permute-start.22 = (f32[176,128]{1,0:T(8,128)S(1)}, f32[176,128]{1,0:T(8,128)S(1)}, u32[]{:S(2)}, u32[]{:S(2)}) collective-permute-start(f32[176,128]{1,0:T(8,128)S(1)} %get-tuple-element.719), channel_id=1, source_target_pairs={{0,2},{2,0},{4,6},{6,4},{8,10},{10,8},{12,14},{14,12},{1,3},{3,1},... | collective-permute-start | bytes 270344 | tf_op jit(solution)/shard_map/ppermute | solution.py:35
  62.6 1.2 %collective-permute-start.29 = (f32[16,128]{1,0:T(8,128)S(1)}, f32[16,128]{1,0:T(8,128)S(1)}, u32[]{:S(2)}, u32[]{:S(2)}) collective-permute-start(f32[16,128]{1,0:T(8,128)S(1)} %get-tuple-element.442), channel_id=1, source_target_pairs={{0,1},{1,0},{2,3},{3,2},{4,5},{5,4},{6,7},{7,6},{8,9},{9,8},{10,11... | collective-permute-start | bytes 24584 | tf_op jit(solution)/shard_map/ppermute | solution.py:48
  63.8 3.7 %collective-permute-start.30 = (f32[16,128]{1,0:T(8,128)S(1)}, f32[16,128]{1,0:T(8,128)S(1)}, u32[]{:S(2)}, u32[]{:S(2)}) collective-permute-start(f32[16,128]{1,0:T(8,128)S(1)} %add.484), channel_id=1, source_target_pairs={{0,2},{2,0},{4,6},{6,4},{8,10},{10,8},{12,14},{14,12},{1,3},{3,1},... | collective-permute-start | bytes 24584 | tf_op jit(solution)/shard_map/ppermute | solution.py:48
  67.4 3.7 %collective-permute-start.31 = (f32[16,128]{1,0:T(8,128)S(1)}, f32[16,128]{1,0:T(8,128)S(1)}, u32[]{:S(2)}, u32[]{:S(2)}) collective-permute-start(f32[16,128]{1,0:T(8,128)S(1)} %add.485), channel_id=1, source_target_pairs={{0,4},{2,6},{4,0},{6,2},{8,12},{10,14},{12,8},{14,10},{1,5},{3,7},... | collective-permute-start | bytes 24584 | tf_op jit(solution)/shard_map/ppermute | solution.py:48
  71.1 4.5 %collective-permute-start.32 = (f32[16,128]{1,0:T(8,128)S(1)}, f32[16,128]{1,0:T(8,128)S(1)}, u32[]{:S(2)}, u32[]{:S(2)}) collective-permute-start(f32[16,128]{1,0:T(8,128)S(1)} %add.486), channel_id=1, source_target_pairs={{0,8},{2,10},{4,12},{6,14},{8,0},{10,2},{12,4},{14,6},{1,9},{3,11}... | collective-permute-start | bytes 24584 | tf_op jit(solution)/shard_map/ppermute | solution.py:48
  78.1 27.5 %copy-start.7 = (f32[2,256,512]{2,1,0:T(8,128)S(1)}, f32[2,256,512]{2,1,0:T(8,128)}, u32[]{:S(2)}) copy-start(f32[2,256,512]{2,1,0:T(8,128)} %iterate_ref.3) | copy-start | bytes 3145732
  78.1 27.5 %copy-start.12 = (f32[256,512]{1,0:T(8,128)S(1)}, f32[256,512]{1,0:T(8,128)}, u32[]{:S(2)}) copy-start(f32[256,512]{1,0:T(8,128)} %diff_ref.1) | copy-start | bytes 1572868
  78.1 27.5 %copy-start.16 = (f32[16]{0:T(128)S(1)}, f32[16]{0:T(128)}, u32[]{:S(2)}) copy-start(f32[16]{0:T(128)} %constant.483) | copy-start | bytes 196
  78.1 27.5 %copy-start.17 = (f32[16]{0:T(128)S(1)}, f32[16]{0:T(128)}, u32[]{:S(2)}) copy-start(f32[16]{0:T(128)} %constant.482) | copy-start | bytes 196
  78.1 27.5 %copy-start.18 = (f32[16,16]{1,0:T(8,128)S(1)}, f32[16,16]{1,0:T(8,128)}, u32[]{:S(2)}) copy-start(f32[16,16]{1,0:T(8,128)} %constant.209.clone..sunk.2) | copy-start | bytes 3076
  78.1 27.5 %all-to-all-start.3 = ((f32[8,64,512]{2,1,0:T(8,128)}), f32[8,64,512]{2,1,0:T(8,128)}, u32[]{:S(2)}, u32[]{:S(2)}) async-start(f32[8,64,512]{2,1,0:T(8,128)} %get-tuple-element.449), calls=%async_computation.3 | async-start | bytes 2097152 | tf_op jit(solution)/shard_map/all_to_all | solution.py:677

commit v7 on v6

--- a/solution.py
+++ b/solution.py
@@ -14,7 +14,7 @@
 DEPTH = 2 * CG_ITERS
 MOMENTS = 2 * DEPTH + 1
 UNROLL = 16
-LEAST_PIVOTS = (2e-2, 2e-3)
+LEAST_PIVOTS = (8e-2, 8e-3)
 PAD = 8
 
 circulant_alpha = 0.05
@@ -524,7 +524,7 @@
                 other = other + spread(crossed, power) * flipped
         block = (total + other).reshape(8 * length, columns)
         result = jnp.dot(
-            mix_ref[...], block, precision=lax.Precision.HIGH, preferred_element_type=jnp.float32
+            mix_ref[...], block, precision=lax.Precision.HIGHEST, preferred_element_type=jnp.float32
         )
         for step in range(length):
             at = (step % steps_dev) * slab + start
@@ -647,7 +647,7 @@
             pltpu.VMEM((rows * 8, columns_dev), jnp.float32),
             pltpu.VMEM((rows * 8, 128), jnp.float32),
         ],
-        compiler_params=params,
+        compiler_params=pltpu.CompilerParams(vmem_limit_bytes=24 * 2**20),
         name="krylov",
     )(place, early, diff_slab, jnp.asarray(block_forward(length, 8)), *late)
 

time: 109 us -> 109 us (level)
  no operation moved by 1% of the time
where the time goes in v7:
time: 109 us; the launch traced here: 108 us
  starting transfers between devices  44.4 us (41%)
  waiting for transfers between devices  31.8 us (29%)
  Pallas kernels  17.1 us (16%)
  other arithmetic  7.31 us (7%)
  local copies, waits for them, and re-layouts  3.41 us (3%)
  blocking collectives  2.45 us (2%)
  between operations  1.71 us (2%)
    ppermute x7, starting transfers between devices, exchanged(): got[k] = lax.ppermute(pieces[k], 'tm', [(i, i ^ k) for i in range(count)])  26.7 us
    all_to_all x1, waiting for transfers between devices, iteration(): lax.all_to_all(corrected, 'tm', split_axis=0, concat_axis=0, tiled=True)  16.2 us
    ppermute x4, waiting for transfers between devices, summed_over_group(): values = values + lax.ppermute(values, axis, pairs)  9.78 us
    pallas_call x1, Pallas kernels, iteration(): pl.pallas_call(functools.partial(krylov_body, length, slab, halo, time_de...  9.52 us
    ppermute x1, starting transfers between devices, from_behind(): lax.ppermute(value, axis, [(source, source + steps) for source in range(i...  5.39 us
    all_to_all x1, starting transfers between devices, iteration(): lax.all_to_all(corrected, 'tm', split_axis=0, concat_axis=0, tiled=True)  4.39 us
    all_to_all x1, starting transfers between devices, iteration(): early = lax.all_to_all(early, 'tm', split_axis=0, concat_axis=0, tiled=True)  4.08 us
    ppermute x4, starting transfers between devices, summed_over_group(): values = values + lax.ppermute(values, axis, pairs)  3.24 us
  transfers between devices with their start and end apart: 16, of which 12 were waited for; matrix products, arithmetic and copies ran while one was open for 8% of the time, Pallas kernels for 1%

profile of v7, /device:TPU:0, one launch (start us, length us, event | category | flops | bytes accessed | tf_op | source)
XLA Modules:
  0.0 108.4 jit_solution(11032669774834973015)
XLA Ops:
  0.6 1.2 %borders.1 = (f32[40,512]{1,0:T(8,128)S(1)}, f32[256,512]{1,0:T(8,128)S(1)}, f32[16,512]{1,0:T(8,128)S(1)}) custom-call(f32[2,256,512]{2,1,0:T(8,128)} %iterate_ref.3, f32[2,256,512]{2,1,0:T(8,128)} %forcing_ref.1, f32[256,512]{1,0:T(8,128)} %diff_ref.1), custom_call_target="tpu_custom_call" | custom-call | tf_op jit(solution)/shard_map/borders/pallas_call | solution.py:553
  1.9 0.6 collective-permute-start.19
  2.4 5.4 %collective-permute-start.20 = (f32[256,512]{1,0:T(8,128)S(1)}, f32[256,512]{1,0:T(8,128)}, u32[]{:S(2)}, u32[]{:S(2)}) collective-permute-start(f32[256,512]{1,0:T(8,128)S(1)} %get-tuple-element.440), channel_id=1, source_target_pairs={{0,2},{2,4},{4,6},{6,8},{8,10},{10,12},{12,14},{1,3},{3,5},{5,7},{... | collective-permute-start | bytes 1572872 | tf_op jit(solution)/shard_map/ppermute | solution.py:28
  7.9 1.1 pad_maximum_fusion.23
  9.0 0.1 fusion.124
  9.3 0.5 copy-done.15
  9.8 0.4 copy-done.11
  10.2 0.5 add_add_fusion.2
  10.7 0.7 copy-done.9
  11.5 1.0 fusion.89.wide_ref.partial_ref
  12.5 0.9 later_steps.1
  13.4 4.1 %all-to-all-start.2 = ((f32[8,176,128]{2,1,0:T(8,128)}), f32[8,176,128]{2,1,0:T(8,128)S(1)}, u32[]{:S(2)}, u32[]{:S(2)}) async-start(f32[8,176,128]{2,1,0:T(8,128)} %later_steps.1), calls=%async_computation.2 | async-start | bytes 1441792 | tf_op jit(solution)/shard_map/all_to_all | solution.py:608
  17.5 1.8 %collective-permute-done.20 = f32[256,512]{1,0:T(8,128)} collective-permute-done((f32[256,512]{1,0:T(8,128)S(1)}, f32[256,512]{1,0:T(8,128)}, u32[]{:S(2)}, u32[]{:S(2)}) %collective-permute-start.20) | collective-permute-done | bytes 524320 | tf_op jit(solution)/shard_map/ppermute | solution.py:28
  19.3 1.1 %broadcast_select_fusion.2.previous_ref = f32[256,512]{1,0:T(8,128)S(1)} fusion(f32[256,512]{1,0:T(8,128)} %param.18, f32[256,512]{1,0:T(8,128)} %collective-permute-done.20, pred[]{:T(512)S(6)} %eq.73), kind=kLoop, calls=%fused_computation.187 | loop fusion | flops 131072 | bytes 1572865 | tf_op jit(solution)/shard_map/jit(_where)/select_n | solution.py:610
  20.5 0.1 add_add_fusion.4.rank_ref
  20.6 1.1 %collective-permute-done.21.low_ref.high_ref = f32[8,512]{1,0:T(8,128)S(1)} collective-permute-done((f32[8,512]{1,0:T(8,128)S(1)}, f32[8,512]{1,0:T(8,128)S(1)}, u32[]{:S(2)}, u32[]{:S(2)}) %collective-permute-start.21) | collective-permute-done | bytes 16416 | tf_op jit(solution)/shard_map/ppermute | solution.py:174
  21.7 0.7 first_step.1
  22.4 9.6 %collective-permute-start.28 = (f32[176,128]{1,0:T(8,128)S(1)}, f32[176,128]{1,0:T(8,128)S(1)}, u32[]{:S(2)}, u32[]{:S(2)}) collective-permute-start(f32[176,128]{1,0:T(8,128)S(1)} %get-tuple-element.713), channel_id=1, source_target_pairs={{0,14},{2,12},{4,10},{6,8},{8,6},{10,4},{12,2},{14,0},{1,15},{3,13... | collective-permute-start | bytes 270344 | tf_op jit(solution)/shard_map/ppermute | solution.py:35
  32.1 1.9 %collective-permute-start.26 = (f32[176,128]{1,0:T(8,128)S(1)}, f32[176,128]{1,0:T(8,128)S(1)}, u32[]{:S(2)}, u32[]{:S(2)}) collective-permute-start(f32[176,128]{1,0:T(8,128)S(1)} %get-tuple-element.715), channel_id=1, source_target_pairs={{0,10},{2,8},{4,14},{6,12},{8,2},{10,0},{12,6},{14,4},{1,11},{3,9}... | collective-permute-start | bytes 270344 | tf_op jit(solution)/shard_map/ppermute | solution.py:35
  33.9 1.1 %collective-permute-start.25 = (f32[176,128]{1,0:T(8,128)S(1)}, f32[176,128]{1,0:T(8,128)S(1)}, u32[]{:S(2)}, u32[]{:S(2)}) collective-permute-start(f32[176,128]{1,0:T(8,128)S(1)} %get-tuple-element.716), channel_id=1, source_target_pairs={{0,8},{2,10},{4,12},{6,14},{8,0},{10,2},{12,4},{14,6},{1,9},{3,11}... | collective-permute-start | bytes 270344 | tf_op jit(solution)/shard_map/ppermute | solution.py:35
  35.1 2.3 %collective-permute-start.24 = (f32[176,128]{1,0:T(8,128)S(1)}, f32[176,128]{1,0:T(8,128)S(1)}, u32[]{:S(2)}, u32[]{:S(2)}) collective-permute-start(f32[176,128]{1,0:T(8,128)S(1)} %get-tuple-element.717), channel_id=1, source_target_pairs={{0,6},{2,4},{4,2},{6,0},{8,14},{10,12},{12,10},{14,8},{1,7},{3,5},... | collective-permute-start | bytes 270344 | tf_op jit(solution)/shard_map/ppermute | solution.py:35
  37.4 0.1 collective-permute-done.28.rest_7_
  37.5 11.1 %collective-permute-start.23 = (f32[176,128]{1,0:T(8,128)S(1)}, f32[176,128]{1,0:T(8,128)S(1)}, u32[]{:S(2)}, u32[]{:S(2)}) collective-permute-start(f32[176,128]{1,0:T(8,128)S(1)} %get-tuple-element.718), channel_id=1, source_target_pairs={{0,4},{2,6},{4,0},{6,2},{8,12},{10,14},{12,8},{14,10},{1,5},{3,7},... | collective-permute-start | bytes 270344 | tf_op jit(solution)/shard_map/ppermute | solution.py:35
  48.5 0.7 collective-permute-start.22
  49.3 0.9 constant_dynamic-slice_fusion.4.diff_ref
  50.2 1.7 %collective-permute-done.26.rest_5_ = f32[176,128]{1,0:T(8,128)S(1)} collective-permute-done((f32[176,128]{1,0:T(8,128)S(1)}, f32[176,128]{1,0:T(8,128)S(1)}, u32[]{:S(2)}, u32[]{:S(2)}) %collective-permute-start.26) | collective-permute-done | bytes 90144 | tf_op jit(solution)/shard_map/ppermute | solution.py:35
  51.9 0.1 collective-permute-done.25.rest_4_
  52.0 0.9 collective-permute-done.23.rest_2_
  52.9 0.2 collective-permute-done.22.rest_1_
  53.1 9.5 %krylov.1 = (f32[704,512]{1,0:T(8,128)S(1)}, f32[704,512]{1,0:T(8,128)S(1)}, f32[704,512]{1,0:T(8,128)S(1)}, f32[704,512]{1,0:T(8,128)S(1)}, f32[704,512]{1,0:T(...) custom-call(s32[3]{0:T(128)S(1)} %add_add_fusion.3.place_ref, f32[8,176,128]{2,1,0:T(8,128)S(1)} %all-to-all-done.2.early_ref, ...), custom_call_target="tpu_custom_call" | custom-call | tf_op jit(solution)/shard_map/krylov/pallas_call | solution.py:639
  62.6 1.2 %collective-permute-done.29 = f32[16,128]{1,0:T(8,128)S(1)} collective-permute-done((f32[16,128]{1,0:T(8,128)S(1)}, f32[16,128]{1,0:T(8,128)S(1)}, u32[]{:S(2)}, u32[]{:S(2)}) %collective-permute-start.29) | collective-permute-done | bytes 8224 | tf_op jit(solution)/shard_map/ppermute | solution.py:48
  63.8 1.2 %collective-permute-start.30 = (f32[16,128]{1,0:T(8,128)S(1)}, f32[16,128]{1,0:T(8,128)S(1)}, u32[]{:S(2)}, u32[]{:S(2)}) collective-permute-start(f32[16,128]{1,0:T(8,128)S(1)} %add.484), channel_id=1, source_target_pairs={{0,2},{2,0},{4,6},{6,4},{8,10},{10,8},{12,14},{14,12},{1,3},{3,1},... | collective-permute-start | bytes 24584 | tf_op jit(solution)/shard_map/ppermute | solution.py:48
  65.0 2.4 %collective-permute-done.30 = f32[16,128]{1,0:T(8,128)S(1)} collective-permute-done((f32[16,128]{1,0:T(8,128)S(1)}, f32[16,128]{1,0:T(8,128)S(1)}, u32[]{:S(2)}, u32[]{:S(2)}) %collective-permute-start.30) | collective-permute-done | bytes 8224 | tf_op jit(solution)/shard_map/ppermute | solution.py:48
  67.4 1.2 %collective-permute-start.31 = (f32[16,128]{1,0:T(8,128)S(1)}, f32[16,128]{1,0:T(8,128)S(1)}, u32[]{:S(2)}, u32[]{:S(2)}) collective-permute-start(f32[16,128]{1,0:T(8,128)S(1)} %add.485), channel_id=1, source_target_pairs={{0,4},{2,6},{4,0},{6,2},{8,12},{10,14},{12,8},{14,10},{1,5},{3,7},... | collective-permute-start | bytes 24584 | tf_op jit(solution)/shard_map/ppermute | solution.py:48
  68.6 2.4 %collective-permute-done.31 = f32[16,128]{1,0:T(8,128)S(1)} collective-permute-done((f32[16,128]{1,0:T(8,128)S(1)}, f32[16,128]{1,0:T(8,128)S(1)}, u32[]{:S(2)}, u32[]{:S(2)}) %collective-permute-start.31) | collective-permute-done | bytes 8224 | tf_op jit(solution)/shard_map/ppermute | solution.py:48
  71.1 0.8 collective-permute-start.32
  71.9 3.8 %collective-permute-done.32 = f32[16,128]{1,0:T(8,128)S(1)} collective-permute-done((f32[16,128]{1,0:T(8,128)S(1)}, f32[16,128]{1,0:T(8,128)S(1)}, u32[]{:S(2)}, u32[]{:S(2)}) %collective-permute-start.32) | collective-permute-done | bytes 8224 | tf_op jit(solution)/shard_map/ppermute | solution.py:48
  75.7 2.6 %combine.1 = (f32[8,64,512]{2,1,0:T(8,128)}, f32[8,128]{1,0:T(8,128)S(1)}) custom-call(f32[16,128]{1,0:T(8,128)S(1)} %add.487.moments_ref, f32[7,16,128]{2,1,0:T(8,128)S(1)} %copy-done.2, f32[2,16,128]{2,1,0:T(8,128)S(1)} %copy-done.3, f32[128,128]{1,0:T(8,128)S(1)} %copy-done, f32[704,512]{1,0:T(8,128)S(1)} %get-tuple-element.443.rest_0_, ...), custom_call_target="tpu_custom_call" | custom-call | tf_op jit(solution)/shard_map/combine/pallas_call | solution.py:660
  78.3 4.4 %all-to-all-start.3 = ((f32[8,64,512]{2,1,0:T(8,128)}), f32[8,64,512]{2,1,0:T(8,128)}, u32[]{:S(2)}, u32[]{:S(2)}) async-start(f32[8,64,512]{2,1,0:T(8,128)} %get-tuple-element.449), calls=%async_computation.3 | async-start | bytes 2097152 | tf_op jit(solution)/shard_map/all_to_all | solution.py:677
  82.7 0.7 fusion.99
  83.5 0.7 reduce_sum.61
  84.1 1.4 %pad_maximum_fusion.24 = f32[2]{0:T(128)S(1)} fusion(f32[1]{0:T(128)} %bitcast.19, f32[1]{0:T(128)} %bitcast.18), kind=kLoop, calls=%fused_computation.208 | loop fusion | flops 2 | bytes 16 | tf_op jit(solution)/shard_map/concatenate | solution.py:626
  85.5 2.4 %psum.7 = f32[2]{0:T(128)S(1)} all-reduce(f32[2]{0:T(128)S(1)} %pad_maximum_fusion.24), channel_id=1, replica_groups=mesh['groups'=2,'tm'=8,'rows'=2] {'rows'}, use_global_device_ids=true, to_apply=%region_9.10 | all-reduce | flops 2 | bytes 16 | tf_op jit(solution)/shard_map/psum | solution.py:627
  88.0 0.5 add_sqrt_fusion
  88.5 0.5 slice.600
  89.7 16.2 %all-to-all-done.3 = f32[8,64,512]{2,1,0:T(8,128)} async-done(((f32[8,64,512]{2,1,0:T(8,128)}), f32[8,64,512]{2,1,0:T(8,128)}, u32[]{:S(2)}, u32[]{:S(2)}) %all-to-all-start.3) | async-done | bytes 1048608 | tf_op jit(solution)/shard_map/all_to_all | solution.py:677
  105.9 0.2 while.48
  106.1 2.1 %finish.1 = f32[2,256,512]{2,1,0:T(8,128)} custom-call(f32[2,256,512]{2,1,0:T(8,128)S(1)} %get-tuple-element.1256, f32[8,64,512]{2,1,0:T(8,128)} %get-tuple-element.1252), custom_call_target="tpu_custom_call" | custom-call | tf_op jit(solution)/shard_map/finish/pallas_call | solution.py:684
  (45 shorter events, 0.4 us)
Async XLA Ops:
  1.9 7.2 %copy-start.6 = (f32[2,256,512]{2,1,0:T(8,128)S(1)}, f32[2,256,512]{2,1,0:T(8,128)}, u32[]{:S(2)}) copy-start(f32[2,256,512]{2,1,0:T(8,128)} %iterate_ref.3) | copy-start | bytes 3145732
  1.9 6.0 %collective-permute-start.19 = (f32[40,512]{1,0:T(8,128)S(1)}, f32[40,512]{1,0:T(8,128)S(1)}, u32[]{:S(2)}, u32[]{:S(2)}) collective-permute-start(f32[40,512]{1,0:T(8,128)S(1)} %get-tuple-element.438), channel_id=1, source_target_pairs={{0,1},{1,0},{2,3},{3,2},{4,5},{5,4},{6,7},{7,6},{8,9},{9,8},{10,11... | collective-permute-start | bytes 245768 | tf_op jit(solution)/shard_map/ppermute | solution.py:566
  2.4 16.8 %collective-permute-start.20 = (f32[256,512]{1,0:T(8,128)S(1)}, f32[256,512]{1,0:T(8,128)}, u32[]{:S(2)}, u32[]{:S(2)}) collective-permute-start(f32[256,512]{1,0:T(8,128)S(1)} %get-tuple-element.440), channel_id=1, source_target_pairs={{0,2},{2,4},{4,6},{6,8},{8,10},{10,12},{12,14},{1,3},{3,5},{5,7},{... | collective-permute-start | bytes 1572872 | tf_op jit(solution)/shard_map/ppermute | solution.py:28
  9.0 0.8 copy-start.15
  9.1 1.1 %copy-start.11 = (f32[256,512]{1,0:T(8,128)S(1)}, f32[256,512]{1,0:T(8,128)}, u32[]{:S(2)}) copy-start(f32[256,512]{1,0:T(8,128)} %diff_ref.1) | copy-start | bytes 1572868
  10.2 1.2 %copy-start.9 = (f32[2,256,512]{2,1,0:T(8,128)S(1)}, f32[2,256,512]{2,1,0:T(8,128)}, u32[]{:S(2)}) copy-start(f32[2,256,512]{2,1,0:T(8,128)} %forcing_ref.1) | copy-start | bytes 3145732
  13.4 39.7 %all-to-all-start.2 = ((f32[8,176,128]{2,1,0:T(8,128)}), f32[8,176,128]{2,1,0:T(8,128)S(1)}, u32[]{:S(2)}, u32[]{:S(2)}) async-start(f32[8,176,128]{2,1,0:T(8,128)} %later_steps.1), calls=%async_computation.2 | async-start | bytes 1441792 | tf_op jit(solution)/shard_map/all_to_all | solution.py:608
  20.4 1.2 %collective-permute-start.21 = (f32[8,512]{1,0:T(8,128)S(1)}, f32[8,512]{1,0:T(8,128)S(1)}, u32[]{:S(2)}, u32[]{:S(2)}) collective-permute-start(f32[8,512]{1,0:T(8,128)S(1)} %slice_select_fusion), channel_id=1, source_target_pairs={{0,1},{1,0},{2,3},{3,2},{4,5},{5,4},{6,7},{7,6},{8,9},{9,8},{10,11... | collective-permute-start | bytes 49160 | tf_op jit(solution)/shard_map/ppermute | solution.py:174
  20.6 32.5 %copy-start.1 = (f32[128,128]{1,0:T(8,128)S(1)}, f32[128,128]{1,0:T(8,128)}, u32[]{:S(2)}) copy-start(f32[128,128]{1,0:T(8,128)} %constant.205.clone.mix_ref) | copy-start | bytes 196612
  22.3 53.3 %copy-start = (f32[128,128]{1,0:T(8,128)S(1)}, f32[128,128]{1,0:T(8,128)}, u32[]{:S(2)}) copy-start(f32[128,128]{1,0:T(8,128)} %constant.208.clone.mix_ref) | copy-start | bytes 196612
  22.3 53.3 %copy-start.2 = (f32[7,16,128]{2,1,0:T(8,128)S(1)}, f32[7,16,128]{2,1,0:T(8,128)}, u32[]{:S(2)}) copy-start(f32[7,16,128]{2,1,0:T(8,128)} %constant.206.clone.table_ref) | copy-start | bytes 172036
  22.3 53.3 %copy-start.3 = (f32[2,16,128]{2,1,0:T(8,128)S(1)}, f32[2,16,128]{2,1,0:T(8,128)}, u32[]{:S(2)}) copy-start(f32[2,16,128]{2,1,0:T(8,128)} %constant.207.clone.shift_ref) | copy-start | bytes 49156
  22.4 15.1 %collective-permute-start.28 = (f32[176,128]{1,0:T(8,128)S(1)}, f32[176,128]{1,0:T(8,128)S(1)}, u32[]{:S(2)}, u32[]{:S(2)}) collective-permute-start(f32[176,128]{1,0:T(8,128)S(1)} %get-tuple-element.713), channel_id=1, source_target_pairs={{0,14},{2,12},{4,10},{6,8},{8,6},{10,4},{12,2},{14,0},{1,15},{3,13... | collective-permute-start | bytes 270344 | tf_op jit(solution)/shard_map/ppermute | solution.py:35
  32.0 16.5 %collective-permute-start.27 = (f32[176,128]{1,0:T(8,128)S(1)}, f32[176,128]{1,0:T(8,128)S(1)}, u32[]{:S(2)}, u32[]{:S(2)}) collective-permute-start(f32[176,128]{1,0:T(8,128)S(1)} %get-tuple-element.714), channel_id=1, source_target_pairs={{0,12},{2,14},{4,8},{6,10},{8,4},{10,6},{12,0},{14,2},{1,13},{3,15... | collective-permute-start | bytes 270344 | tf_op jit(solution)/shard_map/ppermute | solution.py:35
  32.1 19.8 %collective-permute-start.26 = (f32[176,128]{1,0:T(8,128)S(1)}, f32[176,128]{1,0:T(8,128)S(1)}, u32[]{:S(2)}, u32[]{:S(2)}) collective-permute-start(f32[176,128]{1,0:T(8,128)S(1)} %get-tuple-element.715), channel_id=1, source_target_pairs={{0,10},{2,8},{4,14},{6,12},{8,2},{10,0},{12,6},{14,4},{1,11},{3,9}... | collective-permute-start | bytes 270344 | tf_op jit(solution)/shard_map/ppermute | solution.py:35
  33.9 18.1 %collective-permute-start.25 = (f32[176,128]{1,0:T(8,128)S(1)}, f32[176,128]{1,0:T(8,128)S(1)}, u32[]{:S(2)}, u32[]{:S(2)}) collective-permute-start(f32[176,128]{1,0:T(8,128)S(1)} %get-tuple-element.716), channel_id=1, source_target_pairs={{0,8},{2,10},{4,12},{6,14},{8,0},{10,2},{12,4},{14,6},{1,9},{3,11}... | collective-permute-start | bytes 270344 | tf_op jit(solution)/shard_map/ppermute | solution.py:35
  35.1 16.9 %collective-permute-start.24 = (f32[176,128]{1,0:T(8,128)S(1)}, f32[176,128]{1,0:T(8,128)S(1)}, u32[]{:S(2)}, u32[]{:S(2)}) collective-permute-start(f32[176,128]{1,0:T(8,128)S(1)} %get-tuple-element.717), channel_id=1, source_target_pairs={{0,6},{2,4},{4,2},{6,0},{8,14},{10,12},{12,10},{14,8},{1,7},{3,5},... | collective-permute-start | bytes 270344 | tf_op jit(solution)/shard_map/ppermute | solution.py:35
  37.5 15.4 %collective-permute-start.23 = (f32[176,128]{1,0:T(8,128)S(1)}, f32[176,128]{1,0:T(8,128)S(1)}, u32[]{:S(2)}, u32[]{:S(2)}) collective-permute-start(f32[176,128]{1,0:T(8,128)S(1)} %get-tuple-element.718), channel_id=1, source_target_pairs={{0,4},{2,6},{4,0},{6,2},{8,12},{10,14},{12,8},{14,10},{1,5},{3,7},... | collective-permute-start | bytes 270344 | tf_op jit(solution)/shard_map/ppermute | solution.py:35
  48.5 4.5 %collective-permute-start.22 = (f32[176,128]{1,0:T(8,128)S(1)}, f32[176,128]{1,0:T(8,128)S(1)}, u32[]{:S(2)}, u32[]{:S(2)}) collective-permute-start(f32[176,128]{1,0:T(8,128)S(1)} %get-tuple-element.719), channel_id=1, source_target_pairs={{0,2},{2,0},{4,6},{6,4},{8,10},{10,8},{12,14},{14,12},{1,3},{3,1},... | collective-permute-start | bytes 270344 | tf_op jit(solution)/shard_map/ppermute | solution.py:35
  62.6 1.2 %collective-permute-start.29 = (f32[16,128]{1,0:T(8,128)S(1)}, f32[16,128]{1,0:T(8,128)S(1)}, u32[]{:S(2)}, u32[]{:S(2)}) collective-permute-start(f32[16,128]{1,0:T(8,128)S(1)} %get-tuple-element.442), channel_id=1, source_target_pairs={{0,1},{1,0},{2,3},{3,2},{4,5},{5,4},{6,7},{7,6},{8,9},{9,8},{10,11... | collective-permute-start | bytes 24584 | tf_op jit(solution)/shard_map/ppermute | solution.py:48
  63.8 3.7 %collective-permute-start.30 = (f32[16,128]{1,0:T(8,128)S(1)}, f32[16,128]{1,0:T(8,128)S(1)}, u32[]{:S(2)}, u32[]{:S(2)}) collective-permute-start(f32[16,128]{1,0:T(8,128)S(1)} %add.484), channel_id=1, source_target_pairs={{0,2},{2,0},{4,6},{6,4},{8,10},{10,8},{12,14},{14,12},{1,3},{3,1},... | collective-permute-start | bytes 24584 | tf_op jit(solution)/shard_map/ppermute | solution.py:48
  67.4 3.7 %collective-permute-start.31 = (f32[16,128]{1,0:T(8,128)S(1)}, f32[16,128]{1,0:T(8,128)S(1)}, u32[]{:S(2)}, u32[]{:S(2)}) collective-permute-start(f32[16,128]{1,0:T(8,128)S(1)} %add.485), channel_id=1, source_target_pairs={{0,4},{2,6},{4,0},{6,2},{8,12},{10,14},{12,8},{14,10},{1,5},{3,7},... | collective-permute-start | bytes 24584 | tf_op jit(solution)/shard_map/ppermute | solution.py:48
  71.1 4.5 %collective-permute-start.32 = (f32[16,128]{1,0:T(8,128)S(1)}, f32[16,128]{1,0:T(8,128)S(1)}, u32[]{:S(2)}, u32[]{:S(2)}) collective-permute-start(f32[16,128]{1,0:T(8,128)S(1)} %add.486), channel_id=1, source_target_pairs={{0,8},{2,10},{4,12},{6,14},{8,0},{10,2},{12,4},{14,6},{1,9},{3,11}... | collective-permute-start | bytes 24584 | tf_op jit(solution)/shard_map/ppermute | solution.py:48
  78.3 27.5 %copy-start.7 = (f32[2,256,512]{2,1,0:T(8,128)S(1)}, f32[2,256,512]{2,1,0:T(8,128)}, u32[]{:S(2)}) copy-start(f32[2,256,512]{2,1,0:T(8,128)} %iterate_ref.3) | copy-start | bytes 3145732
  78.3 27.5 %copy-start.12 = (f32[256,512]{1,0:T(8,128)S(1)}, f32[256,512]{1,0:T(8,128)}, u32[]{:S(2)}) copy-start(f32[256,512]{1,0:T(8,128)} %diff_ref.1) | copy-start | bytes 1572868
  78.3 27.5 %copy-start.16 = (f32[16]{0:T(128)S(1)}, f32[16]{0:T(128)}, u32[]{:S(2)}) copy-start(f32[16]{0:T(128)} %constant.483) | copy-start | bytes 196
  78.3 27.5 %copy-start.17 = (f32[16]{0:T(128)S(1)}, f32[16]{0:T(128)}, u32[]{:S(2)}) copy-start(f32[16]{0:T(128)} %constant.482) | copy-start | bytes 196
  78.3 27.5 %copy-start.18 = (f32[16,16]{1,0:T(8,128)S(1)}, f32[16,16]{1,0:T(8,128)}, u32[]{:S(2)}) copy-start(f32[16,16]{1,0:T(8,128)} %constant.209.clone..sunk.2) | copy-start | bytes 3076
  78.3 27.5 %all-to-all-start.3 = ((f32[8,64,512]{2,1,0:T(8,128)}), f32[8,64,512]{2,1,0:T(8,128)}, u32[]{:S(2)}, u32[]{:S(2)}) async-start(f32[8,64,512]{2,1,0:T(8,128)} %get-tuple-element.449), calls=%async_computation.3 | async-start | bytes 2097152 | tf_op jit(solution)/shard_map/all_to_all | solution.py:677
